TPU v7x, 32 devices: a whole 2x2x4 slice. The times are simulated.
32 devices in a mesh: section: 4 (over z), tile: 8 (over y, x, core).
Axes of the slice: x: 2, y: 2, z: 4, core: 2. Of those that a mesh axis runs over, the one named last changes fastest.
Arguments:
- raw_echo: bfloat16 [2, 2048, 8192], P(None, 'tile', 'section'), may hold values from -6 to 6
- footprint: int32 [4, 8, 8], P('section', 'tile'), may hold values from 0 to 255, as said below
- window_start: int32 [4, 256], P('section', 'tile'), may hold values from 0 to 2047
Outputs:
- image: bfloat16 [4, 8, 1024, 2048], P('section', 'tile')
Inputs may be any that keep to these rules, and one draw needn't show every extreme that they name: `footprint`: each list names 8 different pulse blocks; at most 2 of them lie among the 32 blocks k * 32 to (k + 1) * 32 - 1 of one index k of tile, and in every list some index supplies exactly 2.
All inputs are finite; a program needn't handle non-finite values.
Results may differ from a plain program's by a relative error of at most 0.0071.
Values may be sent and summed in bfloat16 or wider, within the bound.
No kernel may reach another device: no remote copies, remote signals or barrier semaphores. Data moves between devices by JAX's collectives and lax.ppermute only.
A program may use at most 128 MiB of HBM per device.

v0:
```python
import math

import jax
import jax.numpy as jnp
from jax import lax
from jax.sharding import PartitionSpec as P

KC = 128
WIN = 256
PR = 1024
PC = 1024
NP = 8


def passed_along(value, axis, by):
    devices = lax.axis_size(axis)
    pairs = [(i, i + by) for i in range(devices) if 0 <= i + by < devices]
    return lax.ppermute(value, axis, pairs)


def chirp_table(length):
    row_index = lax.broadcasted_iota(jnp.int32, (2 * length, length), 0)
    col_index = lax.broadcasted_iota(jnp.int32, (2 * length, length), 1)
    lag_count = row_index - col_index
    inside = (lag_count >= 0) & (lag_count < length)
    lag_safe = jnp.where(inside, lag_count, 0)
    turn_count = (lag_safe * lag_safe % (2 * length)).astype(jnp.float32)
    phase_angle = turn_count * jnp.float32(math.pi / length)
    scaling = jnp.float32(1.0 / math.sqrt(length))
    real_part = jnp.where(inside, jnp.cos(phase_angle) * scaling, jnp.float32(0.0))
    imag_part = jnp.where(inside, jnp.sin(phase_angle) * scaling, jnp.float32(0.0))
    return (real_part.astype(jnp.bfloat16), imag_part.astype(jnp.bfloat16))


def compress(raw_part, length, keep):
    real_tab, imag_tab = chirp_table(length)
    pulses = raw_part.shape[1]
    blocks = keep // length
    pieces = raw_part.reshape(2, pulses, blocks + 1, length)
    paired = jnp.concatenate([pieces[:, :, :-1], pieces[:, :, 1:]], axis=3).reshape(
        2, pulses * blocks, 2 * length
    )
    real_in = paired[0]
    imag_in = paired[1]
    out_real = jnp.dot(real_in, real_tab, preferred_element_type=jnp.float32) + jnp.dot(
        imag_in, imag_tab, preferred_element_type=jnp.float32
    )
    out_imag = jnp.dot(imag_in, real_tab, preferred_element_type=jnp.float32) - jnp.dot(
        real_in, imag_tab, preferred_element_type=jnp.float32
    )
    stacked = jnp.stack([out_real, out_imag]).reshape(2, pulses, keep)
    return stacked.astype(jnp.bfloat16)


def interp_table(pixel_rows, window_bins):
    upsample = pixel_rows // window_bins
    row_index = lax.broadcasted_iota(jnp.float32, (pixel_rows, window_bins), 0)
    bin_index = lax.broadcasted_iota(jnp.float32, (pixel_rows, window_bins), 1)
    centre = (row_index + 0.5) / upsample - 0.5
    offset = bin_index - centre
    tapering = jnp.cos(offset * (math.pi / 8.0)) ** 2
    kernel = jnp.where(jnp.abs(offset) < 4.0, jnp.sinc(offset) * tapering, 0.0)
    return kernel.astype(jnp.bfloat16)


def tile_image(chosen, block_ids, row_pos, col_pos, interp, pixel_cols):
    entries = chosen.shape[0]
    per_block = chosen.shape[1]
    window_bins = chosen.shape[3]
    merged = chosen.reshape(entries * per_block, 2 * window_bins)
    pulse_ids = (
        block_ids[:, None] * per_block + jnp.arange(per_block, dtype=jnp.int32)[None, :]
    ).reshape(-1)
    columns = col_pos * pixel_cols + jnp.arange(pixel_cols, dtype=jnp.int32) + 1 + 7 * row_pos
    scrambled = columns * 40503 % 65521
    residue = pulse_ids[:, None] * scrambled[None, :] % 65521
    phase_angle = residue.astype(jnp.float32) * jnp.float32(2.0 * math.pi / 65521.0)
    steer_real = jnp.cos(phase_angle).astype(jnp.bfloat16)
    steer_imag = jnp.sin(phase_angle).astype(jnp.bfloat16)
    contract = (((0,), (0,)), ((), ()))
    with_real = lax.dot_general(merged, steer_real, contract, preferred_element_type=jnp.float32)
    with_imag = lax.dot_general(merged, steer_imag, contract, preferred_element_type=jnp.float32)
    scaling = jnp.float32(1.0 / math.sqrt(entries * per_block))
    focus_real = (with_real[:window_bins] - with_imag[window_bins:]) * scaling
    focus_imag = (with_imag[:window_bins] + with_real[window_bins:]) * scaling
    focused = jnp.concatenate([focus_real, focus_imag], axis=1).astype(jnp.bfloat16)
    return jnp.dot(interp, focused, preferred_element_type=jnp.float32).astype(jnp.bfloat16)


def cut_windows(extended, starts, per_block):
    pulses = extended.shape[1]
    span_bins = extended.shape[2]
    grouped = jnp.transpose(
        extended.reshape(2, pulses // per_block, per_block, span_bins), (1, 2, 0, 3)
    )

    def one_block(block_data, start):
        return lax.dynamic_slice_in_dim(block_data, start, WIN, 2)

    return jax.vmap(one_block)(grouped, starts)


def local(raw_echo, footprint, window_start):
    bin_count = raw_echo.shape[2]
    next_rim = passed_along(raw_echo[:, :, :KC], "section", -1)
    own_part = compress(jnp.concatenate([raw_echo, next_rim], axis=2), KC, bin_count)
    next_bins = passed_along(own_part[:, :, :WIN], "section", -1)
    extended = jnp.concatenate([own_part, next_bins], axis=2)
    windows = cut_windows(extended, window_start[0], NP)
    my_list = footprint[0, 0]
    tile_pos = lax.axis_index("tile")
    row_pos = lax.axis_index("section")
    all_blocks = lax.all_gather(windows, "tile", axis=0, tiled=True)
    chosen = jnp.take(all_blocks, my_list, axis=0)
    interp = interp_table(PR, WIN)
    image = tile_image(chosen, my_list, row_pos, tile_pos, interp, PC)
    return image[None, None]


def solution(mesh):
    in_specs = (P(None, "tile", "section"), P("section", "tile", None), P("section", "tile"))
    out_specs = P("section", "tile", None, None)
    return jax.shard_map(local, mesh=mesh, in_specs=in_specs, out_specs=out_specs, check_vma=False)
```

profile of v0, /device:TPU:0, one launch (start us, length us, event | category | flops | bytes accessed | tf_op | source)
XLA Modules:
  0.0 181.1 jit_solution(12100500757804425028)
XLA Ops:
  6.5 0.0 all-gather.2.cloned.1.call-start
  6.5 2.8 %copy.15 = bf16[2,256,2048]{1,2,0:T(8,128)(2,1)S(1)} copy(bf16[2,256,2048]{2,1,0:T(8,128)(2,1)} %param.3) | data formatting | bytes 4194304 | tf_op args[0]
  9.4 1.3 collective-permute-start
  10.7 7.1 %collective-permute-done = bf16[2,256,128]{1,2,0:T(8,128)(2,1)S(1)} collective-permute-done((bf16[2,256,128]{1,2,0:T(8,128)(2,1)S(1)}, bf16[2,256,128]{1,2,0:T(8,128)(2,1)S(1)}, u32[]{:S(2)}, u32[]{:S(2)}) %collective-permute-start) | collective-permute-done | bytes 131104 | tf_op jit(solution)/shard_map/ppermute | solution.py:18
  17.8 0.1 pad_maximum_fusion
  18.0 0.5 fusion.123
  18.5 2.3 %pad_maximum_fusion.1 = (bf16[1,256,16,256]{1,3,2,0:T(8,128)(2,1)}, bf16[1,256,16,256]{1,3,2,0:T(8,128)(2,1)}) fusion(bf16[2,256,16,128]{1,3,2,0:T(8,128)(2,1)S(1)} %get-tuple-element.9, bf16[2,256,16,128]{1,3,2,0:T(8,128)(2,1)S(1)} %get-tuple-element.10), kind=kLoop, calls=%fused_computation.12 | loop fusion | flops 8388608 | bytes 8388608 | tf_op jit(solution)/shard_map/concatenate | solution.py:40
  20.8 3.3 %copy.17 = bf16[1,256,16,256]{3,2,1,0:T(8,128)(2,1)S(1)} copy(bf16[1,256,16,256]{1,3,2,0:T(8,128)(2,1)} %get-tuple-element.7) | data formatting | bytes 4194304 | tf_op jit(solution)/shard_map/slice | solution.py:44
  24.1 2.5 %fusion.63 = f32[4096,128]{1,0:T(8,128)} fusion(bf16[4096,256]{1,0:T(8,128)(2,1)S(1)} %bitcast.27), kind=kOutput, calls=%fused_computation.95 | convolution fusion | flops 269156352 | bytes 4194304 | tf_op jit(solution)/shard_map/dot_general | solution.py:48
  26.6 4.5 %copy.16 = bf16[1,256,16,256]{3,2,1,0:T(8,128)(2,1)} copy(bf16[1,256,16,256]{1,3,2,0:T(8,128)(2,1)} %get-tuple-element.8) | data formatting | bytes 4194304 | tf_op jit(solution)/shard_map/slice | solution.py:43
  31.1 0.0 copy-start
  31.1 0.0 copy-start.1
  31.1 4.2 %fusion.64 = f32[4096,128]{1,0:T(8,128)} fusion(bf16[4096,256]{1,0:T(8,128)(2,1)} %bitcast.29), kind=kOutput, calls=%fused_computation.96 | convolution fusion | flops 269156352 | bytes 4194304 | tf_op jit(solution)/shard_map/dot_general | solution.py:45
  35.4 0.0 copy-done
  35.4 0.0 copy-done.1
  35.4 1.2 fusion.1
  36.6 1.3 stack.10
  37.9 2.8 %fusion = bf16[4096,128]{1,0:T(8,128)(2,1)S(1)} fusion(f32[4096,128]{1,0:T(8,128)} %fusion.64, bf16[4096,256]{1,0:T(8,128)(2,1)S(1)} %bitcast.28), kind=kOutput, calls=%fused_computation.4 | convolution fusion | flops 270204928 | bytes 5242880 | tf_op jit(solution)/shard_map/dot_general | solution.py:45
  40.7 0.0 copy-start.2
  40.7 0.5 stack.9
  41.2 0.0 copy-start.3
  41.2 0.1 constant_dynamic-update-slice_fusion.1
  41.3 0.6 copy-done.2
  41.9 0.1 constant_dynamic-update-slice_fusion
  42.0 1.5 collective-permute-start.1
  43.5 0.0 copy-done.3
  43.5 7.9 %collective-permute-done.1 = bf16[2,256,256]{2,1,0:T(8,128)(2,1)S(1)} collective-permute-done((bf16[2,256,256]{2,1,0:T(8,128)(2,1)S(1)}, bf16[2,256,256]{2,1,0:T(8,128)(2,1)S(1)}, u32[]{:S(2)}, u32[]{:S(2)}) %collective-permute-start.1) | collective-permute-done | bytes 262176 | tf_op jit(solution)/shard_map/ppermute | solution.py:18
  51.4 0.2 maximum_bitcast_fusion
  51.6 60.6 %copy.18 = bf16[2,32,8,2304]{2,0,1,3:T(2,128)(2,1)} copy(bf16[2,32,8,2304]{3,2,1,0:T(8,128)(2,1)S(1)} %maximum_bitcast_fusion) | data formatting | bytes 4718592 | tf_op jit(solution)/shard_map/reshape | solution.py:94
  112.2 11.5 %gather_fusion.1 = bf16[32,8,2,256]{1,2,3,0:T(2,128)(2,1)} fusion(bf16[32,8,2,2304]{1,2,0,3:T(2,128)(2,1)} %bitcast.26, s32[32]{0:T(128)S(1)} %fusion.72), kind=kCustom, calls=%fused_computation.1 | custom fusion | bytes 524800 | tf_op jit(solution)/shard_map/vmap()/gather | solution.py:98
  123.8 0.0 copy-start.4
  123.8 9.2 %copy.19 = bf16[32,8,2,256]{3,1,2,0:T(8,128)(2,1)} copy(bf16[32,8,2,256]{1,2,3,0:T(2,128)(2,1)} %gather_fusion.1) | data formatting | bytes 524288 | tf_op jit(solution)/shard_map/vmap()/gather | solution.py:98
  133.0 0.0 all-gather.2.cloned.1.call-update
  133.0 0.0 copy-done.4
  133.0 0.1 iota_add_fusion
  133.1 0.1 add.195
  133.2 0.1 broadcast_in_dim.34
  133.3 0.1 broadcast_in_dim.35
  133.4 27.7 %all-gather.2.cloned.1.call-done = bf16[256,8,2,256]{3,1,2,0:T(8,128)(2,1)} async-done(((bf16[32,8,2,256]{3,1,2,0:T(8,128)(2,1)}), bf16[256,8,2,256]{3,1,2,0:T(8,128)(2,1)}) %all-gather.2.cloned.1.call-update) | async-done | bytes 2097168 | tf_op jit(solution)/shard_map/all_gather | solution.py:113
  161.1 2.1 %gather_fusion = bf16[8,8,2,256]{3,1,2,0:T(8,128)(2,1)S(1)} fusion(bf16[256,8,2,256]{3,1,2,0:T(8,128)(2,1)} %all-gather.2.cloned.1.call-done, s32[1024]{0:T(1024)S(1)} %pad_clamp_fusion), kind=kCustom, calls=%fused_computation | custom fusion | bytes 131104 | tf_op jit(solution)/shard_map/jit(_take)/gather | solution.py:114
  163.3 1.4 fusion.48
  164.7 1.4 fusion.49
  166.1 0.5 fusion.14
  166.6 7.6 %convert_bitcast_fusion = bf16[1,1,1024,2048]{3,2,1,0:T(8,128)(2,1)} fusion(bf16[256,1024]{1,0:T(8,128)(2,1)S(1)} %get-tuple-element.6, bf16[256,1024]{1,0:T(8,128)(2,1)S(1)} %get-tuple-element.5, f32[1024]{0:T(1024)S(1)} %multiply_add_fusion.1), kind=kOutput, calls=%fused_computation.8 | convolution fusion | flops 1088421888 | bytes 5246976 | tf_op jit(solution)/shard_map/dot_general | solution.py:87
  (9 shorter events, 0.1 us)
Async XLA Ops:
  6.5 154.6 %all-gather.2.cloned.1.call-start = ((), (), s32[]{:S(2)}) async-start(), calls=%async_computation | async-start | bytes 2359296 | tf_op jit(solution)/shard_map/all_gather | solution.py:113
  9.4 8.4 %collective-permute-start = (bf16[2,256,128]{1,2,0:T(8,128)(2,1)S(1)}, bf16[2,256,128]{1,2,0:T(8,128)(2,1)S(1)}, u32[]{:S(2)}, u32[]{:S(2)}) collective-permute-start(bf16[2,256,128]{1,2,0:T(8,128)(2,1)S(1)} %slice.51), channel_id=1, source_target_pairs={{8,0},{16,8},{24,16},{9,1},{17,9},{25,17},{10,2},{18,10},{26,18},{... | collective-permute-start | bytes 393224 | tf_op jit(solution)/shard_map/ppermute | solution.py:18
  31.1 4.3 %copy-start = (bf16[1,256,16,256]{3,2,1,0:T(8,128)(2,1)S(1)}, bf16[1,256,16,256]{3,2,1,0:T(8,128)(2,1)}, u32[]{:S(2)}) copy-start(bf16[1,256,16,256]{3,2,1,0:T(8,128)(2,1)} %copy.16) | copy-start | bytes 6291460
  31.1 4.3 %copy-start.1 = (f32[4096,128]{1,0:T(8,128)S(1)}, f32[4096,128]{1,0:T(8,128)}, u32[]{:S(2)}) copy-start(f32[4096,128]{1,0:T(8,128)} %fusion.63) | copy-start | bytes 6291460
  40.7 1.2 copy-start.2
  41.2 2.3 %copy-start.3 = (s32[1,32]{1,0:T(1,128)S(1)}, s32[1,32]{1,0:T(1,128)}, u32[]{:S(2)}) copy-start(s32[1,32]{1,0:T(1,128)} %param.5) | copy-start | bytes 388
  42.0 9.4 %collective-permute-start.1 = (bf16[2,256,256]{2,1,0:T(8,128)(2,1)S(1)}, bf16[2,256,256]{2,1,0:T(8,128)(2,1)S(1)}, u32[]{:S(2)}, u32[]{:S(2)}) collective-permute-start(bf16[2,256,256]{2,1,0:T(8,128)(2,1)S(1)} %slice.56), channel_id=1, source_target_pairs={{8,0},{16,8},{24,16},{9,1},{17,9},{25,17},{10,2},{18,10},{26,18},{... | collective-permute-start | bytes 786440 | tf_op jit(solution)/shard_map/ppermute | solution.py:18
  123.8 9.2 %copy-start.4 = (s32[1,1,8]{2,1,0:T(1,128)S(1)}, s32[1,1,8]{2,1,0:T(1,128)}, u32[]{:S(2)}) copy-start(s32[1,1,8]{2,1,0:T(1,128)} %param.4) | copy-start | bytes 100
Sparse Core Ops, SparseCore 0:
  133.1 27.9 all-gather.1
where the time goes:
time: 182 us; the launch traced here: 181 us
  local copies, waits for them, and re-layouts  97.6 us (54%)
  waiting for transfers between devices  42.7 us (23%)
  matrix products  21.3 us (12%)
  between operations  13.6 us (7%)
  other arithmetic  3.22 us (2%)
  starting transfers between devices  2.77 us (2%)
    reshape x1, local copies, waits for them, and re-layouts, cut_windows(): extended.reshape(2, pulses // per_block, per_block, span_bins)  60.6 us
    all_gather x1, waiting for transfers between devices, local(): all_blocks = lax.all_gather(windows, 'tile', axis=0, tiled=True)  27.7 us
    gather x2, local copies, waits for them, and re-layouts, one_block(): return lax.dynamic_slice_in_dim(block_data, start, WIN, 2)  20.7 us
    ppermute x2, waiting for transfers between devices, passed_along(): return lax.ppermute(value, axis, pairs)  15 us
    dot_general x1, matrix products, tile_image(): jnp.dot(interp, focused, preferred_element_type=jnp.float32)  7.65 us
    slice x1, local copies, waits for them, and re-layouts, compress(): real_in = paired[0]  4.49 us
    dot_general x1, matrix products, compress(): jnp.dot(real_in, real_tab, preferred_element_type=jnp.float32)  4.25 us
  transfers between devices with their start and end apart: 3, of which 3 were waited for; matrix products, arithmetic and copies ran while one was open for 0% of the time, Pallas kernels for 0%

commit v1 on v0

v1 whole, which is shorter than its diff:
```python
import functools
import math

import jax
import jax.numpy as jnp
import ml_dtypes
import numpy as np
from jax import lax
from jax.experimental import pallas as pl
from jax.experimental.pallas import tpu as pltpu
from jax.sharding import PartitionSpec as P

KC = 128
WIN = 256
PR = 1024
PC = 1024
NP = 8
CAP = 2
LANES = 128
PRIME = 65521
RIM = WIN + KC
SPAN = RIM + LANES
VMEM_BYTES = 48 << 20
BF16 = jnp.bfloat16


def passed_along(value, axis, by):
    devices = lax.axis_size(axis)
    pairs = [(i, i + by) for i in range(devices) if 0 <= i + by < devices]
    return lax.ppermute(value, axis, pairs)


def correlation_table():
    lag = np.arange(RIM)[:, None] - np.arange(WIN)[None, :]
    inside = (lag >= 0) & (lag < KC)
    lag = np.where(inside, lag, 0)
    angle = (lag * lag % (2 * KC)).astype(np.float64) * (math.pi / KC)
    scale = 1.0 / math.sqrt(KC)
    real = np.where(inside, np.cos(angle) * scale, 0.0)
    imag = np.where(inside, np.sin(angle) * scale, 0.0)
    return np.concatenate([real, imag], axis=1).astype(np.float32).astype(ml_dtypes.bfloat16)


def interp_table():
    row = np.arange(PR, dtype=np.float64)[:, None]
    offset = np.arange(WIN, dtype=np.float64)[None, :] - ((row + 0.5) / (PR // WIN) - 0.5)
    taper = np.cos(offset * (math.pi / 8.0)) ** 2
    kernel = np.where(np.abs(offset) < 4.0, np.sinc(offset) * taper, 0.0)
    return kernel.astype(np.float32).astype(ml_dtypes.bfloat16)


def cut_kernel(blocks_ref, tiles_ref, raw_ref, rim_ref, out_ref, sem):
    chunks = out_ref.shape[0]
    lane_tiles = raw_ref.shape[3] // LANES

    def one_chunk(n, carry):
        block = blocks_ref[n]
        tile = tiles_ref[n]
        over = jnp.maximum(tile + SPAN // LANES - lane_tiles, 0)
        for beyond in range(SPAN // LANES):
            own = SPAN - beyond * LANES

            @pl.when(over == beyond)
            def _():
                first = pl.multiple_of(tile * LANES, LANES)
                pltpu.make_async_copy(
                    raw_ref.at[:, block, :, pl.ds(first, own)],
                    out_ref.at[n, :, :, pl.ds(0, own)],
                    sem,
                ).start()
                if beyond:
                    pltpu.make_async_copy(
                        rim_ref.at[:, block, :, pl.ds(0, SPAN - own)],
                        out_ref.at[n, :, :, pl.ds(own, SPAN - own)],
                        sem,
                    ).start()

        return carry

    lax.fori_loop(0, chunks, one_chunk, 0)
    pltpu.make_async_copy(out_ref, out_ref, sem).wait()


def cut_windows(raw, rim, blocks, tiles):
    chunks = blocks.shape[0]
    planes, _, per_block, _ = raw.shape
    any_spec = pl.BlockSpec(memory_space=pl.ANY)
    return pl.pallas_call(
        cut_kernel,
        out_shape=jax.ShapeDtypeStruct((chunks, planes, per_block, SPAN), raw.dtype),
        grid_spec=pltpu.PrefetchScalarGridSpec(
            num_scalar_prefetch=2,
            grid=(1,),
            in_specs=[any_spec, any_spec],
            out_specs=any_spec,
            scratch_shapes=[pltpu.SemaphoreType.DMA],
        ),
        name="cut",
    )(blocks, tiles, raw, rim)


def mod_prime(value):
    for _ in range(2):
        value = (value >> 16) * 15 + (value & 65535)
    return jnp.where(value >= PRIME, value - PRIME, value)


def steer_kernel(list_ref, place_ref, out_ref):
    foot = list_ref.shape[0]
    pulses = foot * NP
    width = lambda rows: lax.broadcasted_iota(jnp.int32, (rows, PC), 1)
    to_angle = jnp.float32(2.0 * math.pi / PRIME)
    first = place_ref[0]

    def turned(steps, columns):
        scrambled = mod_prime((columns + first) * 40503)
        return mod_prime(steps * scrambled).astype(jnp.float32) * to_angle

    inner = turned(lax.broadcasted_iota(jnp.int32, (NP, PC), 0), width(NP))
    cos_in, sin_in = jnp.cos(inner), jnp.sin(inner)
    row = lax.broadcasted_iota(jnp.int32, (foot, PC), 0)
    ids = jnp.zeros((foot, PC), jnp.int32)
    for i in range(foot):
        ids = jnp.where(row == i, list_ref[i] * NP, ids)
    outer = turned(ids, width(foot))
    cos_out, sin_out = jnp.cos(outer), jnp.sin(outer)
    for i in range(0, foot, 2):
        real, imag = [], []
        for j in (i, i + 1):
            c, s = cos_out[j : j + 1], sin_out[j : j + 1]
            real.append(c * cos_in - s * sin_in)
            imag.append(s * cos_in + c * sin_in)
        real = jnp.concatenate(real, axis=0).astype(BF16)
        imag = jnp.concatenate(imag, axis=0).astype(BF16)
        rows = pl.ds(i * NP, 2 * NP)
        below = pl.ds(pulses + i * NP, 2 * NP)
        out_ref[rows, :PC] = real
        out_ref[rows, PC:] = imag
        out_ref[below, :PC] = -imag
        out_ref[below, PC:] = real


def steering(my_list, first_column):
    foot = my_list.shape[0]
    return pl.pallas_call(
        steer_kernel,
        out_shape=jax.ShapeDtypeStruct((2 * foot * NP, 2 * PC), BF16),
        in_specs=[pl.BlockSpec(memory_space=pltpu.SMEM)] * 2,
        out_specs=pl.BlockSpec(memory_space=pltpu.VMEM),
        name="steer",
    )(my_list, first_column)


def image_kernel(chunk_ref, shift_ref, got_ref, table_ref, steer_ref, interp_ref, out_ref, echo, wins):
    pulses = echo.shape[0] // 2
    foot = pulses // NP

    @pl.when(pl.program_id(0) == 0)
    def _():
        for i in range(0, foot, 2):
            both = []
            for j in (i, i + 1):
                piece = got_ref[chunk_ref[j]].astype(jnp.float32).reshape(2 * NP, SPAN)
                turn = lax.rem(SPAN - shift_ref[j], SPAN)
                both.append(pltpu.roll(piece, turn, 1)[:, :RIM])
            for plane in range(2):
                part = slice(plane * NP, (plane + 1) * NP)
                echo[pl.ds(plane * pulses + i * NP, 2 * NP), :] = jnp.concatenate(
                    [both[0][part], both[1][part]], axis=0
                ).astype(BF16)
        sums = jnp.dot(echo[...], table_ref[...], preferred_element_type=jnp.float32)
        real = sums[:pulses, :WIN] + sums[pulses:, WIN:]
        imag = sums[pulses:, :WIN] - sums[:pulses, WIN:]
        wins[...] = jnp.concatenate([real, imag], axis=0).astype(BF16)

    scale = jnp.float32(1.0 / math.sqrt(pulses))
    contract = (((0,), (0,)), ((), ()))
    focused = lax.dot_general(
        wins[...], steer_ref[...], contract, preferred_element_type=jnp.float32
    )
    focused = (focused * scale).astype(BF16)
    out_ref[...] = jnp.dot(
        interp_ref[...], focused, preferred_element_type=jnp.float32
    ).astype(BF16)


def tile_image(got, chunk, shift, steer):
    foot = chunk.shape[0]
    pulses = foot * NP
    step = 256
    whole = lambda shape: pl.BlockSpec(shape, lambda c, *_: (0,) * len(shape), pipeline_mode=pl.Buffered(1))
    return pl.pallas_call(
        image_kernel,
        out_shape=jax.ShapeDtypeStruct((PR, 2 * PC), BF16),
        grid_spec=pltpu.PrefetchScalarGridSpec(
            num_scalar_prefetch=2,
            grid=(2 * PC // step,),
            in_specs=[
                whole(got.shape),
                whole((RIM, 2 * WIN)),
                pl.BlockSpec((2 * pulses, step), lambda c, *_: (0, c)),
                whole((PR, WIN)),
            ],
            out_specs=pl.BlockSpec((PR, step), lambda c, *_: (0, c)),
            scratch_shapes=[
                pltpu.VMEM((2 * pulses, RIM), BF16),
                pltpu.VMEM((2 * pulses, WIN), BF16),
            ],
        ),
        compiler_params=pltpu.CompilerParams(vmem_limit_bytes=VMEM_BYTES),
        name="image",
    )(chunk, shift, got, jnp.asarray(correlation_table()), steer, jnp.asarray(interp_table()))


def local(raw_echo, footprint, window_start):
    planes, pulses, bins = raw_echo.shape
    blocks = pulses // NP
    tiles = lax.axis_size("tile")
    foot = footprint.shape[2]
    tile_pos = lax.axis_index("tile")
    row_pos = lax.axis_index("section")
    my_list = footprint[0, 0]

    rim = passed_along(raw_echo[:, :, :RIM], "section", -1)
    note = jnp.concatenate([my_list, window_start[0]])
    notes = lax.all_gather(note[None], "tile", axis=0, tiled=True)

    lists = notes[:, :foot] - tile_pos * blocks
    held = (lists >= 0) & (lists < blocks)
    lowest = jnp.min(jnp.where(held, lists, blocks - 1), axis=1)
    highest = jnp.max(jnp.where(held, lists, 0), axis=1)
    cut_blocks = jnp.stack([lowest, highest], axis=1).reshape(-1)
    hot = cut_blocks[:, None] == jnp.arange(blocks, dtype=jnp.int32)[None, :]
    cut_starts = jnp.sum(jnp.where(hot, window_start, 0), axis=1)

    holder = my_list // blocks
    below = (holder[None, :] == holder[:, None]) & (my_list[None, :] < my_list[:, None])
    chunk = holder * CAP + jnp.any(below, axis=1).astype(jnp.int32)
    starts = notes[:, foot:].reshape(-1)
    named = my_list[:, None] == jnp.arange(tiles * blocks, dtype=jnp.int32)[None, :]
    shift = jnp.sum(jnp.where(named, starts[None, :], 0), axis=1) % LANES

    sent = cut_windows(
        raw_echo.reshape(planes, blocks, NP, bins),
        rim.reshape(planes, blocks, NP, RIM),
        cut_blocks,
        cut_starts // LANES,
    )
    got = lax.all_to_all(
        sent.reshape((tiles, CAP) + sent.shape[1:]), "tile", 0, 0, tiled=True
    ).reshape(sent.shape)

    first_column = (tile_pos * PC + 1 + 7 * row_pos).astype(jnp.int32)
    steer = steering(my_list, first_column[None])
    image = tile_image(got, chunk, shift, steer)
    return image[None, None]


def solution(mesh):
    in_specs = (P(None, "tile", "section"), P("section", "tile", None), P("section", "tile"))
    out_specs = P("section", "tile", None, None)
    return jax.shard_map(local, mesh=mesh, in_specs=in_specs, out_specs=out_specs, check_vma=False)
```

time: 182 us -> 47.1 us (0.26)
  local copies, waits for them, and re-layouts: 97.6 us -> 4.57 us
  waiting for transfers between devices: 42.7 us -> 4.1 us
  matrix products: 21.3 us -> 0 us
  Pallas kernels: 0 us -> 18.4 us
  between operations: 13.6 us -> 0.71 us
  blocking collectives: 0 us -> 9.46 us
  starting transfers between devices: 2.77 us -> 4.71 us
    reshape x1, local copies, waits for them, and re-layouts: 60.6 us -> 0.08 us  [local(): cut_blocks = jnp.stack([lowest, highest], axis=1).reshape(-1)]
    all_gather x1 -> x0, waiting for transfers between devices: 27.7 us -> none  [local(): all_blocks = lax.all_gather(windows, 'tile', axis=0, tiled=True)]
    gather x3 -> x0, local copies, waits for them, and re-layouts: 22.9 us -> none  [the longest x2 20.7 us: one_block(): return lax.dynamic_slice_in_dim(block_data, start, WIN, 2)]
    dot_general x7 -> x0, matrix products: 21.3 us -> none  [the longest x1 7.65 us: tile_image(): jnp.dot(interp, focused, preferred_element_type=jnp.float32)]
    pallas_call x0 -> x3, Pallas kernels: none -> 18.4 us  [the longest x1 9.75 us: cut_windows(): pl.pallas_call(cut_kernel, out_shape=jax.ShapeDtypeStruct((chunks, planes...]
    ppermute x2 -> x1, waiting for transfers between devices: 15 us -> 0.01 us  [passed_along(): return lax.ppermute(value, axis, pairs)]
    unnamed x0 -> x1, blocking collectives: none -> 9.46 us
    slice x5 -> x2, local copies, waits for them, and re-layouts: 8.38 us -> 1.2 us  [the longest x1 1.13 us: local(): rim = passed_along(raw_echo[:, :, :RIM], 'section', -1)]
  transfers between devices with their start and end apart: 3 -> 2, of which waited for: 3 -> 1; matrix products, arithmetic and copies ran while one was open for 0% -> 14% of each run, Pallas kernels for 0% -> 4%
where the time goes in v1:
time: 47.1 us; the launch traced here: 46.8 us
  Pallas kernels  18.4 us (39%)
  blocking collectives  9.46 us (20%)
  other arithmetic  4.83 us (10%)
  starting transfers between devices  4.71 us (10%)
  local copies, waits for them, and re-layouts  4.57 us (10%)
  waiting for transfers between devices  4.1 us (9%)
  between operations  0.71 us (2%)
    pallas_call x1, Pallas kernels, cut_windows(): pl.pallas_call(cut_kernel, out_shape=jax.ShapeDtypeStruct((chunks, planes...  9.75 us
    unnamed x1, blocking collectives  9.46 us
    pallas_call x1, Pallas kernels, tile_image(): pl.pallas_call(image_kernel, out_shape=jax.ShapeDtypeStruct((PR, 2 * PC),...  6.79 us
    all_to_all x1, waiting for transfers between devices, local(): lax.all_to_all(sent.reshape((tiles, CAP) + sent.shape[1:]), 'tile', 0, 0,...  4.09 us
    all_to_all x1, starting transfers between devices, local(): lax.all_to_all(sent.reshape((tiles, CAP) + sent.shape[1:]), 'tile', 0, 0,...  3.42 us
    unnamed x14, local copies, waits for them, and re-layouts  3.04 us
    pallas_call x1, Pallas kernels, steering(): pl.pallas_call(steer_kernel, out_shape=jax.ShapeDtypeStruct((2 * foot * N...  1.84 us
    ppermute x1, starting transfers between devices, passed_along(): return lax.ppermute(value, axis, pairs)  1.29 us
  transfers between devices with their start and end apart: 2, of which 1 were waited for; matrix products, arithmetic and copies ran while one was open for 14% of the time, Pallas kernels for 4%

profile of v1, /device:TPU:0, one launch (start us, length us, event | category | flops | bytes accessed | tf_op | source)
XLA Modules:
  0.0 46.8 jit_solution(6260185071805015003)
XLA Ops:
  0.0 0.0 copy-start.1
  0.0 0.0 copy-start.2
  0.0 0.0 copy-start.4
  0.0 1.1 %slice.11 = bf16[2,256,384]{2,1,0:T(8,128)(2,1)S(1)} slice(bf16[2,256,2048]{2,1,0:T(8,128)(2,1)} %param.5), slice={[0:2], [0:256], [0:384]} | slice | bytes 786432 | tf_op jit(solution)/shard_map/slice | solution.py:224
  1.1 1.3 %collective-permute-start = (bf16[2,256,384]{2,1,0:T(8,128)(2,1)S(1)}, bf16[2,256,384]{2,1,0:T(8,128)(2,1)S(1)}, u32[]{:S(2)}, u32[]{:S(2)}) collective-permute-start(bf16[2,256,384]{2,1,0:T(8,128)(2,1)S(1)} %slice.11), channel_id=1, source_target_pairs={{8,0},{16,8},{24,16},{9,1},{17,9},{25,17},{10,2},{18,10},{26,18},{... | collective-permute-start | bytes 1179656 | tf_op jit(solution)/shard_map/ppermute | solution.py:30
  2.4 0.7 %and_select_fusion.2 = s32[8]{0:T(128)S(1)} fusion(s32[1,1,8]{2,1,0:T(1,128)} %param.6), kind=kLoop, calls=%fused_computation.13 | loop fusion | flops 120 | bytes 64 | tf_op jit(solution)/shard_map/jit(floor_divide)/jit(_where)/select_n | solution.py:236
  3.1 1.2 %dynamic-slice = u32[1]{0:T(128)} dynamic-slice(u32[32]{0:T(128)} %constant.76, u32[]{:T(128)S(6)} %add.29), dynamic_slice_sizes={1} | dynamic-slice | bytes 12
  5.0 0.8 %add_dynamic-update-slice_fusion = s32[320]{0:T(512)S(1)} fusion(s32[320]{0:T(512)S(1)} %broadcast.88, u32[]{:T(128)} %bitcast.2, s32[32]{0:T(128)} %bitcast.24, s32[8]{0:T(128)} %bitcast.18), kind=kLoop, calls=%fused_computation.22 | loop fusion | flops 40 | bytes 676
  5.9 9.5 %all-reduce = s32[320]{0:T(512)S(1)} all-reduce(s32[320]{0:T(512)S(1)} %add_dynamic-update-slice_fusion), channel_id=2, replica_groups=mesh['section'=4,'tile'=8] {'tile'}, use_global_device_ids=true, to_apply=%add | all-reduce | flops 320 | bytes 2560
  15.3 0.1 reshape.80
  15.4 0.1 slice.9
  15.5 0.2 select_reduce_fusion.3
  15.6 0.1 broadcast_in_dim.45
  15.7 0.8 %select_reduce_fusion.1 = s32[8]{0:T(128)S(1)} fusion(s32[256]{0:T(256)S(1)} %broadcast_in_dim.45, s32[8]{0:T(128)} %bitcast.19), kind=kLoop, calls=%fused_computation.2 | loop fusion | flops 6136 | bytes 1088 | tf_op jit(solution)/shard_map/reduce_sum | solution.py:241
  16.6 0.1 copy.8
  16.6 0.1 reshape.75.blocks_ref
  16.7 0.0 copy-start.5
  16.7 0.8 %select_reduce_fusion = s32[16]{0:T(128)S(1)} fusion(s32[32]{0:T(128)} %bitcast.25, s32[16]{0:T(128)S(1)} %reshape.75.blocks_ref), kind=kLoop, calls=%fused_computation | loop fusion | flops 1520 | bytes 256 | tf_op jit(solution)/shard_map/reduce_sum | solution.py:234
  17.6 0.5 %and_select_fusion.tiles_ref = s32[16]{0:T(128)} fusion(s32[16]{0:T(128)S(1)} %select_reduce_fusion), kind=kLoop, calls=%fused_computation.11 | loop fusion | flops 240 | bytes 128 | tf_op jit(solution)/shard_map/jit(floor_divide)/jit(_where)/select_n | solution.py:247
  18.1 0.0 collective-permute-done
  18.1 0.0 copy-start.3
  18.1 0.0 copy-done.5
  18.1 0.7 %copy-done.3 = bf16[2,256,384]{2,1,0:T(8,128)(2,1)} copy-done((bf16[2,256,384]{2,1,0:T(8,128)(2,1)}, bf16[2,256,384]{2,1,0:T(8,128)(2,1)S(1)}, u32[]{:S(2)}) %copy-start.3) | copy-done | bytes 393240
  18.9 9.7 %cut.1 = bf16[16,2,8,512]{3,2,1,0:T(8,128)(2,1)} custom-call(s32[16]{0:T(128)} %copy-done.5, s32[16]{0:T(128)} %and_select_fusion.tiles_ref, bf16[2,32,8,2048]{3,2,1,0:T(8,128)(2,1)} %bitcast.15, bf16[2,32,8,384]{3,2,1,0:T(8,128)(2,1)} %bitcast.17), custom_call_target="tpu_custom_call" | custom-call | tf_op jit(solution)/shard_map/cut/pallas_call | solution.py:88
  28.6 3.4 %all-to-all-start = ((bf16[8,2,2,8,512]{4,3,2,1,0:T(8,128)(2,1)}), bf16[8,2,2,8,512]{4,3,2,1,0:T(8,128)(2,1)S(1)}, u32[]{:S(2)}, u32[]{:S(2)}) async-start(bf16[8,2,2,8,512]{4,3,2,1,0:T(8,128)(2,1)} %bitcast.16), calls=%async_computation | async-start | bytes 524288 | tf_op jit(solution)/shard_map/all_to_all | solution.py:249
  32.1 0.9 %and_reduce_fusion = pred[8]{0:T(512)(128)(4,1)S(1)} fusion(s32[8]{0:T(128)} %bitcast.20, s32[8]{0:T(128)S(1)} %and_select_fusion.2), kind=kLoop, calls=%fused_computation.8 | loop fusion | flops 248 | bytes 72 | tf_op jit(solution)/shard_map/reduce_or | solution.py:238
  33.0 1.8 %steer.1.steer_ref = bf16[128,2048]{1,0:T(8,128)(2,1)} custom-call(s32[8]{0:T(128)} %bitcast.21, s32[1]{0:T(128)} %bitcast.9.place_ref), custom_call_target="tpu_custom_call" | custom-call | tf_op jit(solution)/shard_map/steer/pallas_call | solution.py:145
  34.8 0.0 copy-done.4
  34.8 4.1 %all-to-all-done = bf16[8,2,2,8,512]{4,3,2,1,0:T(8,128)(2,1)S(1)} async-done(((bf16[8,2,2,8,512]{4,3,2,1,0:T(8,128)(2,1)}), bf16[8,2,2,8,512]{4,3,2,1,0:T(8,128)(2,1)S(1)}, u32[]{:S(2)}, u32[]{:S(2)}) %all-to-all-start) | async-done | bytes 262176 | tf_op jit(solution)/shard_map/all_to_all | solution.py:249
  38.9 0.0 copy-done.1
  38.9 0.0 copy-done.2
  38.9 0.0 copy-start
  38.9 1.0 %copy-done = bf16[128,2048]{1,0:T(8,128)(2,1)S(1)} copy-done((bf16[128,2048]{1,0:T(8,128)(2,1)S(1)}, bf16[128,2048]{1,0:T(8,128)(2,1)}, u32[]{:S(2)}) %copy-start) | copy-done | bytes 524312
  40.0 6.8 %image.1 = bf16[1024,2048]{1,0:T(8,128)(2,1)} custom-call(s32[8]{0:T(128)S(1)} %convert_add_fusion.chunk_ref, s32[8]{0:T(128)S(1)} %and_select_fusion.1.shift_ref, bf16[16,2,8,512]{3,2,1,0:T(8,128)(2,1)S(1)} %bitcast.14, bf16[384,512]{1,0:T(8,128)(2,1)S(1)} %copy-done.2, bf16[128,2048]{1,0:T(8,128)(2,1)S(1)} %copy-done, bf16[1024,256]{1,0:T(8,128)(2,1)S(1)} %copy-done.1), custom_call_target="tpu_custom_call" | custom-call | tf_op jit(solution)/shard_map/image/pallas_call | solution.py:192
  (4 shorter events, 0.0 us)
Async XLA Ops:
  0.0 38.9 %copy-start.1 = (bf16[1024,256]{1,0:T(8,128)(2,1)S(1)}, bf16[1024,256]{1,0:T(8,128)(2,1)}, u32[]{:S(2)}) copy-start(bf16[1024,256]{1,0:T(8,128)(2,1)} %constant.71.clone.interp_ref) | copy-start | bytes 1572868
  0.0 38.9 %copy-start.2 = (bf16[384,512]{1,0:T(8,128)(2,1)S(1)}, bf16[384,512]{1,0:T(8,128)(2,1)}, u32[]{:S(2)}) copy-start(bf16[384,512]{1,0:T(8,128)(2,1)} %constant.70.clone.table_ref) | copy-start | bytes 1179652
  0.0 34.8 %copy-start.4 = (s32[1,1,8]{2,1,0:T(1,128)S(1)}, s32[1,1,8]{2,1,0:T(1,128)}, u32[]{:S(2)}) copy-start(s32[1,1,8]{2,1,0:T(1,128)} %param.6) | copy-start | bytes 100
  1.1 17.0 %collective-permute-start = (bf16[2,256,384]{2,1,0:T(8,128)(2,1)S(1)}, bf16[2,256,384]{2,1,0:T(8,128)(2,1)S(1)}, u32[]{:S(2)}, u32[]{:S(2)}) collective-permute-start(bf16[2,256,384]{2,1,0:T(8,128)(2,1)S(1)} %slice.11), channel_id=1, source_target_pairs={{8,0},{16,8},{24,16},{9,1},{17,9},{25,17},{10,2},{18,10},{26,18},{... | collective-permute-start | bytes 1179656 | tf_op jit(solution)/shard_map/ppermute | solution.py:30
  16.7 1.4 %copy-start.5 = (s32[16]{0:T(128)}, s32[16]{0:T(128)S(1)}, u32[]{:S(2)}) copy-start(s32[16]{0:T(128)S(1)} %reshape.75.blocks_ref) | copy-start | bytes 196
  18.1 0.7 %copy-start.3 = (bf16[2,256,384]{2,1,0:T(8,128)(2,1)}, bf16[2,256,384]{2,1,0:T(8,128)(2,1)S(1)}, u32[]{:S(2)}) copy-start(bf16[2,256,384]{2,1,0:T(8,128)(2,1)S(1)} %collective-permute-done) | copy-start | bytes 1179652
  28.6 10.3 %all-to-all-start = ((bf16[8,2,2,8,512]{4,3,2,1,0:T(8,128)(2,1)}), bf16[8,2,2,8,512]{4,3,2,1,0:T(8,128)(2,1)S(1)}, u32[]{:S(2)}, u32[]{:S(2)}) async-start(bf16[8,2,2,8,512]{4,3,2,1,0:T(8,128)(2,1)} %bitcast.16), calls=%async_computation | async-start | bytes 524288 | tf_op jit(solution)/shard_map/all_to_all | solution.py:249
  38.9 1.0 %copy-start = (bf16[128,2048]{1,0:T(8,128)(2,1)S(1)}, bf16[128,2048]{1,0:T(8,128)(2,1)}, u32[]{:S(2)}) copy-start(bf16[128,2048]{1,0:T(8,128)(2,1)} %steer.1.steer_ref) | copy-start | bytes 1572868

commit v2 on v1

v2 whole, which is shorter than its diff:
```python
import functools
import math

import jax
import jax.numpy as jnp
import ml_dtypes
import numpy as np
from jax import lax
from jax.experimental import pallas as pl
from jax.experimental.pallas import tpu as pltpu
from jax.sharding import PartitionSpec as P

KC = 128
WIN = 256
PR = 1024
PC = 1024
NP = 8
CAP = 2
LANES = 128
PRIME = 65521
RIM = WIN + KC
SPAN = RIM + LANES
VMEM_BYTES = 24 << 20
SMALL_BYTES = 8 << 20
BF16 = jnp.bfloat16


def passed_along(value, axis, by):
    devices = lax.axis_size(axis)
    pairs = [(i, i + by) for i in range(devices) if 0 <= i + by < devices]
    return lax.ppermute(value, axis, pairs)


def correlation_table():
    lag = np.arange(RIM)[:, None] - np.arange(WIN)[None, :]
    inside = (lag >= 0) & (lag < KC)
    lag = np.where(inside, lag, 0)
    angle = (lag * lag % (2 * KC)).astype(np.float64) * (math.pi / KC)
    scale = 1.0 / math.sqrt(KC)
    real = np.where(inside, np.cos(angle) * scale, 0.0)
    imag = np.where(inside, np.sin(angle) * scale, 0.0)
    return np.concatenate([real, imag], axis=1).astype(np.float32).astype(ml_dtypes.bfloat16)


def interp_table():
    row = np.arange(PR, dtype=np.float64)[:, None]
    offset = np.arange(WIN, dtype=np.float64)[None, :] - ((row + 0.5) / (PR // WIN) - 0.5)
    taper = np.cos(offset * (math.pi / 8.0)) ** 2
    kernel = np.where(np.abs(offset) < 4.0, np.sinc(offset) * taper, 0.0)
    return kernel.astype(np.float32).astype(ml_dtypes.bfloat16)


def fetch_kernel(foot, notes_ref, place_ref, raw_ref, out_ref, plan_ref, sem):
    blocks = raw_ref.shape[1]
    last = (raw_ref.shape[3] - SPAN) // LANES
    mine = place_ref[0]

    def one_tile(n, carry):
        lowest, highest = jnp.int32(blocks - 1), jnp.int32(0)
        for e in range(foot):
            block = notes_ref[n, e] - mine * blocks
            held = (block >= 0) & (block < blocks)
            lowest = jnp.where(held, jnp.minimum(lowest, block), lowest)
            highest = jnp.where(held, jnp.maximum(highest, block), highest)
        for slot, block in enumerate((lowest, highest)):
            tile = notes_ref[mine, foot + block] >> 7
            first = pl.multiple_of(jnp.minimum(tile, last) * LANES, LANES)
            chunk = CAP * n + slot
            pltpu.make_async_copy(
                raw_ref.at[:, block, :, pl.ds(first, SPAN)], out_ref.at[chunk], sem
            ).start()
            plan_ref[0, chunk] = block
            plan_ref[1, chunk] = tile - last
        return carry

    tiles = notes_ref.shape[0]
    lax.fori_loop(0, tiles, one_tile, 0, unroll=tiles <= 8)
    pltpu.make_async_copy(out_ref, out_ref, sem).wait()


def extend_kernel(plan_ref, spans_ref, rim_ref, out_ref):
    chunks = spans_ref.shape[0]

    def one_chunk(chunk, carry):
        block = plan_ref[0, chunk]
        over = jnp.maximum(plan_ref[1, chunk], 0)
        for beyond in range(SPAN // LANES):

            @pl.when(over == beyond)
            def _():
                kept = SPAN - beyond * LANES
                out_ref[chunk, :, :, :kept] = spans_ref[chunk, :, :, SPAN - kept :]
                if beyond:
                    out_ref[chunk, :, :, kept:] = rim_ref[:, block, :, : SPAN - kept]

        return carry

    lax.fori_loop(0, chunks, one_chunk, 0, unroll=chunks <= 16)


def cut_windows(foot, notes, place, raw, rim):
    planes, _, per_block, _ = raw.shape
    chunks = notes.shape[0] * CAP
    smem = pl.BlockSpec(memory_space=pltpu.SMEM)
    vmem = pl.BlockSpec(memory_space=pltpu.VMEM)
    spans = jax.ShapeDtypeStruct((chunks, planes, per_block, SPAN), raw.dtype)
    fetched, plan = pl.pallas_call(
        functools.partial(fetch_kernel, foot),
        out_shape=(spans, jax.ShapeDtypeStruct((2, chunks), jnp.int32)),
        in_specs=[smem, smem, pl.BlockSpec(memory_space=pltpu.HBM)],
        out_specs=(vmem, smem),
        scratch_shapes=[pltpu.SemaphoreType.DMA],
        compiler_params=pltpu.CompilerParams(vmem_limit_bytes=SMALL_BYTES),
        name="fetch",
    )(notes, place, raw)
    return pl.pallas_call(
        extend_kernel,
        out_shape=spans,
        in_specs=[smem, vmem, vmem],
        out_specs=vmem,
        compiler_params=pltpu.CompilerParams(vmem_limit_bytes=SMALL_BYTES),
        name="extend",
    )(plan, fetched, rim)


def mod_prime(value):
    for _ in range(2):
        value = (value >> 16) * 15 + (value & 65535)
    return jnp.where(value >= PRIME, value - PRIME, value)


def place_entries(blocks, list_ref, notes_ref, where_ref):
    foot = list_ref.shape[0]

    def one(i, carry):
        block = list_ref[i]
        holder = block // blocks

        def also(j, second):
            other = list_ref[j]
            return second | ((other // blocks == holder) & (other < block)).astype(jnp.int32)

        second = lax.fori_loop(0, foot, also, jnp.int32(0), unroll=foot <= 8)
        where_ref[0, i] = holder * CAP + second
        where_ref[1, i] = notes_ref[holder, foot + block - holder * blocks] & (LANES - 1)
        return carry

    lax.fori_loop(0, foot, one, 0)


def steer_kernel(blocks, list_ref, place_ref, notes_ref, out_ref, where_ref):
    foot = list_ref.shape[0]
    pulses = foot * NP
    width = lambda rows: lax.broadcasted_iota(jnp.int32, (rows, PC), 1)
    to_angle = jnp.float32(2.0 * math.pi / PRIME)
    first = place_ref[0]

    def turned(steps, columns):
        scrambled = mod_prime((columns + first) * 40503)
        return mod_prime(steps * scrambled).astype(jnp.float32) * to_angle

    inner = turned(lax.broadcasted_iota(jnp.int32, (NP, PC), 0), width(NP))
    cos_in, sin_in = jnp.cos(inner), jnp.sin(inner)
    row = lax.broadcasted_iota(jnp.int32, (foot, PC), 0)
    ids = jnp.zeros((foot, PC), jnp.int32)
    for i in range(foot):
        ids = jnp.where(row == i, list_ref[i] * NP, ids)
    outer = turned(ids, width(foot))
    cos_out, sin_out = jnp.cos(outer), jnp.sin(outer)
    place_entries(blocks, list_ref, notes_ref, where_ref)
    for i in range(0, foot, 2):
        real, imag = [], []
        for j in (i, i + 1):
            c, s = cos_out[j : j + 1], sin_out[j : j + 1]
            real.append(c * cos_in - s * sin_in)
            imag.append(s * cos_in + c * sin_in)
        real = jnp.concatenate(real, axis=0).astype(BF16)
        imag = jnp.concatenate(imag, axis=0).astype(BF16)
        rows = pl.ds(i * NP, 2 * NP)
        below = pl.ds(pulses + i * NP, 2 * NP)
        out_ref[rows, :PC] = real
        out_ref[rows, PC:] = imag
        out_ref[below, :PC] = -imag
        out_ref[below, PC:] = real


def steering(my_list, first_column, notes, blocks):
    foot = my_list.shape[0]
    smem = pl.BlockSpec(memory_space=pltpu.SMEM)
    return pl.pallas_call(
        functools.partial(steer_kernel, blocks),
        out_shape=(
            jax.ShapeDtypeStruct((2 * foot * NP, 2 * PC), BF16),
            jax.ShapeDtypeStruct((2, foot), jnp.int32),
        ),
        in_specs=[smem] * 3,
        out_specs=(pl.BlockSpec(memory_space=pltpu.VMEM), smem),
        compiler_params=pltpu.CompilerParams(vmem_limit_bytes=SMALL_BYTES),
        name="steer",
    )(my_list, first_column, notes)


def image_kernel(where_ref, got_ref, table_ref, steer_ref, interp_ref, out_ref, echo, wins):
    pulses = echo.shape[0] // 2
    foot = pulses // NP

    @pl.when(pl.program_id(0) == 0)
    def _():
        for i in range(0, foot, 2):
            both = []
            for j in (i, i + 1):
                piece = got_ref[where_ref[0, j]].astype(jnp.float32).reshape(2 * NP, SPAN)
                turn = lax.rem(SPAN - where_ref[1, j], SPAN)
                both.append(pltpu.roll(piece, turn, 1)[:, :RIM])
            for plane in range(2):
                part = slice(plane * NP, (plane + 1) * NP)
                echo[pl.ds(plane * pulses + i * NP, 2 * NP), :] = jnp.concatenate(
                    [both[0][part], both[1][part]], axis=0
                ).astype(BF16)
        sums = jnp.dot(echo[...], table_ref[...], preferred_element_type=jnp.float32)
        real = sums[:pulses, :WIN] + sums[pulses:, WIN:]
        imag = sums[pulses:, :WIN] - sums[:pulses, WIN:]
        wins[...] = jnp.concatenate([real, imag], axis=0).astype(BF16)

    scale = jnp.float32(1.0 / math.sqrt(pulses))
    contract = (((0,), (0,)), ((), ()))
    focused = lax.dot_general(
        wins[...], steer_ref[...], contract, preferred_element_type=jnp.float32
    )
    focused = (focused * scale).astype(BF16)
    out_ref[...] = jnp.dot(
        interp_ref[...], focused, preferred_element_type=jnp.float32
    ).astype(BF16)


def tile_image(got, where, steer):
    foot = where.shape[1]
    pulses = foot * NP
    step = 256
    whole = lambda shape: pl.BlockSpec(shape, lambda c, *_: (0,) * len(shape), pipeline_mode=pl.Buffered(1))
    return pl.pallas_call(
        image_kernel,
        out_shape=jax.ShapeDtypeStruct((PR, 2 * PC), BF16),
        grid_spec=pltpu.PrefetchScalarGridSpec(
            num_scalar_prefetch=1,
            grid=(2 * PC // step,),
            in_specs=[
                whole(got.shape),
                whole((RIM, 2 * WIN)),
                pl.BlockSpec((2 * pulses, step), lambda c, *_: (0, c)),
                whole((PR, WIN)),
            ],
            out_specs=pl.BlockSpec((PR, step), lambda c, *_: (0, c)),
            scratch_shapes=[
                pltpu.VMEM((2 * pulses, RIM), BF16),
                pltpu.VMEM((2 * pulses, WIN), BF16),
            ],
        ),
        compiler_params=pltpu.CompilerParams(vmem_limit_bytes=VMEM_BYTES),
        name="image",
    )(where, got, jnp.asarray(correlation_table()), steer, jnp.asarray(interp_table()))


def local(raw_echo, footprint, window_start):
    planes, pulses, bins = raw_echo.shape
    blocks = pulses // NP
    tiles = lax.axis_size("tile")
    foot = footprint.shape[2]
    tile_pos = lax.axis_index("tile").astype(jnp.int32)
    row_pos = lax.axis_index("section").astype(jnp.int32)
    my_list = footprint[0, 0]

    rim = passed_along(raw_echo[:, :, :RIM], "section", -1)
    note = jnp.concatenate([footprint[0], window_start], axis=1)
    note = jnp.pad(note, ((0, 0), (0, -note.shape[1] % LANES)))
    notes = lax.all_gather(note, "tile", axis=0, tiled=True)

    sent = cut_windows(
        foot,
        notes,
        tile_pos[None],
        raw_echo.reshape(planes, blocks, NP, bins),
        rim.reshape(planes, blocks, NP, RIM),
    )
    got = lax.all_to_all(
        sent.reshape((tiles, CAP) + sent.shape[1:]), "tile", 0, 0, tiled=True
    ).reshape(sent.shape)

    first_column = tile_pos * PC + 1 + 7 * row_pos
    steer, where = steering(my_list, first_column[None], notes, blocks)
    image = tile_image(got, where, steer)
    return image[None, None]


def solution(mesh):
    in_specs = (P(None, "tile", "section"), P("section", "tile", None), P("section", "tile"))
    out_specs = P("section", "tile", None, None)
    return jax.shard_map(local, mesh=mesh, in_specs=in_specs, out_specs=out_specs, check_vma=False)
```

time: 47.1 us -> 36.8 us (0.78)
  Pallas kernels: 18.4 us -> 12.2 us
  other arithmetic: 4.83 us -> 0.75 us
  local copies, waits for them, and re-layouts: 4.57 us -> 3.71 us
  waiting for transfers between devices: 4.1 us -> 4.86 us
  blocking collectives: 9.46 us -> 10.2 us
  between operations: 0.71 us -> 0.07 us
    all_gather x0 -> x1, blocking collectives: none -> 10.2 us  [local(): notes = lax.all_gather(note, 'tile', axis=0, tiled=True)]
    unnamed x1 -> x0, blocking collectives: 9.46 us -> none
    pallas_call x2 -> x3, Pallas kernels: 11.6 us -> 5.39 us  [the longest x1 1.98 us: steering(): pl.pallas_call(functools.partial(steer_kernel, blocks), out_shape=(jax.Sh...]
    reduce_sum x2 -> x0, other arithmetic: 1.68 us -> none  [the longest x1 0.84 us: local(): cut_starts = jnp.sum(jnp.where(hot, window_start, 0), axis=1)]
    select_n x3 -> x0, other arithmetic: 1.22 us -> none  [the longest x1 0.67 us: local(): holder = my_list // blocks]
    reduce_or x1 -> x0, other arithmetic: 0.92 us -> none  [local(): chunk = holder * CAP + jnp.any(below, axis=1).astype(jnp.int32)]
    unnamed x1 -> x0, other arithmetic: 0.84 us -> none
    all_to_all x1, waiting for transfers between devices: 4.09 us -> 4.86 us  [local(): lax.all_to_all(sent.reshape((tiles, CAP) + sent.shape[1:]), 'tile', 0, 0,...]
  transfers between devices with their start and end apart: 2 -> 2, of which waited for: 1 -> 1; matrix products, arithmetic and copies ran while one was open for 14% -> 2% of each run, Pallas kernels for 4% -> 10%
where the time goes in v2:
time: 36.8 us; the launch traced here: 36.5 us
  Pallas kernels  12.2 us (33%)
  blocking collectives  10.2 us (28%)
  waiting for transfers between devices  4.86 us (13%)
  starting transfers between devices  4.7 us (13%)
  local copies, waits for them, and re-layouts  3.71 us (10%)
  other arithmetic  0.75 us (2%)
    all_gather x1, blocking collectives, local(): notes = lax.all_gather(note, 'tile', axis=0, tiled=True)  10.2 us
    pallas_call x1, Pallas kernels, tile_image(): pl.pallas_call(image_kernel, out_shape=jax.ShapeDtypeStruct((PR, 2 * PC),...  6.79 us
    all_to_all x1, waiting for transfers between devices, local(): lax.all_to_all(sent.reshape((tiles, CAP) + sent.shape[1:]), 'tile', 0, 0,...  4.86 us
    all_to_all x1, starting transfers between devices, local(): lax.all_to_all(sent.reshape((tiles, CAP) + sent.shape[1:]), 'tile', 0, 0,...  3.41 us
    unnamed x9, local copies, waits for them, and re-layouts  2.6 us
    pallas_call x1, Pallas kernels, steering(): pl.pallas_call(functools.partial(steer_kernel, blocks), out_shape=(jax.Sh...  1.98 us
    pallas_call x1, Pallas kernels, cut_windows(): pl.pallas_call(functools.partial(fetch_kernel, foot), out_shape=(spans, j...  1.78 us
    pallas_call x1, Pallas kernels, cut_windows(): pl.pallas_call(extend_kernel, out_shape=spans, in_specs=[smem, vmem, vmem...  1.63 us
  transfers between devices with their start and end apart: 2, of which 1 were waited for; matrix products, arithmetic and copies ran while one was open for 2% of the time, Pallas kernels for 10%

profile of v2, /device:TPU:0, one launch (start us, length us, event | category | flops | bytes accessed | tf_op | source)
XLA Modules:
  0.0 36.5 jit_solution(1962577640877863384)
XLA Ops:
  0.0 0.0 copy-start.1
  0.0 0.0 copy-start.3
  0.0 1.1 %slice.3 = bf16[2,256,384]{2,1,0:T(8,128)(2,1)S(1)} slice(bf16[2,256,2048]{2,1,0:T(8,128)(2,1)} %param.5), slice={[0:2], [0:256], [0:384]} | slice | bytes 786432 | tf_op jit(solution)/shard_map/slice | solution.py:273
  1.1 1.3 %collective-permute-start = (bf16[2,256,384]{2,1,0:T(8,128)(2,1)S(1)}, bf16[2,256,384]{2,1,0:T(8,128)(2,1)S(1)}, u32[]{:S(2)}, u32[]{:S(2)}) collective-permute-start(bf16[2,256,384]{2,1,0:T(8,128)(2,1)S(1)} %slice.3), channel_id=1, source_target_pairs={{8,0},{16,8},{24,16},{9,1},{17,9},{25,17},{10,2},{18,10},{26,18},{... | collective-permute-start | bytes 1179656 | tf_op jit(solution)/shard_map/ppermute | solution.py:31
  2.4 0.7 %pad_add_fusion = s32[1,40]{1,0:T(1,128)S(1)} fusion(s32[1,32]{1,0:T(1,128)} %param.7, s32[1,8]{1,0:T(1,128)} %bitcast.17), kind=kLoop, calls=%fused_computation | loop fusion | flops 40 | bytes 320 | tf_op jit(solution)/shard_map/concatenate | solution.py:274
  3.2 10.2 %all-gather = s32[8,1,128]{2,1,0:T(1,128)S(1)} all-gather(s32[1,1,128]{2,1,0:T(1,128)S(1)} %pad_bitcast_fusion), channel_id=1, replica_groups=mesh['section'=4,'tile'=8] {'tile'}, dimensions={0}, use_global_device_ids=true | all-gather | bytes 4608 | tf_op jit(solution)/shard_map/all_gather | solution.py:276
  13.4 0.0 copy-start
  13.4 1.6 %copy-done = bf16[2,256,2048]{2,1,0:T(8,128)(2,1)S(1)} copy-done((bf16[2,256,2048]{2,1,0:T(8,128)(2,1)S(1)}, bf16[2,256,2048]{2,1,0:T(8,128)(2,1)}, u32[]{:S(2)}) %copy-start) | copy-done | bytes 2097176
  15.0 1.8 %fetch.1 = (bf16[16,2,8,512]{3,2,1,0:T(8,128)(2,1)S(1)}, s32[2,16]{1,0:T(2,128)S(1)}) custom-call(s32[8,128]{1,0:T(8,128)S(1)} %bitcast.15, s32[1]{0:T(128)} %bitcast.5.place_ref, bf16[2,32,8,2048]{3,2,1,0:T(8,128)(2,1)S(1)} %bitcast.12), custom_call_target="tpu_custom_call" | custom-call | tf_op jit(solution)/shard_map/fetch/pallas_call | solution.py:107
  16.7 0.0 collective-permute-done
  16.8 1.6 %extend.1 = bf16[16,2,8,512]{3,2,1,0:T(8,128)(2,1)} custom-call(s32[2,16]{1,0:T(2,128)S(1)} %get-tuple-element.10.plan_ref, bf16[16,2,8,512]{3,2,1,0:T(8,128)(2,1)S(1)} %get-tuple-element.11.spans_ref, bf16[2,32,8,384]{3,2,1,0:T(8,128)(2,1)S(1)} %bitcast.14), custom_call_target="tpu_custom_call" | custom-call | tf_op jit(solution)/shard_map/extend/pallas_call | solution.py:116
  18.4 3.4 %all-to-all-start = ((bf16[8,2,2,8,512]{4,3,2,1,0:T(8,128)(2,1)}), bf16[8,2,2,8,512]{4,3,2,1,0:T(8,128)(2,1)S(1)}, u32[]{:S(2)}, u32[]{:S(2)}) async-start(bf16[8,2,2,8,512]{4,3,2,1,0:T(8,128)(2,1)} %bitcast.8), calls=%async_computation | async-start | bytes 524288 | tf_op jit(solution)/shard_map/all_to_all | solution.py:285
  21.8 0.0 copy-done.3
  21.8 2.0 %steer.1 = (bf16[128,2048]{1,0:T(8,128)(2,1)S(1)}, s32[2,8]{1,0:T(2,128)S(1)}) custom-call(s32[8]{0:T(128)S(1)} %bitcast.18, s32[1]{0:T(128)} %bitcast.1.place_ref, s32[8,128]{1,0:T(8,128)S(1)} %bitcast.16), custom_call_target="tpu_custom_call" | custom-call | tf_op jit(solution)/shard_map/steer/pallas_call | solution.py:190
  23.8 4.9 %all-to-all-done = bf16[8,2,2,8,512]{4,3,2,1,0:T(8,128)(2,1)S(1)} async-done(((bf16[8,2,2,8,512]{4,3,2,1,0:T(8,128)(2,1)}), bf16[8,2,2,8,512]{4,3,2,1,0:T(8,128)(2,1)S(1)}, u32[]{:S(2)}, u32[]{:S(2)}) %all-to-all-start) | async-done | bytes 262176 | tf_op jit(solution)/shard_map/all_to_all | solution.py:285
  28.7 0.0 copy-done.1
  28.7 0.0 copy-start.2
  28.7 1.0 %copy-done.2 = bf16[384,512]{1,0:T(8,128)(2,1)S(1)} copy-done((bf16[384,512]{1,0:T(8,128)(2,1)S(1)}, bf16[384,512]{1,0:T(8,128)(2,1)}, u32[]{:S(2)}) %copy-start.2) | copy-done | bytes 393240
  29.7 6.8 %image.1 = bf16[1024,2048]{1,0:T(8,128)(2,1)} custom-call(s32[2,8]{1,0:T(2,128)S(1)} %get-tuple-element.9.where_ref, bf16[16,2,8,512]{3,2,1,0:T(8,128)(2,1)S(1)} %bitcast.13, bf16[384,512]{1,0:T(8,128)(2,1)S(1)} %copy-done.2, bf16[128,2048]{1,0:T(8,128)(2,1)S(1)} %get-tuple-element.12.steer_ref, bf16[1024,256]{1,0:T(8,128)(2,1)S(1)} %copy-done.1), custom_call_target="tpu_custom_call" | custom-call | tf_op jit(solution)/shard_map/image/pallas_call | solution.py:241
  (1 shorter events, 0.0 us)
Async XLA Ops:
  0.0 28.7 %copy-start.1 = (bf16[1024,256]{1,0:T(8,128)(2,1)S(1)}, bf16[1024,256]{1,0:T(8,128)(2,1)}, u32[]{:S(2)}) copy-start(bf16[1024,256]{1,0:T(8,128)(2,1)} %constant.21.clone.interp_ref) | copy-start | bytes 1572868
  0.0 21.8 %copy-start.3 = (s32[1,1,8]{2,1,0:T(1,128)S(1)}, s32[1,1,8]{2,1,0:T(1,128)}, u32[]{:S(2)}) copy-start(s32[1,1,8]{2,1,0:T(1,128)} %param.6) | copy-start | bytes 100
  1.1 15.6 %collective-permute-start = (bf16[2,256,384]{2,1,0:T(8,128)(2,1)S(1)}, bf16[2,256,384]{2,1,0:T(8,128)(2,1)S(1)}, u32[]{:S(2)}, u32[]{:S(2)}) collective-permute-start(bf16[2,256,384]{2,1,0:T(8,128)(2,1)S(1)} %slice.3), channel_id=1, source_target_pairs={{8,0},{16,8},{24,16},{9,1},{17,9},{25,17},{10,2},{18,10},{26,18},{... | collective-permute-start | bytes 1179656 | tf_op jit(solution)/shard_map/ppermute | solution.py:31
  13.4 1.6 %copy-start = (bf16[2,256,2048]{2,1,0:T(8,128)(2,1)S(1)}, bf16[2,256,2048]{2,1,0:T(8,128)(2,1)}, u32[]{:S(2)}) copy-start(bf16[2,256,2048]{2,1,0:T(8,128)(2,1)} %param.5) | copy-start | bytes 6291460
  18.4 10.3 %all-to-all-start = ((bf16[8,2,2,8,512]{4,3,2,1,0:T(8,128)(2,1)}), bf16[8,2,2,8,512]{4,3,2,1,0:T(8,128)(2,1)S(1)}, u32[]{:S(2)}, u32[]{:S(2)}) async-start(bf16[8,2,2,8,512]{4,3,2,1,0:T(8,128)(2,1)} %bitcast.8), calls=%async_computation | async-start | bytes 524288 | tf_op jit(solution)/shard_map/all_to_all | solution.py:285
  28.7 1.0 %copy-start.2 = (bf16[384,512]{1,0:T(8,128)(2,1)S(1)}, bf16[384,512]{1,0:T(8,128)(2,1)}, u32[]{:S(2)}) copy-start(bf16[384,512]{1,0:T(8,128)(2,1)} %constant.20.clone.table_ref) | copy-start | bytes 1179652

commit v3 on v2

v3 whole, which is shorter than its diff:
```python
import functools
import math

import jax
import jax.numpy as jnp
import ml_dtypes
import numpy as np
from jax import lax
from jax.experimental import pallas as pl
from jax.experimental.pallas import tpu as pltpu
from jax.sharding import PartitionSpec as P

KC = 128
WIN = 256
PR = 1024
PC = 1024
NP = 8
CAP = 2
LANES = 128
PRIME = 65521
RIM = WIN + KC
SPAN = RIM + LANES
VMEM_BYTES = 24 << 20
SMALL_BYTES = 8 << 20
ROWS = 256
BF16 = jnp.bfloat16


def passed_along(value, axis, by):
    devices = lax.axis_size(axis)
    pairs = [(i, i + by) for i in range(devices) if 0 <= i + by < devices]
    return lax.ppermute(value, axis, pairs)


def correlation_table():
    lag = np.arange(RIM)[:, None] - np.arange(WIN)[None, :]
    inside = (lag >= 0) & (lag < KC)
    lag = np.where(inside, lag, 0)
    angle = (lag * lag % (2 * KC)).astype(np.float64) * (math.pi / KC)
    scale = 1.0 / math.sqrt(KC)
    real = np.where(inside, np.cos(angle) * scale, 0.0)
    imag = np.where(inside, np.sin(angle) * scale, 0.0)
    return np.concatenate([real, imag], axis=1).astype(np.float32).astype(ml_dtypes.bfloat16)


def interp_table():
    row = np.arange(PR, dtype=np.float64)[:, None]
    offset = np.arange(WIN, dtype=np.float64)[None, :] - ((row + 0.5) / (PR // WIN) - 0.5)
    taper = np.cos(offset * (math.pi / 8.0)) ** 2
    kernel = np.where(np.abs(offset) < 4.0, np.sinc(offset) * taper, 0.0)
    return kernel.astype(np.float32).astype(ml_dtypes.bfloat16)


def fetch_kernel(foot, notes_ref, place_ref, raw_ref, *refs):
    *out_refs, plan_ref, sem = refs
    blocks = raw_ref.shape[1]
    last = (raw_ref.shape[3] - SPAN) // LANES
    mine = place_ref[0]
    own_note = mine ^ place_ref[1]
    tiles = notes_ref.shape[0]
    each = tiles // len(out_refs)

    def plan(n, carry):
        lowest, highest = jnp.int32(blocks - 1), jnp.int32(0)
        for e in range(foot):
            block = notes_ref[n, e] - mine * blocks
            held = (block >= 0) & (block < blocks)
            lowest = jnp.where(held, jnp.minimum(lowest, block), lowest)
            highest = jnp.where(held, jnp.maximum(highest, block), highest)
        for slot, block in enumerate((lowest, highest)):
            plan_ref[0, CAP * n + slot] = block
            plan_ref[1, CAP * n + slot] = (notes_ref[own_note, foot + block] >> 7) - last
        return carry

    lax.fori_loop(0, tiles, plan, 0, unroll=tiles <= 8)
    for group, out_ref in enumerate(out_refs):

        def fetch(at, carry):
            n = group * each * CAP + at
            first = pl.multiple_of((last + jnp.minimum(plan_ref[1, n], 0)) * LANES, LANES)
            pltpu.make_async_copy(
                raw_ref.at[:, plan_ref[0, n], :, pl.ds(first, SPAN)], out_ref.at[at], sem
            ).start()
            return carry

        lax.fori_loop(0, each * CAP, fetch, 0, unroll=tiles <= 8)
    for out_ref in out_refs:
        pltpu.make_async_copy(out_ref, out_ref, sem).wait()
    for group, out_ref in enumerate(out_refs):

        def shift(at, carry):
            over = plan_ref[1, group * each * CAP + at]
            for beyond in range(1, SPAN // LANES):

                @pl.when(over == beyond)
                def _():
                    kept = SPAN - beyond * LANES
                    out_ref[at, :, :, :kept] = out_ref[at, :, :, SPAN - kept :]

            return carry

        lax.fori_loop(0, each * CAP, shift, 0, unroll=tiles <= 8)


def extend_kernel(count, plan_ref, rim_ref, after_ref, *refs):
    out_refs, sem = refs[count : 2 * count], refs[2 * count]
    each = out_refs[0].shape[0]

    def visit(act):
        for group, out_ref in enumerate(out_refs):

            def one(at, carry):
                n = group * each + at
                over = plan_ref[1, n]
                for beyond in range(1, SPAN // LANES):

                    @pl.when(over == beyond)
                    def _():
                        kept = SPAN - beyond * LANES
                        act(
                            pltpu.make_async_copy(
                                rim_ref.at[:, plan_ref[0, n], :, pl.ds(0, SPAN - kept)],
                                out_ref.at[at, :, :, pl.ds(kept, SPAN - kept)],
                                sem,
                            )
                        )

                return carry

            lax.fori_loop(0, each, one, 0, unroll=count * each <= 16)

    visit(lambda copy: copy.start())
    visit(lambda copy: copy.wait())


def cut_windows(foot, notes, place, raw, rim, groups, after):
    planes, _, per_block, _ = raw.shape
    chunks = notes.shape[0] * CAP
    smem = pl.BlockSpec(memory_space=pltpu.SMEM)
    vmem = pl.BlockSpec(memory_space=pltpu.VMEM)
    anywhere = pl.BlockSpec(memory_space=pl.ANY)
    params = pltpu.CompilerParams(vmem_limit_bytes=SMALL_BYTES)
    spans = (jax.ShapeDtypeStruct((chunks // groups, planes, per_block, SPAN), raw.dtype),) * groups
    *fetched, plan = pl.pallas_call(
        functools.partial(fetch_kernel, foot),
        out_shape=spans + (jax.ShapeDtypeStruct((2, chunks), jnp.int32),),
        in_specs=[smem, smem, pl.BlockSpec(memory_space=pltpu.HBM)],
        out_specs=(vmem,) * groups + (smem,),
        scratch_shapes=[pltpu.SemaphoreType.DMA],
        compiler_params=params,
        name="fetch",
    )(notes, place, pltpu.with_memory_space_constraint(raw, pltpu.HBM))
    return pl.pallas_call(
        functools.partial(extend_kernel, groups),
        out_shape=spans,
        in_specs=[smem, vmem] + [anywhere] * (1 + groups),
        out_specs=(anywhere,) * groups,
        input_output_aliases={3 + g: g for g in range(groups)},
        scratch_shapes=[pltpu.SemaphoreType.DMA],
        compiler_params=params,
        name="extend",
    )(plan, rim, after, *fetched)


def mod_prime(value):
    for _ in range(2):
        value = (value >> 16) * 15 + (value & 65535)
    return jnp.where(value >= PRIME, value - PRIME, value)


def place_entries(blocks, paired, list_ref, twist, notes_ref, where_ref):
    foot = list_ref.shape[0]

    def one(i, carry):
        block = list_ref[i]
        holder = block // blocks

        def also(j, second):
            other = list_ref[j]
            return second | ((other // blocks == holder) & (other < block)).astype(jnp.int32)

        second = lax.fori_loop(0, foot, also, jnp.int32(0), unroll=foot <= 8)
        position = holder ^ twist
        where_ref[0, i] = (position // 2 if paired else position) * CAP + second
        where_ref[1, i] = notes_ref[position, foot + block - holder * blocks] & (LANES - 1)
        where_ref[2, i] = (position & 1) if paired else 0
        return carry

    lax.fori_loop(0, foot, one, 0)


def steer_kernel(blocks, paired, list_ref, place_ref, notes_ref, table_ref, out_ref, where_ref, held_ref):
    foot = list_ref.shape[0]
    pulses = foot * NP
    width = lambda rows: lax.broadcasted_iota(jnp.int32, (rows, PC), 1)
    to_angle = jnp.float32(2.0 * math.pi / PRIME)
    first = place_ref[0]
    held_ref[...] = table_ref[...]

    def turned(steps, columns):
        scrambled = mod_prime((columns + first) * 40503)
        return mod_prime(steps * scrambled).astype(jnp.float32) * to_angle

    inner = turned(lax.broadcasted_iota(jnp.int32, (NP, PC), 0), width(NP))
    cos_in, sin_in = jnp.cos(inner), jnp.sin(inner)
    row = lax.broadcasted_iota(jnp.int32, (foot, PC), 0)
    ids = jnp.zeros((foot, PC), jnp.int32)
    for i in range(foot):
        ids = jnp.where(row == i, list_ref[i] * NP, ids)
    outer = turned(ids, width(foot))
    cos_out, sin_out = jnp.cos(outer), jnp.sin(outer)
    place_entries(blocks, paired, list_ref, place_ref[1], notes_ref, where_ref)
    for i in range(0, foot, 2):
        real, imag = [], []
        for j in (i, i + 1):
            c, s = cos_out[j : j + 1], sin_out[j : j + 1]
            real.append(c * cos_in - s * sin_in)
            imag.append(s * cos_in + c * sin_in)
        real = jnp.concatenate(real, axis=0).astype(BF16)
        imag = jnp.concatenate(imag, axis=0).astype(BF16)
        rows = pl.ds(i * NP, 2 * NP)
        below = pl.ds(pulses + i * NP, 2 * NP)
        out_ref[rows, :PC] = real
        out_ref[rows, PC:] = imag
        out_ref[below, :PC] = -imag
        out_ref[below, PC:] = real


def steering(my_list, place, notes, blocks, paired):
    foot = my_list.shape[0]
    smem = pl.BlockSpec(memory_space=pltpu.SMEM)
    vmem = pl.BlockSpec(memory_space=pltpu.VMEM)
    table = jnp.asarray(correlation_table())
    return pl.pallas_call(
        functools.partial(steer_kernel, blocks, paired),
        out_shape=(
            jax.ShapeDtypeStruct((2 * foot * NP, 2 * PC), BF16),
            jax.ShapeDtypeStruct((3, foot), jnp.int32),
            jax.ShapeDtypeStruct(table.shape, BF16),
        ),
        in_specs=[smem] * 3 + [vmem],
        out_specs=(vmem, smem, vmem),
        compiler_params=pltpu.CompilerParams(vmem_limit_bytes=SMALL_BYTES),
        name="steer",
    )(my_list, place, notes, table)


def image_kernel(where_ref, direct_ref, sibling_ref, table_ref, steer_ref, interp_ref, out_ref, echo, wins, focused, pixels, sem):
    pulses = echo.shape[0] // 2
    foot = pulses // NP
    for i in range(0, foot, 2):
        both = []
        for j in (i, i + 1):
            chunk = where_ref[0, j]
            piece = direct_ref[chunk].astype(jnp.float32)
            if sibling_ref is not None:
                other = sibling_ref[chunk].astype(jnp.float32)
                piece = jnp.where(where_ref[2, j] == 1, other, piece)
            turn = lax.rem(SPAN - where_ref[1, j], SPAN)
            both.append(pltpu.roll(piece.reshape(2 * NP, SPAN), turn, 1)[:, :RIM])
        for plane in range(2):
            part = slice(plane * NP, (plane + 1) * NP)
            echo[pl.ds(plane * pulses + i * NP, 2 * NP), :] = jnp.concatenate(
                [both[0][part], both[1][part]], axis=0
            ).astype(BF16)
    sums = jnp.dot(echo[...], table_ref[...], preferred_element_type=jnp.float32)
    real = sums[:pulses, :WIN] + sums[pulses:, WIN:]
    imag = sums[pulses:, :WIN] - sums[:pulses, WIN:]
    wins[...] = jnp.concatenate([real, imag], axis=0).T.astype(BF16)
    scale = jnp.float32(1.0 / math.sqrt(pulses))
    focused[...] = (
        jnp.dot(wins[...], steer_ref[...], preferred_element_type=jnp.float32) * scale
    ).astype(BF16)
    copies = []
    for step in range(PR // ROWS):
        rows = pl.ds(step * ROWS, ROWS)
        pixels[rows, :] = jnp.dot(
            interp_ref[rows, :], focused[...], preferred_element_type=jnp.float32
        ).astype(BF16)
        copy = pltpu.make_async_copy(pixels.at[rows], out_ref.at[rows], sem.at[step])
        copy.start()
        copies.append(copy)
    for copy in copies:
        copy.wait()


def tile_image(direct, sibling, where, steer, table):
    foot = where.shape[1]
    pulses = foot * NP
    vmem = pl.BlockSpec(memory_space=pltpu.VMEM)
    operands = [direct] + ([] if sibling is None else [sibling])

    def kernel(where_ref, direct_ref, *refs):
        refs = refs if sibling is not None else (None,) + refs
        image_kernel(where_ref, direct_ref, *refs)

    return pl.pallas_call(
        kernel,
        out_shape=jax.ShapeDtypeStruct((PR, 2 * PC), BF16),
        in_specs=[pl.BlockSpec(memory_space=pltpu.SMEM)] + [vmem] * (len(operands) + 3),
        out_specs=pl.BlockSpec(memory_space=pltpu.HBM),
        scratch_shapes=[
            pltpu.VMEM((2 * pulses, RIM), BF16),
            pltpu.VMEM((WIN, 2 * pulses), BF16),
            pltpu.VMEM((WIN, 2 * PC), BF16),
            pltpu.VMEM((PR, 2 * PC), BF16),
            pltpu.SemaphoreType.DMA((PR // ROWS,)),
        ],
        compiler_params=pltpu.CompilerParams(vmem_limit_bytes=VMEM_BYTES),
        name="image",
    )(where, *operands, table, steer, jnp.asarray(interp_table()))


def swapped(value, turn):
    tiles = lax.axis_size("tile")
    return lax.ppermute(value, "tile", [(i, i ^ turn) for i in range(tiles)])


def gather_notes(note):
    pair = jnp.concatenate([note, swapped(note, 1)], axis=0)
    return jnp.concatenate([pair] + [swapped(pair, 2 * c) for c in range(1, 4)], axis=0)


def exchange(spans):
    got = [spans[0]] + [swapped(spans[c], 2 * c) for c in range(1, 4)]
    theirs = jnp.concatenate([part[CAP:] for part in got], axis=0)
    ours = jnp.concatenate([part[:CAP] for part in got], axis=0)
    return ours, swapped(theirs, 1)


def local(raw_echo, footprint, window_start):
    planes, pulses, bins = raw_echo.shape
    blocks = pulses // NP
    tiles = lax.axis_size("tile")
    paired = tiles == 8
    foot = footprint.shape[2]
    tile_pos = lax.axis_index("tile").astype(jnp.int32)
    row_pos = lax.axis_index("section").astype(jnp.int32)
    my_list = footprint[0, 0]

    rim = passed_along(raw_echo[:, :, :RIM], "section", -1)
    note = jnp.concatenate([footprint[0], window_start], axis=1)
    note = jnp.pad(note, ((0, 0), (0, -note.shape[1] % LANES)))
    notes = gather_notes(note) if paired else lax.all_gather(note, "tile", axis=0, tiled=True)
    twist = tile_pos if paired else jnp.int32(0)

    first_column = tile_pos * PC + 1 + 7 * row_pos
    place = jnp.stack([first_column, twist])
    steer, where, table = steering(my_list, place, notes, blocks, paired)

    spans = cut_windows(
        foot,
        notes,
        jnp.stack([tile_pos, twist]),
        raw_echo.reshape(planes, blocks, NP, bins),
        rim.reshape(planes, blocks, NP, RIM),
        4 if paired else 1,
        steer,
    )
    if paired:
        direct, sibling = exchange(spans)
    else:
        sent = spans[0].reshape((tiles, CAP) + spans[0].shape[1:])
        direct = lax.all_to_all(sent, "tile", 0, 0, tiled=True).reshape(spans[0].shape)
        sibling = None

    image = tile_image(direct, sibling, where, steer, table)
    return image[None, None]


def solution(mesh):
    in_specs = (P(None, "tile", "section"), P("section", "tile", None), P("section", "tile"))
    out_specs = P("section", "tile", None, None)
    return jax.shard_map(local, mesh=mesh, in_specs=in_specs, out_specs=out_specs, check_vma=False)
```

time: 36.8 us -> 32.2 us (0.88)
  blocking collectives: 10.2 us -> 0 us
  starting transfers between devices: 4.7 us -> 9.75 us
  waiting for transfers between devices: 4.86 us -> 9.08 us
  Pallas kernels: 12.2 us -> 9.27 us
  local copies, waits for them, and re-layouts: 3.71 us -> 2.79 us
    all_gather x1 -> x0, blocking collectives: 10.2 us -> none  [local(): notes = lax.all_gather(note, 'tile', axis=0, tiled=True)]
    ppermute x0 -> x8, waiting for transfers between devices: none -> 9.07 us  [swapped(): return lax.ppermute(value, 'tile', [(i, i ^ turn) for i in range(tiles)])]
    ppermute x0 -> x8, starting transfers between devices: none -> 8.46 us  [swapped(): return lax.ppermute(value, 'tile', [(i, i ^ turn) for i in range(tiles)])]
    all_to_all x1 -> x0, waiting for transfers between devices: 4.86 us -> none  [local(): lax.all_to_all(sent.reshape((tiles, CAP) + sent.shape[1:]), 'tile', 0, 0,...]
    all_to_all x1 -> x0, starting transfers between devices: 3.41 us -> none  [local(): lax.all_to_all(sent.reshape((tiles, CAP) + sent.shape[1:]), 'tile', 0, 0,...]
    pallas_call x4, Pallas kernels: 12.2 us -> 9.27 us  [the longest x1 3.78 us: tile_image(): pl.pallas_call(kernel, out_shape=jax.ShapeDtypeStruct((PR, 2 * PC), BF16)...]
    unnamed x9 -> x6, local copies, waits for them, and re-layouts: 2.6 us -> 1.65 us
  transfers between devices with their start and end apart: 2 -> 9, of which waited for: 1 -> 8; matrix products, arithmetic and copies ran while one was open for 2% -> 3% of each run, Pallas kernels for 10% -> 14%
where the time goes in v3:
time: 32.2 us; the launch traced here: 31.8 us
  starting transfers between devices  9.75 us (30%)
  Pallas kernels  9.27 us (29%)
  waiting for transfers between devices  9.08 us (28%)
  local copies, waits for them, and re-layouts  2.79 us (9%)
  other arithmetic  0.87 us (3%)
    ppermute x8, waiting for transfers between devices, swapped(): return lax.ppermute(value, 'tile', [(i, i ^ turn) for i in range(tiles)])  9.07 us
    ppermute x8, starting transfers between devices, swapped(): return lax.ppermute(value, 'tile', [(i, i ^ turn) for i in range(tiles)])  8.46 us
    pallas_call x1, Pallas kernels, tile_image(): pl.pallas_call(kernel, out_shape=jax.ShapeDtypeStruct((PR, 2 * PC), BF16)...  3.78 us
    pallas_call x1, Pallas kernels, cut_windows(): pl.pallas_call(functools.partial(fetch_kernel, foot), out_shape=spans + (...  2.44 us
    pallas_call x1, Pallas kernels, steering(): pl.pallas_call(functools.partial(steer_kernel, blocks, paired), out_shape...  2.06 us
    unnamed x6, local copies, waits for them, and re-layouts  1.65 us
    ppermute x1, starting transfers between devices, passed_along(): return lax.ppermute(value, axis, pairs)  1.29 us
    slice x1, local copies, waits for them, and re-layouts, local(): rim = passed_along(raw_echo[:, :, :RIM], 'section', -1)  1.09 us
  transfers between devices with their start and end apart: 9, of which 8 were waited for; matrix products, arithmetic and copies ran while one was open for 3% of the time, Pallas kernels for 14%

profile of v3, /device:TPU:0, one launch (start us, length us, event | category | flops | bytes accessed | tf_op | source)
XLA Modules:
  0.0 31.8 jit_solution(6126654189452420022)
XLA Ops:
  0.0 0.0 copy-start
  0.0 1.1 %slice.27 = bf16[2,256,384]{2,1,0:T(8,128)(2,1)S(1)} slice(bf16[2,256,2048]{2,1,0:T(8,128)(2,1)} %param.5), slice={[0:2], [0:256], [0:384]} | slice | bytes 786432 | tf_op jit(solution)/shard_map/slice | solution.py:341
  1.1 1.3 %collective-permute-start.4 = (bf16[2,256,384]{2,1,0:T(8,128)(2,1)S(1)}, bf16[2,256,384]{2,1,0:T(8,128)(2,1)S(1)}, u32[]{:S(2)}, u32[]{:S(2)}) collective-permute-start(bf16[2,256,384]{2,1,0:T(8,128)(2,1)S(1)} %slice.27), channel_id=1, source_target_pairs={{8,0},{16,8},{24,16},{9,1},{17,9},{25,17},{10,2},{18,10},{26,18},{... | collective-permute-start | bytes 1179656 | tf_op jit(solution)/shard_map/ppermute | solution.py:32
  2.4 0.7 %pad_add_fusion.2 = s32[1,40]{1,0:T(1,128)S(1)} fusion(s32[1,32]{1,0:T(1,128)} %param.7, s32[1,8]{1,0:T(1,128)} %bitcast.8), kind=kLoop, calls=%fused_computation.4 | loop fusion | flops 40 | bytes 320 | tf_op jit(solution)/shard_map/concatenate | solution.py:342
  3.2 0.5 %collective-permute-start = (s32[1,128]{1,0:T(1,128)S(1)}, s32[1,128]{1,0:T(1,128)S(1)}, u32[]{:S(2)}, u32[]{:S(2)}) collective-permute-start(s32[1,128]{1,0:T(1,128)S(1)} %pad.4), channel_id=1, source_target_pairs={{0,1},{1,0},{2,3},{3,2},{4,5},{5,4},{6,7},{7,6},{8,9},{9,8},{10,11... | collective-permute-start | bytes 1544 | tf_op jit(solution)/shard_map/ppermute | solution.py:316
  3.6 0.8 %collective-permute-done = s32[1,128]{1,0:T(1,128)S(1)} collective-permute-done((s32[1,128]{1,0:T(1,128)S(1)}, s32[1,128]{1,0:T(1,128)S(1)}, u32[]{:S(2)}, u32[]{:S(2)}) %collective-permute-start) | collective-permute-done | bytes 544 | tf_op jit(solution)/shard_map/ppermute | solution.py:316
  4.4 3.7 %collective-permute-start.3 = (s32[2,128]{1,0:T(2,128)S(1)}, s32[2,128]{1,0:T(2,128)S(1)}, u32[]{:S(2)}, u32[]{:S(2)}) collective-permute-start(s32[2,128]{1,0:T(2,128)S(1)} %pad_add_fusion), channel_id=1, source_target_pairs={{0,6},{1,7},{2,4},{3,5},{4,2},{5,3},{6,0},{7,1},{8,14},{9,15},{10,... | collective-permute-start | bytes 3080 | tf_op jit(solution)/shard_map/ppermute | solution.py:316
  8.2 0.5 %collective-permute-start.2 = (s32[2,128]{1,0:T(2,128)S(1)}, s32[2,128]{1,0:T(2,128)S(1)}, u32[]{:S(2)}, u32[]{:S(2)}) collective-permute-start(s32[2,128]{1,0:T(2,128)S(1)} %pad_add_fusion), channel_id=1, source_target_pairs={{0,4},{1,5},{2,6},{3,7},{4,0},{5,1},{6,2},{7,3},{8,12},{9,13},{10,... | collective-permute-start | bytes 3080 | tf_op jit(solution)/shard_map/ppermute | solution.py:316
  8.7 0.1 collective-permute-start.1
  8.8 0.1 pad_add_fusion.1
  8.9 0.8 %collective-permute-done.3 = s32[2,128]{1,0:T(2,128)S(1)} collective-permute-done((s32[2,128]{1,0:T(2,128)S(1)}, s32[2,128]{1,0:T(2,128)S(1)}, u32[]{:S(2)}, u32[]{:S(2)}) %collective-permute-start.3) | collective-permute-done | bytes 1056 | tf_op jit(solution)/shard_map/ppermute | solution.py:316
  9.7 2.0 %collective-permute-done.2 = s32[2,128]{1,0:T(2,128)S(1)} collective-permute-done((s32[2,128]{1,0:T(2,128)S(1)}, s32[2,128]{1,0:T(2,128)S(1)}, u32[]{:S(2)}, u32[]{:S(2)}) %collective-permute-start.2) | collective-permute-done | bytes 1056 | tf_op jit(solution)/shard_map/ppermute | solution.py:316
  11.8 0.5 %collective-permute-done.1 = s32[2,128]{1,0:T(2,128)S(1)} collective-permute-done((s32[2,128]{1,0:T(2,128)S(1)}, s32[2,128]{1,0:T(2,128)S(1)}, u32[]{:S(2)}, u32[]{:S(2)}) %collective-permute-start.1) | collective-permute-done | bytes 1056 | tf_op jit(solution)/shard_map/ppermute | solution.py:316
  12.3 2.4 %fetch.1 = (bf16[4,2,8,512]{3,2,1,0:T(8,128)(2,1)S(1)}, bf16[4,2,8,512]{3,2,1,0:T(8,128)(2,1)S(1)}, bf16[4,2,8,512]{3,2,1,0:T(8,128)(2,1)S(1)}, bf16[4,2,8,512]{3,2,1,0:T(8,128)(2,1)S(1)}, s32[2,16]{1,0:T(2,128)S(1)}) custom-call(s32[8,128]{1,0:T(8,128)S(1)} %concatenate.18.notes_ref, s32[2]{0:T(128)S(1)} %get-tuple-element.38.place_ref, ...), custom_call_target="tpu_custom_call" | custom-call | tf_op jit(solution)/shard_map/fetch/pallas_call | solution.py:144
  14.7 0.0 copy-start.1
  14.7 1.0 %copy-done.1 = bf16[384,512]{1,0:T(8,128)(2,1)S(1)} copy-done((bf16[384,512]{1,0:T(8,128)(2,1)S(1)}, bf16[384,512]{1,0:T(8,128)(2,1)}, u32[]{:S(2)}) %copy-start.1) | copy-done | bytes 393240
  15.7 0.0 copy-start.2
  15.7 0.7 %copy-done.2 = s32[1,1,8]{2,1,0:T(1,128)S(1)} copy-done((s32[1,1,8]{2,1,0:T(1,128)S(1)}, s32[1,1,8]{2,1,0:T(1,128)}, u32[]{:S(2)}) %copy-start.2) | copy-done | bytes 56
  16.4 2.1 %steer.1 = (bf16[128,2048]{1,0:T(8,128)(2,1)S(1)}, s32[3,8]{1,0:T(4,128)S(1)}, bf16[384,512]{1,0:T(8,128)(2,1)S(1)}) custom-call(s32[8]{0:T(128)S(1)} %bitcast.9, s32[2]{0:T(128)S(1)} %get-tuple-element.37.place_ref, s32[8,128]{1,0:T(8,128)S(1)} %concatenate.18.notes_ref, bf16[384,512]{1,0:T(8,128)(2,1)S(1)} %copy-done.1), custom_call_target="tpu_custom_call" | custom-call | tf_op jit(solution)/shard_map/steer/pallas_call | solution.py:234
  18.4 0.0 collective-permute-done.4
  18.5 1.0 %extend.1 = (bf16[4,2,8,512]{3,2,1,0:T(8,128)(2,1)S(1)}, bf16[4,2,8,512]{3,2,1,0:T(8,128)(2,1)S(1)}, bf16[4,2,8,512]{3,2,1,0:T(8,128)(2,1)S(1)}, bf16[4,2,8,512]{3,2,1,0:T(8,128)(2,1)S(1)}) custom-call(s32[2,16]{1,0:T(2,128)S(1)} %get-tuple-element.18.plan_ref, ...), custom_call_target="tpu_custom_call", output_to_operand_aliasing={{0}: (3, {}), {1}: (4, {}), {2}: (5, {}), {3}: (6, {})} | custom-call | tf_op jit(solution)/shard_map/extend/pallas_call | solution.py:153
  19.5 0.1 collective-permute-start.5
  19.6 1.8 %collective-permute-start.6 = (bf16[4,2,8,512]{3,2,1,0:T(8,128)(2,1)S(1)}, bf16[4,2,8,512]{3,2,1,0:T(8,128)(2,1)S(1)}, u32[]{:S(2)}, u32[]{:S(2)}) collective-permute-start(bf16[4,2,8,512]{3,2,1,0:T(8,128)(2,1)S(1)} %get-tuple-element.26), channel_id=1, source_target_pairs={{0,4},{1,5},{2,6},{3,7},{4,0},{5,1},{6,2},{7,3},{8,12},{9,13},{10,... | collective-permute-start | bytes 196616 | tf_op jit(solution)/shard_map/ppermute | solution.py:316
  21.5 1.6 %collective-permute-start.7 = (bf16[4,2,8,512]{3,2,1,0:T(8,128)(2,1)S(1)}, bf16[4,2,8,512]{3,2,1,0:T(8,128)(2,1)S(1)}, u32[]{:S(2)}, u32[]{:S(2)}) collective-permute-start(bf16[4,2,8,512]{3,2,1,0:T(8,128)(2,1)S(1)} %get-tuple-element.27), channel_id=1, source_target_pairs={{0,6},{1,7},{2,4},{3,5},{4,2},{5,3},{6,0},{7,1},{8,14},{9,15},{10,... | collective-permute-start | bytes 196616 | tf_op jit(solution)/shard_map/ppermute | solution.py:316
  23.0 0.8 %collective-permute-done.5 = bf16[4,2,8,512]{3,2,1,0:T(8,128)(2,1)S(1)} collective-permute-done((bf16[4,2,8,512]{3,2,1,0:T(8,128)(2,1)S(1)}, bf16[4,2,8,512]{3,2,1,0:T(8,128)(2,1)S(1)}, u32[]{:S(2)}, u32[]{:S(2)}) %collective-permute-start.5) | collective-permute-done | bytes 65568 | tf_op jit(solution)/shard_map/ppermute | solution.py:316
  23.8 0.8 %collective-permute-done.6 = bf16[4,2,8,512]{3,2,1,0:T(8,128)(2,1)S(1)} collective-permute-done((bf16[4,2,8,512]{3,2,1,0:T(8,128)(2,1)S(1)}, bf16[4,2,8,512]{3,2,1,0:T(8,128)(2,1)S(1)}, u32[]{:S(2)}, u32[]{:S(2)}) %collective-permute-start.6) | collective-permute-done | bytes 65568 | tf_op jit(solution)/shard_map/ppermute | solution.py:316
  24.6 2.0 %collective-permute-done.7 = bf16[4,2,8,512]{3,2,1,0:T(8,128)(2,1)S(1)} collective-permute-done((bf16[4,2,8,512]{3,2,1,0:T(8,128)(2,1)S(1)}, bf16[4,2,8,512]{3,2,1,0:T(8,128)(2,1)S(1)}, u32[]{:S(2)}, u32[]{:S(2)}) %collective-permute-start.7) | collective-permute-done | bytes 65568 | tf_op jit(solution)/shard_map/ppermute | solution.py:316
  26.7 0.1 collective-permute-start.8
  26.8 1.3 %collective-permute-done.8.refs_0_ = bf16[8,2,8,512]{3,2,1,0:T(8,128)(2,1)S(1)} collective-permute-done((bf16[8,2,8,512]{3,2,1,0:T(8,128)(2,1)S(1)}, bf16[8,2,8,512]{3,2,1,0:T(8,128)(2,1)S(1)}, u32[]{:S(2)}, u32[]{:S(2)}) %collective-permute-start.8) | collective-permute-done | bytes 131104 | tf_op jit(solution)/shard_map/ppermute | solution.py:316
  28.1 0.0 copy-done
  28.1 3.8 %image.1 = bf16[1024,2048]{1,0:T(8,128)(2,1)} custom-call(s32[3,8]{1,0:T(4,128)S(1)} %get-tuple-element.17.where_ref, bf16[8,2,8,512]{3,2,1,0:T(8,128)(2,1)S(1)} %pad_maximum_fusion.direct_ref, bf16[8,2,8,512]{3,2,1,0:T(8,128)(2,1)S(1)} %collective-permute-done.8.refs_0_, bf16[384,512]{1,0:T(8,128)(2,1)S(1)} %get-tuple-element.28.refs_1_, ...), custom_call_target="tpu_custom_call" | custom-call | tf_op jit(solution)/shard_map/image/pallas_call | solution.py:297
  (9 shorter events, 0.1 us)
Async XLA Ops:
  0.0 28.1 %copy-start = (bf16[1024,256]{1,0:T(8,128)(2,1)S(1)}, bf16[1024,256]{1,0:T(8,128)(2,1)}, u32[]{:S(2)}) copy-start(bf16[1024,256]{1,0:T(8,128)(2,1)} %constant.21.clone.refs_3_) | copy-start | bytes 1572868
  1.1 17.4 %collective-permute-start.4 = (bf16[2,256,384]{2,1,0:T(8,128)(2,1)S(1)}, bf16[2,256,384]{2,1,0:T(8,128)(2,1)S(1)}, u32[]{:S(2)}, u32[]{:S(2)}) collective-permute-start(bf16[2,256,384]{2,1,0:T(8,128)(2,1)S(1)} %slice.27), channel_id=1, source_target_pairs={{8,0},{16,8},{24,16},{9,1},{17,9},{25,17},{10,2},{18,10},{26,18},{... | collective-permute-start | bytes 1179656 | tf_op jit(solution)/shard_map/ppermute | solution.py:32
  3.2 1.3 %collective-permute-start = (s32[1,128]{1,0:T(1,128)S(1)}, s32[1,128]{1,0:T(1,128)S(1)}, u32[]{:S(2)}, u32[]{:S(2)}) collective-permute-start(s32[1,128]{1,0:T(1,128)S(1)} %pad.4), channel_id=1, source_target_pairs={{0,1},{1,0},{2,3},{3,2},{4,5},{5,4},{6,7},{7,6},{8,9},{9,8},{10,11... | collective-permute-start | bytes 1544 | tf_op jit(solution)/shard_map/ppermute | solution.py:316
  4.4 5.3 %collective-permute-start.3 = (s32[2,128]{1,0:T(2,128)S(1)}, s32[2,128]{1,0:T(2,128)S(1)}, u32[]{:S(2)}, u32[]{:S(2)}) collective-permute-start(s32[2,128]{1,0:T(2,128)S(1)} %pad_add_fusion), channel_id=1, source_target_pairs={{0,6},{1,7},{2,4},{3,5},{4,2},{5,3},{6,0},{7,1},{8,14},{9,15},{10,... | collective-permute-start | bytes 3080 | tf_op jit(solution)/shard_map/ppermute | solution.py:316
  8.2 3.6 %collective-permute-start.2 = (s32[2,128]{1,0:T(2,128)S(1)}, s32[2,128]{1,0:T(2,128)S(1)}, u32[]{:S(2)}, u32[]{:S(2)}) collective-permute-start(s32[2,128]{1,0:T(2,128)S(1)} %pad_add_fusion), channel_id=1, source_target_pairs={{0,4},{1,5},{2,6},{3,7},{4,0},{5,1},{6,2},{7,3},{8,12},{9,13},{10,... | collective-permute-start | bytes 3080 | tf_op jit(solution)/shard_map/ppermute | solution.py:316
  8.7 3.6 %collective-permute-start.1 = (s32[2,128]{1,0:T(2,128)S(1)}, s32[2,128]{1,0:T(2,128)S(1)}, u32[]{:S(2)}, u32[]{:S(2)}) collective-permute-start(s32[2,128]{1,0:T(2,128)S(1)} %pad_add_fusion), channel_id=1, source_target_pairs={{0,2},{1,3},{2,0},{3,1},{4,6},{5,7},{6,4},{7,5},{8,10},{9,11},{10,... | collective-permute-start | bytes 3080 | tf_op jit(solution)/shard_map/ppermute | solution.py:316
  14.7 1.0 %copy-start.1 = (bf16[384,512]{1,0:T(8,128)(2,1)S(1)}, bf16[384,512]{1,0:T(8,128)(2,1)}, u32[]{:S(2)}) copy-start(bf16[384,512]{1,0:T(8,128)(2,1)} %constant.20.clone.table_ref) | copy-start | bytes 1179652
  15.7 0.7 %copy-start.2 = (s32[1,1,8]{2,1,0:T(1,128)S(1)}, s32[1,1,8]{2,1,0:T(1,128)}, u32[]{:S(2)}) copy-start(s32[1,1,8]{2,1,0:T(1,128)} %param.6) | copy-start | bytes 100
  19.5 4.3 %collective-permute-start.5 = (bf16[4,2,8,512]{3,2,1,0:T(8,128)(2,1)S(1)}, bf16[4,2,8,512]{3,2,1,0:T(8,128)(2,1)S(1)}, u32[]{:S(2)}, u32[]{:S(2)}) collective-permute-start(bf16[4,2,8,512]{3,2,1,0:T(8,128)(2,1)S(1)} %get-tuple-element.25), channel_id=1, source_target_pairs={{0,2},{1,3},{2,0},{3,1},{4,6},{5,7},{6,4},{7,5},{8,10},{9,11},{10,... | collective-permute-start | bytes 196616 | tf_op jit(solution)/shard_map/ppermute | solution.py:316
  19.6 5.0 %collective-permute-start.6 = (bf16[4,2,8,512]{3,2,1,0:T(8,128)(2,1)S(1)}, bf16[4,2,8,512]{3,2,1,0:T(8,128)(2,1)S(1)}, u32[]{:S(2)}, u32[]{:S(2)}) collective-permute-start(bf16[4,2,8,512]{3,2,1,0:T(8,128)(2,1)S(1)} %get-tuple-element.26), channel_id=1, source_target_pairs={{0,4},{1,5},{2,6},{3,7},{4,0},{5,1},{6,2},{7,3},{8,12},{9,13},{10,... | collective-permute-start | bytes 196616 | tf_op jit(solution)/shard_map/ppermute | solution.py:316
  21.5 5.2 %collective-permute-start.7 = (bf16[4,2,8,512]{3,2,1,0:T(8,128)(2,1)S(1)}, bf16[4,2,8,512]{3,2,1,0:T(8,128)(2,1)S(1)}, u32[]{:S(2)}, u32[]{:S(2)}) collective-permute-start(bf16[4,2,8,512]{3,2,1,0:T(8,128)(2,1)S(1)} %get-tuple-element.27), channel_id=1, source_target_pairs={{0,6},{1,7},{2,4},{3,5},{4,2},{5,3},{6,0},{7,1},{8,14},{9,15},{10,... | collective-permute-start | bytes 196616 | tf_op jit(solution)/shard_map/ppermute | solution.py:316
  26.7 1.4 %collective-permute-start.8 = (bf16[8,2,8,512]{3,2,1,0:T(8,128)(2,1)S(1)}, bf16[8,2,8,512]{3,2,1,0:T(8,128)(2,1)S(1)}, u32[]{:S(2)}, u32[]{:S(2)}) collective-permute-start(bf16[8,2,8,512]{3,2,1,0:T(8,128)(2,1)S(1)} %pad_maximum_fusion.1), channel_id=1, source_target_pairs={{0,1},{1,0},{2,3},{3,2},{4,5},{5,4},{6,7},{7,6},{8,9},{9,8},{10,11... | collective-permute-start | bytes 393224 | tf_op jit(solution)/shard_map/ppermute | solution.py:316

commit v4 on v3

--- a/solution.py
+++ b/solution.py
@@ -51,8 +51,29 @@
     return kernel.astype(np.float32).astype(ml_dtypes.bfloat16)
 
 
+def place_entries(foot, blocks, paired, mine, twist, notes_ref, where_ref):
+    own_note = mine ^ twist
+
+    def one(i, carry):
+        block = notes_ref[own_note, i]
+        holder = block // blocks
+
+        def also(j, second):
+            other = notes_ref[own_note, j]
+            return second | ((other // blocks == holder) & (other < block)).astype(jnp.int32)
+
+        second = lax.fori_loop(0, foot, also, jnp.int32(0), unroll=foot <= 8)
+        position = holder ^ twist
+        where_ref[0, i] = (position // 2 if paired else position) * CAP + second
+        where_ref[1, i] = notes_ref[position, foot + block - holder * blocks] & (LANES - 1)
+        where_ref[2, i] = (position & 1) if paired else 0
+        return carry
+
+    lax.fori_loop(0, foot, one, 0, unroll=foot <= 8)
+
+
 def fetch_kernel(foot, notes_ref, place_ref, raw_ref, *refs):
-    *out_refs, plan_ref, sem = refs
+    *out_refs, plan_ref, where_ref, sem = refs
     blocks = raw_ref.shape[1]
     last = (raw_ref.shape[3] - SPAN) // LANES
     mine = place_ref[0]
@@ -84,6 +105,7 @@
             return carry
 
         lax.fori_loop(0, each * CAP, fetch, 0, unroll=tiles <= 8)
+    place_entries(foot, blocks, len(out_refs) > 1, mine, place_ref[1], notes_ref, where_ref)
     for out_ref in out_refs:
         pltpu.make_async_copy(out_ref, out_ref, sem).wait()
     for group, out_ref in enumerate(out_refs):
@@ -102,7 +124,7 @@
         lax.fori_loop(0, each * CAP, shift, 0, unroll=tiles <= 8)
 
 
-def extend_kernel(count, plan_ref, rim_ref, after_ref, *refs):
+def extend_kernel(count, plan_ref, rim_ref, *refs):
     out_refs, sem = refs[count : 2 * count], refs[2 * count]
     each = out_refs[0].shape[0]
 
@@ -133,7 +155,7 @@
     visit(lambda copy: copy.wait())
 
 
-def cut_windows(foot, notes, place, raw, rim, groups, after):
+def cut_windows(foot, notes, place, raw, rim, groups):
     planes, _, per_block, _ = raw.shape
     chunks = notes.shape[0] * CAP
     smem = pl.BlockSpec(memory_space=pltpu.SMEM)
@@ -141,25 +163,30 @@
     anywhere = pl.BlockSpec(memory_space=pl.ANY)
     params = pltpu.CompilerParams(vmem_limit_bytes=SMALL_BYTES)
     spans = (jax.ShapeDtypeStruct((chunks // groups, planes, per_block, SPAN), raw.dtype),) * groups
-    *fetched, plan = pl.pallas_call(
+    *fetched, plan, where = pl.pallas_call(
         functools.partial(fetch_kernel, foot),
-        out_shape=spans + (jax.ShapeDtypeStruct((2, chunks), jnp.int32),),
+        out_shape=spans
+        + (
+            jax.ShapeDtypeStruct((2, chunks), jnp.int32),
+            jax.ShapeDtypeStruct((3, foot), jnp.int32),
+        ),
         in_specs=[smem, smem, pl.BlockSpec(memory_space=pltpu.HBM)],
-        out_specs=(vmem,) * groups + (smem,),
+        out_specs=(vmem,) * groups + (smem, smem),
         scratch_shapes=[pltpu.SemaphoreType.DMA],
         compiler_params=params,
         name="fetch",
     )(notes, place, pltpu.with_memory_space_constraint(raw, pltpu.HBM))
-    return pl.pallas_call(
+    spans = pl.pallas_call(
         functools.partial(extend_kernel, groups),
         out_shape=spans,
-        in_specs=[smem, vmem] + [anywhere] * (1 + groups),
+        in_specs=[smem, vmem] + [anywhere] * groups,
         out_specs=(anywhere,) * groups,
-        input_output_aliases={3 + g: g for g in range(groups)},
+        input_output_aliases={2 + g: g for g in range(groups)},
         scratch_shapes=[pltpu.SemaphoreType.DMA],
         compiler_params=params,
         name="extend",
-    )(plan, rim, after, *fetched)
+    )(plan, rim, *fetched)
+    return spans, where
 
 
 def mod_prime(value):
@@ -168,34 +195,14 @@
     return jnp.where(value >= PRIME, value - PRIME, value)
 
 
-def place_entries(blocks, paired, list_ref, twist, notes_ref, where_ref):
-    foot = list_ref.shape[0]
-
-    def one(i, carry):
-        block = list_ref[i]
-        holder = block // blocks
-
-        def also(j, second):
-            other = list_ref[j]
-            return second | ((other // blocks == holder) & (other < block)).astype(jnp.int32)
-
-        second = lax.fori_loop(0, foot, also, jnp.int32(0), unroll=foot <= 8)
-        position = holder ^ twist
-        where_ref[0, i] = (position // 2 if paired else position) * CAP + second
-        where_ref[1, i] = notes_ref[position, foot + block - holder * blocks] & (LANES - 1)
-        where_ref[2, i] = (position & 1) if paired else 0
-        return carry
-
-    lax.fori_loop(0, foot, one, 0)
-
-
-def steer_kernel(blocks, paired, list_ref, place_ref, notes_ref, table_ref, out_ref, where_ref, held_ref):
-    foot = list_ref.shape[0]
-    pulses = foot * NP
+def steer_kernel(note_ref, place_ref, table_ref, out_ref, held_ref, sem):
+    pulses = out_ref.shape[0] // 2
+    foot = pulses // NP
+    holding = pltpu.make_async_copy(table_ref, held_ref, sem)
+    holding.start()
     width = lambda rows: lax.broadcasted_iota(jnp.int32, (rows, PC), 1)
     to_angle = jnp.float32(2.0 * math.pi / PRIME)
     first = place_ref[0]
-    held_ref[...] = table_ref[...]
 
     def turned(steps, columns):
         scrambled = mod_prime((columns + first) * 40503)
@@ -206,10 +213,9 @@
     row = lax.broadcasted_iota(jnp.int32, (foot, PC), 0)
     ids = jnp.zeros((foot, PC), jnp.int32)
     for i in range(foot):
-        ids = jnp.where(row == i, list_ref[i] * NP, ids)
+        ids = jnp.where(row == i, note_ref[0, i] * NP, ids)
     outer = turned(ids, width(foot))
     cos_out, sin_out = jnp.cos(outer), jnp.sin(outer)
-    place_entries(blocks, paired, list_ref, place_ref[1], notes_ref, where_ref)
     for i in range(0, foot, 2):
         real, imag = [], []
         for j in (i, i + 1):
@@ -224,25 +230,26 @@
         out_ref[rows, PC:] = imag
         out_ref[below, :PC] = -imag
         out_ref[below, PC:] = real
-
-
-def steering(my_list, place, notes, blocks, paired):
-    foot = my_list.shape[0]
+    holding.wait()
+
+
+def steering(foot, note, first_column):
     smem = pl.BlockSpec(memory_space=pltpu.SMEM)
     vmem = pl.BlockSpec(memory_space=pltpu.VMEM)
     table = jnp.asarray(correlation_table())
     return pl.pallas_call(
-        functools.partial(steer_kernel, blocks, paired),
+        steer_kernel,
         out_shape=(
             jax.ShapeDtypeStruct((2 * foot * NP, 2 * PC), BF16),
-            jax.ShapeDtypeStruct((3, foot), jnp.int32),
             jax.ShapeDtypeStruct(table.shape, BF16),
         ),
-        in_specs=[smem] * 3 + [vmem],
-        out_specs=(vmem, smem, vmem),
+        in_specs=[smem, smem, pl.BlockSpec(memory_space=pltpu.HBM)],
+        out_specs=(vmem, vmem),
+        scratch_shapes=[pltpu.SemaphoreType.DMA],
         compiler_params=pltpu.CompilerParams(vmem_limit_bytes=SMALL_BYTES),
+        cost_estimate=pl.CostEstimate(flops=0, bytes_accessed=4 << 20, transcendentals=0),
         name="steer",
-    )(my_list, place, notes, table)
+    )(note, first_column, pltpu.with_memory_space_constraint(table, pltpu.HBM))
 
 
 def image_kernel(where_ref, direct_ref, sibling_ref, table_ref, steer_ref, interp_ref, out_ref, echo, wins, focused, pixels, sem):
@@ -336,7 +343,6 @@
     foot = footprint.shape[2]
     tile_pos = lax.axis_index("tile").astype(jnp.int32)
     row_pos = lax.axis_index("section").astype(jnp.int32)
-    my_list = footprint[0, 0]
 
     rim = passed_along(raw_echo[:, :, :RIM], "section", -1)
     note = jnp.concatenate([footprint[0], window_start], axis=1)
@@ -345,17 +351,16 @@
     twist = tile_pos if paired else jnp.int32(0)
 
     first_column = tile_pos * PC + 1 + 7 * row_pos
-    place = jnp.stack([first_column, twist])
-    steer, where, table = steering(my_list, place, notes, blocks, paired)
-
-    spans = cut_windows(
+    steer, table = steering(foot, note, first_column[None])
+    notes, steer, table = lax.optimization_barrier((notes, steer, table))
+
+    spans, where = cut_windows(
         foot,
         notes,
         jnp.stack([tile_pos, twist]),
         raw_echo.reshape(planes, blocks, NP, bins),
         rim.reshape(planes, blocks, NP, RIM),
         4 if paired else 1,
-        steer,
     )
     if paired:
         direct, sibling = exchange(spans)

time: 32.2 us -> 30 us (0.932)
  local copies, waits for them, and re-layouts: 2.79 us -> 1.15 us
  waiting for transfers between devices: 9.08 us -> 8.71 us
    unnamed x6 -> x2, local copies, waits for them, and re-layouts: 1.65 us -> 0.01 us
    pallas_call x1, Pallas kernels: 2.06 us -> 1.54 us  [steering(): pl.pallas_call(steer_kernel, out_shape=(jax.ShapeDtypeStruct((2 * foot *...]
    pallas_call x1, Pallas kernels: 2.44 us -> 2.9 us  [cut_windows(): pl.pallas_call(functools.partial(fetch_kernel, foot), out_shape=spans + (...]
    ppermute x8, waiting for transfers between devices: 9.07 us -> 8.71 us  [swapped(): return lax.ppermute(value, 'tile', [(i, i ^ turn) for i in range(tiles)])]
  transfers between devices with their start and end apart: 9 -> 9, of which waited for: 8 -> 7; matrix products, arithmetic and copies ran while one was open for 3% -> 3% of each run, Pallas kernels for 14% -> 15%
where the time goes in v4:
time: 30 us; the launch traced here: 29.7 us
  starting transfers between devices  9.75 us (32%)
  Pallas kernels  9.18 us (31%)
  waiting for transfers between devices  8.71 us (29%)
  local copies, waits for them, and re-layouts  1.15 us (4%)
  other arithmetic  0.87 us (3%)
    ppermute x8, waiting for transfers between devices, swapped(): return lax.ppermute(value, 'tile', [(i, i ^ turn) for i in range(tiles)])  8.71 us
    ppermute x8, starting transfers between devices, swapped(): return lax.ppermute(value, 'tile', [(i, i ^ turn) for i in range(tiles)])  8.46 us
    pallas_call x1, Pallas kernels, tile_image(): pl.pallas_call(kernel, out_shape=jax.ShapeDtypeStruct((PR, 2 * PC), BF16)...  3.77 us
    pallas_call x1, Pallas kernels, cut_windows(): pl.pallas_call(functools.partial(fetch_kernel, foot), out_shape=spans + (...  2.9 us
    pallas_call x1, Pallas kernels, steering(): pl.pallas_call(steer_kernel, out_shape=(jax.ShapeDtypeStruct((2 * foot *...  1.54 us
    ppermute x1, starting transfers between devices, passed_along(): return lax.ppermute(value, axis, pairs)  1.29 us
    slice x1, local copies, waits for them, and re-layouts, local(): rim = passed_along(raw_echo[:, :, :RIM], 'section', -1)  1.09 us
    pallas_call x1, Pallas kernels, cut_windows(): pl.pallas_call(functools.partial(extend_kernel, groups), out_shape=spans,...  0.97 us
  transfers between devices with their start and end apart: 9, of which 7 were waited for; matrix products, arithmetic and copies ran while one was open for 3% of the time, Pallas kernels for 15%

profile of v4, /device:TPU:0, one launch (start us, length us, event | category | flops | bytes accessed | tf_op | source)
XLA Modules:
  0.0 29.7 jit_solution(5932334603975427607)
XLA Ops:
  0.0 0.0 copy-start
  0.0 1.1 %slice.27 = bf16[2,256,384]{2,1,0:T(8,128)(2,1)S(1)} slice(bf16[2,256,2048]{2,1,0:T(8,128)(2,1)} %param.5), slice={[0:2], [0:256], [0:384]} | slice | bytes 786432 | tf_op jit(solution)/shard_map/slice | solution.py:347
  1.1 1.3 %collective-permute-start.4 = (bf16[2,256,384]{2,1,0:T(8,128)(2,1)S(1)}, bf16[2,256,384]{2,1,0:T(8,128)(2,1)S(1)}, u32[]{:S(2)}, u32[]{:S(2)}) collective-permute-start(bf16[2,256,384]{2,1,0:T(8,128)(2,1)S(1)} %slice.27), channel_id=1, source_target_pairs={{8,0},{16,8},{24,16},{9,1},{17,9},{25,17},{10,2},{18,10},{26,18},{... | collective-permute-start | bytes 1179656 | tf_op jit(solution)/shard_map/ppermute | solution.py:32
  2.4 0.7 %pad_add_fusion.1 = s32[1,40]{1,0:T(1,128)S(1)} fusion(s32[1,32]{1,0:T(1,128)} %param.7, s32[1,8]{1,0:T(1,128)} %bitcast.8), kind=kLoop, calls=%fused_computation.3 | loop fusion | flops 40 | bytes 320 | tf_op jit(solution)/shard_map/concatenate | solution.py:348
  3.2 0.5 %collective-permute-start = (s32[1,128]{1,0:T(1,128)S(1)}, s32[1,128]{1,0:T(1,128)S(1)}, u32[]{:S(2)}, u32[]{:S(2)}) collective-permute-start(s32[1,128]{1,0:T(1,128)S(1)} %pad.4.note_ref), channel_id=1, source_target_pairs={{0,1},{1,0},{2,3},{3,2},{4,5},{5,4},{6,7},{7,6},{8,9},{9,8},{10,11... | collective-permute-start | bytes 1544 | tf_op jit(solution)/shard_map/ppermute | solution.py:323
  3.6 0.8 %collective-permute-done = s32[1,128]{1,0:T(1,128)S(1)} collective-permute-done((s32[1,128]{1,0:T(1,128)S(1)}, s32[1,128]{1,0:T(1,128)S(1)}, u32[]{:S(2)}, u32[]{:S(2)}) %collective-permute-start) | collective-permute-done | bytes 544 | tf_op jit(solution)/shard_map/ppermute | solution.py:323
  4.4 3.7 %collective-permute-start.3 = (s32[2,128]{1,0:T(2,128)S(1)}, s32[2,128]{1,0:T(2,128)S(1)}, u32[]{:S(2)}, u32[]{:S(2)}) collective-permute-start(s32[2,128]{1,0:T(2,128)S(1)} %pad_add_fusion), channel_id=1, source_target_pairs={{0,6},{1,7},{2,4},{3,5},{4,2},{5,3},{6,0},{7,1},{8,14},{9,15},{10,... | collective-permute-start | bytes 3080 | tf_op jit(solution)/shard_map/ppermute | solution.py:323
  8.2 0.5 %collective-permute-start.2 = (s32[2,128]{1,0:T(2,128)S(1)}, s32[2,128]{1,0:T(2,128)S(1)}, u32[]{:S(2)}, u32[]{:S(2)}) collective-permute-start(s32[2,128]{1,0:T(2,128)S(1)} %pad_add_fusion), channel_id=1, source_target_pairs={{0,4},{1,5},{2,6},{3,7},{4,0},{5,1},{6,2},{7,3},{8,12},{9,13},{10,... | collective-permute-start | bytes 3080 | tf_op jit(solution)/shard_map/ppermute | solution.py:323
  8.7 0.1 collective-permute-start.1
  8.8 0.1 pad_add_fusion.2.place_ref
  8.9 1.5 %steer.1 = (bf16[128,2048]{1,0:T(8,128)(2,1)S(1)}, bf16[384,512]{1,0:T(8,128)(2,1)S(1)}) custom-call(s32[1,128]{1,0:T(1,128)S(1)} %pad.4.note_ref, s32[1]{0:T(128)} %bitcast.1.place_ref, bf16[384,512]{1,0:T(8,128)(2,1)} %constant.20.clone.table_ref), custom_call_target="tpu_custom_call" | custom-call | bytes 4194304 | tf_op jit(solution)/shard_map/steer/pallas_call | solution.py:240
  10.4 0.0 collective-permute-done.3
  10.5 1.3 %collective-permute-done.2 = s32[2,128]{1,0:T(2,128)S(1)} collective-permute-done((s32[2,128]{1,0:T(2,128)S(1)}, s32[2,128]{1,0:T(2,128)S(1)}, u32[]{:S(2)}, u32[]{:S(2)}) %collective-permute-start.2) | collective-permute-done | bytes 1056 | tf_op jit(solution)/shard_map/ppermute | solution.py:323
  11.8 0.5 %collective-permute-done.1 = s32[2,128]{1,0:T(2,128)S(1)} collective-permute-done((s32[2,128]{1,0:T(2,128)S(1)}, s32[2,128]{1,0:T(2,128)S(1)}, u32[]{:S(2)}, u32[]{:S(2)}) %collective-permute-start.1) | collective-permute-done | bytes 1056 | tf_op jit(solution)/shard_map/ppermute | solution.py:323
  12.3 2.9 %fetch.1 = (bf16[4,2,8,512]{3,2,1,0:T(8,128)(2,1)S(1)}, bf16[4,2,8,512]{3,2,1,0:T(8,128)(2,1)S(1)}, bf16[4,2,8,512]{3,2,1,0:T(8,128)(2,1)S(1)}, bf16[4,2,8,512]{...) custom-call(s32[8,128]{1,0:T(8,128)S(1)} %concatenate.18.notes_ref, s32[2]{0:T(128)S(1)} %pad_add_fusion.2.place_ref, ...), custom_call_target="tpu_custom_call" | custom-call | tf_op jit(solution)/shard_map/fetch/pallas_call | solution.py:166
  15.2 0.0 collective-permute-done.4
  15.2 1.0 %extend.1 = (bf16[4,2,8,512]{3,2,1,0:T(8,128)(2,1)S(1)}, bf16[4,2,8,512]{3,2,1,0:T(8,128)(2,1)S(1)}, bf16[4,2,8,512]{3,2,1,0:T(8,128)(2,1)S(1)}, bf16[4,2,8,512]{3,2,1,0:T(8,128)(2,1)S(1)}) custom-call(s32[2,16]{1,0:T(2,128)S(1)} %get-tuple-element.24.plan_ref, ...), custom_call_target="tpu_custom_call", output_to_operand_aliasing={{0}: (2, {}), {1}: (3, {}), {2}: (4, {}), {3}: (5, {})} | custom-call | tf_op jit(solution)/shard_map/extend/pallas_call | solution.py:179
  16.2 1.7 %collective-permute-start.5 = (bf16[4,2,8,512]{3,2,1,0:T(8,128)(2,1)S(1)}, bf16[4,2,8,512]{3,2,1,0:T(8,128)(2,1)S(1)}, u32[]{:S(2)}, u32[]{:S(2)}) collective-permute-start(bf16[4,2,8,512]{3,2,1,0:T(8,128)(2,1)S(1)} %get-tuple-element.30), channel_id=1, source_target_pairs={{0,2},{1,3},{2,0},{3,1},{4,6},{5,7},{6,4},{7,5},{8,10},{9,11},{10,... | collective-permute-start | bytes 196616 | tf_op jit(solution)/shard_map/ppermute | solution.py:323
  17.9 1.5 %collective-permute-start.6 = (bf16[4,2,8,512]{3,2,1,0:T(8,128)(2,1)S(1)}, bf16[4,2,8,512]{3,2,1,0:T(8,128)(2,1)S(1)}, u32[]{:S(2)}, u32[]{:S(2)}) collective-permute-start(bf16[4,2,8,512]{3,2,1,0:T(8,128)(2,1)S(1)} %get-tuple-element.31), channel_id=1, source_target_pairs={{0,4},{1,5},{2,6},{3,7},{4,0},{5,1},{6,2},{7,3},{8,12},{9,13},{10,... | collective-permute-start | bytes 196616 | tf_op jit(solution)/shard_map/ppermute | solution.py:323
  19.4 0.4 %collective-permute-start.7 = (bf16[4,2,8,512]{3,2,1,0:T(8,128)(2,1)S(1)}, bf16[4,2,8,512]{3,2,1,0:T(8,128)(2,1)S(1)}, u32[]{:S(2)}, u32[]{:S(2)}) collective-permute-start(bf16[4,2,8,512]{3,2,1,0:T(8,128)(2,1)S(1)} %get-tuple-element.32), channel_id=1, source_target_pairs={{0,6},{1,7},{2,4},{3,5},{4,2},{5,3},{6,0},{7,1},{8,14},{9,15},{10,... | collective-permute-start | bytes 196616 | tf_op jit(solution)/shard_map/ppermute | solution.py:323
  19.7 1.0 %collective-permute-done.5 = bf16[4,2,8,512]{3,2,1,0:T(8,128)(2,1)S(1)} collective-permute-done((bf16[4,2,8,512]{3,2,1,0:T(8,128)(2,1)S(1)}, bf16[4,2,8,512]{3,2,1,0:T(8,128)(2,1)S(1)}, u32[]{:S(2)}, u32[]{:S(2)}) %collective-permute-start.5) | collective-permute-done | bytes 65568 | tf_op jit(solution)/shard_map/ppermute | solution.py:323
  20.8 1.9 %collective-permute-done.6 = bf16[4,2,8,512]{3,2,1,0:T(8,128)(2,1)S(1)} collective-permute-done((bf16[4,2,8,512]{3,2,1,0:T(8,128)(2,1)S(1)}, bf16[4,2,8,512]{3,2,1,0:T(8,128)(2,1)S(1)}, u32[]{:S(2)}, u32[]{:S(2)}) %collective-permute-start.6) | collective-permute-done | bytes 65568 | tf_op jit(solution)/shard_map/ppermute | solution.py:323
  22.7 1.8 %collective-permute-done.7 = bf16[4,2,8,512]{3,2,1,0:T(8,128)(2,1)S(1)} collective-permute-done((bf16[4,2,8,512]{3,2,1,0:T(8,128)(2,1)S(1)}, bf16[4,2,8,512]{3,2,1,0:T(8,128)(2,1)S(1)}, u32[]{:S(2)}, u32[]{:S(2)}) %collective-permute-start.7) | collective-permute-done | bytes 65568 | tf_op jit(solution)/shard_map/ppermute | solution.py:323
  24.6 0.1 collective-permute-start.8
  24.7 1.3 %collective-permute-done.8.refs_0_ = bf16[8,2,8,512]{3,2,1,0:T(8,128)(2,1)S(1)} collective-permute-done((bf16[8,2,8,512]{3,2,1,0:T(8,128)(2,1)S(1)}, bf16[8,2,8,512]{3,2,1,0:T(8,128)(2,1)S(1)}, u32[]{:S(2)}, u32[]{:S(2)}) %collective-permute-start.8) | collective-permute-done | bytes 131104 | tf_op jit(solution)/shard_map/ppermute | solution.py:323
  26.0 0.0 copy-done
  26.0 3.8 %image.1 = bf16[1024,2048]{1,0:T(8,128)(2,1)} custom-call(s32[3,8]{1,0:T(4,128)S(1)} %get-tuple-element.23.where_ref, bf16[8,2,8,512]{3,2,1,0:T(8,128)(2,1)S(1)} %pad_maximum_fusion.direct_ref, bf16[8,2,8,512]{3,2,1,0:T(8,128)(2,1)S(1)} %collective-permute-done.8.refs_0_, bf16[384,512]{1,0:T(8,128)(2,1)S(1)} %get-tuple-element.33.refs_1_, ...), custom_call_target="tpu_custom_call" | custom-call | tf_op jit(solution)/shard_map/image/pallas_call | solution.py:304
  (9 shorter events, 0.1 us)
Async XLA Ops:
  0.0 26.0 %copy-start = (bf16[1024,256]{1,0:T(8,128)(2,1)S(1)}, bf16[1024,256]{1,0:T(8,128)(2,1)}, u32[]{:S(2)}) copy-start(bf16[1024,256]{1,0:T(8,128)(2,1)} %constant.21.clone.refs_3_) | copy-start | bytes 1572868
  1.1 14.1 %collective-permute-start.4 = (bf16[2,256,384]{2,1,0:T(8,128)(2,1)S(1)}, bf16[2,256,384]{2,1,0:T(8,128)(2,1)S(1)}, u32[]{:S(2)}, u32[]{:S(2)}) collective-permute-start(bf16[2,256,384]{2,1,0:T(8,128)(2,1)S(1)} %slice.27), channel_id=1, source_target_pairs={{8,0},{16,8},{24,16},{9,1},{17,9},{25,17},{10,2},{18,10},{26,18},{... | collective-permute-start | bytes 1179656 | tf_op jit(solution)/shard_map/ppermute | solution.py:32
  3.2 1.3 %collective-permute-start = (s32[1,128]{1,0:T(1,128)S(1)}, s32[1,128]{1,0:T(1,128)S(1)}, u32[]{:S(2)}, u32[]{:S(2)}) collective-permute-start(s32[1,128]{1,0:T(1,128)S(1)} %pad.4.note_ref), channel_id=1, source_target_pairs={{0,1},{1,0},{2,3},{3,2},{4,5},{5,4},{6,7},{7,6},{8,9},{9,8},{10,11... | collective-permute-start | bytes 1544 | tf_op jit(solution)/shard_map/ppermute | solution.py:323
  4.4 6.0 %collective-permute-start.3 = (s32[2,128]{1,0:T(2,128)S(1)}, s32[2,128]{1,0:T(2,128)S(1)}, u32[]{:S(2)}, u32[]{:S(2)}) collective-permute-start(s32[2,128]{1,0:T(2,128)S(1)} %pad_add_fusion), channel_id=1, source_target_pairs={{0,6},{1,7},{2,4},{3,5},{4,2},{5,3},{6,0},{7,1},{8,14},{9,15},{10,... | collective-permute-start | bytes 3080 | tf_op jit(solution)/shard_map/ppermute | solution.py:323
  8.2 3.6 %collective-permute-start.2 = (s32[2,128]{1,0:T(2,128)S(1)}, s32[2,128]{1,0:T(2,128)S(1)}, u32[]{:S(2)}, u32[]{:S(2)}) collective-permute-start(s32[2,128]{1,0:T(2,128)S(1)} %pad_add_fusion), channel_id=1, source_target_pairs={{0,4},{1,5},{2,6},{3,7},{4,0},{5,1},{6,2},{7,3},{8,12},{9,13},{10,... | collective-permute-start | bytes 3080 | tf_op jit(solution)/shard_map/ppermute | solution.py:323
  8.7 3.6 %collective-permute-start.1 = (s32[2,128]{1,0:T(2,128)S(1)}, s32[2,128]{1,0:T(2,128)S(1)}, u32[]{:S(2)}, u32[]{:S(2)}) collective-permute-start(s32[2,128]{1,0:T(2,128)S(1)} %pad_add_fusion), channel_id=1, source_target_pairs={{0,2},{1,3},{2,0},{3,1},{4,6},{5,7},{6,4},{7,5},{8,10},{9,11},{10,... | collective-permute-start | bytes 3080 | tf_op jit(solution)/shard_map/ppermute | solution.py:323
  16.2 4.6 %collective-permute-start.5 = (bf16[4,2,8,512]{3,2,1,0:T(8,128)(2,1)S(1)}, bf16[4,2,8,512]{3,2,1,0:T(8,128)(2,1)S(1)}, u32[]{:S(2)}, u32[]{:S(2)}) collective-permute-start(bf16[4,2,8,512]{3,2,1,0:T(8,128)(2,1)S(1)} %get-tuple-element.30), channel_id=1, source_target_pairs={{0,2},{1,3},{2,0},{3,1},{4,6},{5,7},{6,4},{7,5},{8,10},{9,11},{10,... | collective-permute-start | bytes 196616 | tf_op jit(solution)/shard_map/ppermute | solution.py:323
  17.9 4.8 %collective-permute-start.6 = (bf16[4,2,8,512]{3,2,1,0:T(8,128)(2,1)S(1)}, bf16[4,2,8,512]{3,2,1,0:T(8,128)(2,1)S(1)}, u32[]{:S(2)}, u32[]{:S(2)}) collective-permute-start(bf16[4,2,8,512]{3,2,1,0:T(8,128)(2,1)S(1)} %get-tuple-element.31), channel_id=1, source_target_pairs={{0,4},{1,5},{2,6},{3,7},{4,0},{5,1},{6,2},{7,3},{8,12},{9,13},{10,... | collective-permute-start | bytes 196616 | tf_op jit(solution)/shard_map/ppermute | solution.py:323
  19.4 5.2 %collective-permute-start.7 = (bf16[4,2,8,512]{3,2,1,0:T(8,128)(2,1)S(1)}, bf16[4,2,8,512]{3,2,1,0:T(8,128)(2,1)S(1)}, u32[]{:S(2)}, u32[]{:S(2)}) collective-permute-start(bf16[4,2,8,512]{3,2,1,0:T(8,128)(2,1)S(1)} %get-tuple-element.32), channel_id=1, source_target_pairs={{0,6},{1,7},{2,4},{3,5},{4,2},{5,3},{6,0},{7,1},{8,14},{9,15},{10,... | collective-permute-start | bytes 196616 | tf_op jit(solution)/shard_map/ppermute | solution.py:323
  24.6 1.4 %collective-permute-start.8 = (bf16[8,2,8,512]{3,2,1,0:T(8,128)(2,1)S(1)}, bf16[8,2,8,512]{3,2,1,0:T(8,128)(2,1)S(1)}, u32[]{:S(2)}, u32[]{:S(2)}) collective-permute-start(bf16[8,2,8,512]{3,2,1,0:T(8,128)(2,1)S(1)} %pad_maximum_fusion.1), channel_id=1, source_target_pairs={{0,1},{1,0},{2,3},{3,2},{4,5},{5,4},{6,7},{7,6},{8,9},{9,8},{10,11... | collective-permute-start | bytes 393224 | tf_op jit(solution)/shard_map/ppermute | solution.py:323

commit v5 on v4

v5 whole, which is shorter than its diff:
```python
import functools
import math

import jax
import jax.numpy as jnp
import ml_dtypes
import numpy as np
from jax import lax
from jax.experimental import pallas as pl
from jax.experimental.pallas import tpu as pltpu
from jax.sharding import PartitionSpec as P

KC = 128
WIN = 256
PR = 1024
PC = 1024
NP = 8
CAP = 2
LANES = 128
PRIME = 65521
RIM = WIN + KC
SPAN = RIM + LANES
ROWS = 256
BF16 = jnp.bfloat16


def vmem_grant(chunks, more=0):
    return (2 + chunks // 4 + more) << 20


def passed_along(value, axis, by):
    devices = lax.axis_size(axis)
    pairs = [(i, i + by) for i in range(devices) if 0 <= i + by < devices]
    return lax.ppermute(value, axis, pairs)


def correlation_table():
    lag = np.arange(RIM)[:, None] - np.arange(WIN)[None, :]
    inside = (lag >= 0) & (lag < KC)
    lag = np.where(inside, lag, 0)
    angle = (lag * lag % (2 * KC)).astype(np.float64) * (math.pi / KC)
    scale = 1.0 / math.sqrt(KC)
    real = np.where(inside, np.cos(angle) * scale, 0.0)
    imag = np.where(inside, np.sin(angle) * scale, 0.0)
    return np.concatenate([real, imag], axis=1).astype(np.float32).astype(ml_dtypes.bfloat16)


def interp_table():
    row = np.arange(PR, dtype=np.float64)[:, None]
    offset = np.arange(WIN, dtype=np.float64)[None, :] - ((row + 0.5) / (PR // WIN) - 0.5)
    taper = np.cos(offset * (math.pi / 8.0)) ** 2
    kernel = np.where(np.abs(offset) < 4.0, np.sinc(offset) * taper, 0.0)
    return kernel.astype(np.float32).astype(ml_dtypes.bfloat16)


def named_blocks(notes_ref, row, foot, holder, blocks):
    lowest, highest, count = jnp.int32(blocks - 1), jnp.int32(0), jnp.int32(0)
    for e in range(foot):
        block = notes_ref[row, e] - holder * blocks
        held = (block >= 0) & (block < blocks)
        lowest = jnp.where(held, jnp.minimum(lowest, block), lowest)
        highest = jnp.where(held, jnp.maximum(highest, block), highest)
        count = count + held.astype(jnp.int32)
    return lowest, highest, count


def fetch_kernel(foot, notes_ref, place_ref, raw_ref, out_ref, plan_ref, sem):
    blocks = raw_ref.shape[1]
    last = (raw_ref.shape[3] - SPAN) // LANES
    mine = place_ref[1]
    own_note = mine ^ place_ref[2]

    def one_tile(n, carry):
        for slot, block in enumerate(named_blocks(notes_ref, n, foot, mine, blocks)[:CAP]):
            chunk = n * CAP + slot
            start = notes_ref[own_note, foot + block]
            first = pl.multiple_of(jnp.minimum(start >> 7, last) * LANES, LANES)
            pltpu.make_async_copy(
                raw_ref.at[:, block, :, pl.ds(first, SPAN)], out_ref.at[chunk], sem
            ).start()
            plan_ref[0, chunk] = block
            plan_ref[1, chunk] = jnp.maximum((start >> 7) - last, 0)
            plan_ref[2, chunk] = lax.rem(SPAN - (start & (LANES - 1)), SPAN)
        return carry

    tiles = notes_ref.shape[0]
    lax.fori_loop(0, tiles, one_tile, 0, unroll=tiles <= 8)
    pltpu.make_async_copy(out_ref, out_ref, sem).wait()


def cut_kernel(plan_ref, spans_ref, rim_ref, table_ref, *refs):
    *out_refs, echo = refs
    chunks = spans_ref.shape[0]
    span_tiles = SPAN // LANES

    def one_chunk(chunk, carry):
        block, over, turn = (plan_ref[row, chunk] for row in range(3))
        pieces = []
        for step in range(span_tiles):
            own = pl.multiple_of(jnp.minimum(step + over, span_tiles - 1) * LANES, LANES)
            piece = spans_ref[chunk, :, :, pl.ds(own, LANES)].astype(jnp.float32)
            if step:
                beyond = pl.multiple_of(jnp.maximum(step + over - span_tiles, 0) * LANES, LANES)
                rim = rim_ref[:, block, :, pl.ds(beyond, LANES)].astype(jnp.float32)
                piece = jnp.where(step + over < span_tiles, piece, rim)
            pieces.append(piece)
        span = jnp.concatenate(pieces, axis=2).reshape(2 * NP, SPAN)
        rows = pl.ds(pl.multiple_of(chunk * 2 * NP, 2 * NP), 2 * NP)
        echo[rows, :] = pltpu.roll(span, turn, 1)[:, :RIM].astype(BF16)
        return carry

    lax.fori_loop(0, chunks, one_chunk, 0, unroll=chunks <= 16)
    sums = jnp.dot(echo[...], table_ref[...], preferred_element_type=jnp.float32)
    sums = sums.reshape(chunks, 2, NP, 2 * WIN)
    real = (sums[:, 0, :, :WIN] + sums[:, 1, :, WIN:]).astype(BF16)
    imag = (sums[:, 1, :, :WIN] - sums[:, 0, :, WIN:]).astype(BF16)
    each = chunks // len(out_refs)
    for group, out_ref in enumerate(out_refs):
        part = slice(group * each, (group + 1) * each)
        out_ref[:, 0] = real[part]
        out_ref[:, 1] = imag[part]


def cut_windows(foot, notes, place, raw, rim, table, groups):
    chunks = notes.shape[0] * CAP
    smem = pl.BlockSpec(memory_space=pltpu.SMEM)
    vmem = pl.BlockSpec(memory_space=pltpu.VMEM)
    params = pltpu.CompilerParams(vmem_limit_bytes=vmem_grant(chunks))
    spans, plan = pl.pallas_call(
        functools.partial(fetch_kernel, foot),
        out_shape=(
            jax.ShapeDtypeStruct((chunks, 2, NP, SPAN), BF16),
            jax.ShapeDtypeStruct((3, chunks), jnp.int32),
        ),
        in_specs=[smem, smem, pl.BlockSpec(memory_space=pltpu.HBM)],
        out_specs=(vmem, smem),
        scratch_shapes=[pltpu.SemaphoreType.DMA],
        compiler_params=params,
        name="fetch",
    )(notes, place, pltpu.with_memory_space_constraint(raw, pltpu.HBM))
    return pl.pallas_call(
        cut_kernel,
        out_shape=(jax.ShapeDtypeStruct((chunks // groups, 2, NP, WIN), BF16),) * groups,
        in_specs=[smem, vmem, vmem, vmem],
        out_specs=(vmem,) * groups,
        scratch_shapes=[pltpu.VMEM((chunks * 2 * NP, RIM), BF16)],
        compiler_params=params,
        name="cut",
    )(plan, spans, rim, table)


def mod_prime(value):
    for _ in range(2):
        value = (value >> 16) * 15 + (value & 65535)
    return jnp.where(value >= PRIME, value - PRIME, value)


def steer_kernel(foot, blocks, order, note_ref, place_ref, table_ref, out_ref, held_ref, sem):
    holding = pltpu.make_async_copy(table_ref, held_ref, sem)
    holding.start()
    chunks = len(order) * CAP
    to_angle = jnp.float32(2.0 * math.pi / PRIME)
    first, twist = place_ref[0], place_ref[2]

    def turned(steps, rows):
        columns = lax.broadcasted_iota(jnp.int32, (rows, PC), 1)
        scrambled = mod_prime((columns + first) * 40503)
        return mod_prime(steps * scrambled).astype(jnp.float32) * to_angle

    inner = turned(lax.broadcasted_iota(jnp.int32, (NP, PC), 0), NP)
    cos_in, sin_in = jnp.cos(inner), jnp.sin(inner)
    row = lax.broadcasted_iota(jnp.int32, (chunks, PC), 0)
    ids = jnp.zeros((chunks, PC), jnp.int32)
    used = jnp.zeros((chunks, PC), jnp.float32)
    for n, position in enumerate(order):
        holder = position ^ twist
        *found, count = named_blocks(note_ref, 0, foot, holder, blocks)
        for slot, block in enumerate(found):
            here = row == n * CAP + slot
            ids = jnp.where(here, (holder * blocks + block) * NP, ids)
            used = jnp.where(here & (count > slot), 1.0, used)
    outer = turned(ids, chunks)
    cos_out, sin_out = jnp.cos(outer) * used, jnp.sin(outer) * used
    for i in range(chunks):
        c, s = cos_out[i : i + 1], sin_out[i : i + 1]
        real = c * cos_in - s * sin_in
        imag = s * cos_in + c * sin_in
        rows = slice(i * 2 * NP, (i + 1) * 2 * NP)
        out_ref[rows, :PC] = jnp.concatenate([real, -imag], axis=0).astype(BF16)
        out_ref[rows, PC:] = jnp.concatenate([imag, real], axis=0).astype(BF16)
    holding.wait()


def steering(foot, blocks, order, note, place):
    smem = pl.BlockSpec(memory_space=pltpu.SMEM)
    vmem = pl.BlockSpec(memory_space=pltpu.VMEM)
    hbm = pl.BlockSpec(memory_space=pltpu.HBM)
    table = jnp.asarray(correlation_table())
    rows = len(order) * CAP * 2 * NP
    return pl.pallas_call(
        functools.partial(steer_kernel, foot, blocks, order),
        out_shape=(
            jax.ShapeDtypeStruct((rows, 2 * PC), BF16),
            jax.ShapeDtypeStruct(table.shape, BF16),
        ),
        in_specs=[smem, smem, hbm],
        out_specs=(vmem, vmem),
        scratch_shapes=[pltpu.SemaphoreType.DMA],
        compiler_params=pltpu.CompilerParams(vmem_limit_bytes=vmem_grant(len(order) * CAP)),
        cost_estimate=pl.CostEstimate(flops=0, bytes_accessed=4 << 20, transcendentals=0),
        name="steer",
    )(note, place, pltpu.with_memory_space_constraint(table, pltpu.HBM))


def image_kernel(scale, *refs):
    *window_refs, steer_ref, interp_ref, out_ref, focused, pixels, sem = refs
    windows = jnp.concatenate(
        [ref[...].reshape(ref.shape[0] * 2 * NP, WIN) for ref in window_refs], axis=0
    )
    contract = (((0,), (0,)), ((), ()))
    focused[...] = (
        lax.dot_general(windows, steer_ref[...], contract, preferred_element_type=jnp.float32)
        * jnp.float32(scale)
    ).astype(BF16)
    copies = []
    for step in range(PR // ROWS):
        rows = pl.ds(step * ROWS, ROWS)
        pixels[rows, :] = jnp.dot(
            interp_ref[rows, :], focused[...], preferred_element_type=jnp.float32
        ).astype(BF16)
        copy = pltpu.make_async_copy(pixels.at[rows], out_ref.at[rows], sem.at[step])
        copy.start()
        copies.append(copy)
    for copy in copies:
        copy.wait()


def tile_image(foot, windows, steer):
    vmem = pl.BlockSpec(memory_space=pltpu.VMEM)
    return pl.pallas_call(
        functools.partial(image_kernel, 1.0 / math.sqrt(foot * NP)),
        out_shape=jax.ShapeDtypeStruct((PR, 2 * PC), BF16),
        in_specs=[vmem] * (len(windows) + 2),
        out_specs=pl.BlockSpec(memory_space=pltpu.HBM),
        scratch_shapes=[
            pltpu.VMEM((WIN, 2 * PC), BF16),
            pltpu.VMEM((PR, 2 * PC), BF16),
            pltpu.SemaphoreType.DMA((PR // ROWS,)),
        ],
        compiler_params=pltpu.CompilerParams(vmem_limit_bytes=vmem_grant(steer.shape[0] // (2 * NP), 5)),
        name="image",
    )(*windows, steer, jnp.asarray(interp_table()))


def swapped(value, turn):
    tiles = lax.axis_size("tile")
    return lax.ppermute(value, "tile", [(i, i ^ turn) for i in range(tiles)])


def gather_notes(note):
    pair = jnp.concatenate([note, swapped(note, 1)], axis=0)
    return jnp.concatenate([pair] + [swapped(pair, 2 * c) for c in range(1, 4)], axis=0)


def exchange(windows):
    got = [windows[0]] + [swapped(windows[c], 2 * c) for c in range(1, 4)]
    theirs = jnp.concatenate([part[CAP:] for part in got], axis=0)
    ours = jnp.concatenate([part[:CAP] for part in got], axis=0)
    return ours, swapped(theirs, 1)


def local(raw_echo, footprint, window_start):
    planes, pulses, bins = raw_echo.shape
    blocks = pulses // NP
    tiles = lax.axis_size("tile")
    paired = tiles == 8
    foot = footprint.shape[2]
    tile_pos = lax.axis_index("tile").astype(jnp.int32)
    row_pos = lax.axis_index("section").astype(jnp.int32)

    rim = passed_along(raw_echo[:, :, :RIM], "section", -1)
    note = jnp.concatenate([footprint[0], window_start], axis=1)
    note = jnp.pad(note, ((0, 0), (0, -note.shape[1] % LANES)))
    notes = gather_notes(note) if paired else lax.all_gather(note, "tile", axis=0, tiled=True)
    twist = tile_pos if paired else jnp.int32(0)
    place = jnp.stack([tile_pos * PC + 1 + 7 * row_pos, tile_pos, twist])
    order = tuple(range(0, tiles, 2)) + tuple(range(1, tiles, 2)) if paired else tuple(range(tiles))

    raw = raw_echo.reshape(planes, blocks, NP, bins)
    steer, table = steering(foot, blocks, order, note, place)
    notes, steer, table = lax.optimization_barrier((notes, steer, table))
    windows = cut_windows(
        foot, notes, place, raw, rim.reshape(planes, blocks, NP, RIM), table, 4 if paired else 1
    )
    if paired:
        windows = exchange(windows)
    else:
        sent = windows[0].reshape((tiles, CAP, 2, NP, WIN))
        got = lax.all_to_all(sent, "tile", 0, 0, tiled=True)
        windows = (got.reshape(windows[0].shape),)
    return tile_image(foot, windows, steer)[None, None]


def solution(mesh):
    in_specs = (P(None, "tile", "section"), P("section", "tile", None), P("section", "tile"))
    out_specs = P("section", "tile", None, None)
    return jax.shard_map(local, mesh=mesh, in_specs=in_specs, out_specs=out_specs, check_vma=False)
```

time: 30 us -> 28.7 us (0.957)
  Pallas kernels: 9.18 us -> 7.87 us
    pallas_call x4, Pallas kernels: 9.18 us -> 7.87 us  [the longest x1 2.77 us: tile_image(): pl.pallas_call(functools.partial(image_kernel, 1.0 / math.sqrt(foot * NP)...]
    ppermute x1, waiting for transfers between devices: 0.01 us -> 0.46 us  [passed_along(): return lax.ppermute(value, axis, pairs)]
    ppermute x8, waiting for transfers between devices: 8.71 us -> 8.33 us  [swapped(): return lax.ppermute(value, 'tile', [(i, i ^ turn) for i in range(tiles)])]
  transfers between devices with their start and end apart: 9 -> 9, of which waited for: 7 -> 8; matrix products, arithmetic and copies ran while one was open for 3% -> 3% of each run, Pallas kernels for 15% -> 14%
where the time goes in v5:
time: 28.7 us; the launch traced here: 28.5 us
  starting transfers between devices  9.75 us (34%)
  waiting for transfers between devices  8.79 us (31%)
  Pallas kernels  7.87 us (27%)
  local copies, waits for them, and re-layouts  1.14 us (4%)
  other arithmetic  0.86 us (3%)
    ppermute x8, starting transfers between devices, swapped(): return lax.ppermute(value, 'tile', [(i, i ^ turn) for i in range(tiles)])  8.46 us
    ppermute x8, waiting for transfers between devices, swapped(): return lax.ppermute(value, 'tile', [(i, i ^ turn) for i in range(tiles)])  8.33 us
    pallas_call x1, Pallas kernels, tile_image(): pl.pallas_call(functools.partial(image_kernel, 1.0 / math.sqrt(foot * NP)...  2.77 us
    pallas_call x1, Pallas kernels, cut_windows(): pl.pallas_call(functools.partial(fetch_kernel, foot), out_shape=(jax.Shap...  2.39 us
    pallas_call x1, Pallas kernels, steering(): pl.pallas_call(functools.partial(steer_kernel, foot, blocks, order), out_...  1.55 us
    ppermute x1, starting transfers between devices, passed_along(): return lax.ppermute(value, axis, pairs)  1.29 us
    pallas_call x1, Pallas kernels, cut_windows(): pl.pallas_call(cut_kernel, out_shape=(jax.ShapeDtypeStruct((chunks // gro...  1.16 us
    slice x1, local copies, waits for them, and re-layouts, local(): rim = passed_along(raw_echo[:, :, :RIM], 'section', -1)  1.09 us
  transfers between devices with their start and end apart: 9, of which 8 were waited for; matrix products, arithmetic and copies ran while one was open for 3% of the time, Pallas kernels for 14%

profile of v5, /device:TPU:0, one launch (start us, length us, event | category | flops | bytes accessed | tf_op | source)
XLA Modules:
  0.0 28.5 jit_solution(6803868603260462212)
XLA Ops:
  0.0 0.0 copy-start
  0.0 1.1 %slice.27 = bf16[2,256,384]{2,1,0:T(8,128)(2,1)S(1)} slice(bf16[2,256,2048]{2,1,0:T(8,128)(2,1)} %param.5), slice={[0:2], [0:256], [0:384]} | slice | bytes 786432 | tf_op jit(solution)/shard_map/slice | solution.py:281
  1.1 1.3 %collective-permute-start.4 = (bf16[2,256,384]{2,1,0:T(8,128)(2,1)S(1)}, bf16[2,256,384]{2,1,0:T(8,128)(2,1)S(1)}, u32[]{:S(2)}, u32[]{:S(2)}) collective-permute-start(bf16[2,256,384]{2,1,0:T(8,128)(2,1)S(1)} %slice.27), channel_id=1, source_target_pairs={{8,0},{16,8},{24,16},{9,1},{17,9},{25,17},{10,2},{18,10},{26,18},{... | collective-permute-start | bytes 1179656 | tf_op jit(solution)/shard_map/ppermute | solution.py:34
  2.4 0.7 %pad_add_fusion.1 = s32[1,40]{1,0:T(1,128)S(1)} fusion(s32[1,32]{1,0:T(1,128)} %param.7, s32[1,8]{1,0:T(1,128)} %bitcast.8), kind=kLoop, calls=%fused_computation.3 | loop fusion | flops 40 | bytes 320 | tf_op jit(solution)/shard_map/concatenate | solution.py:282
  3.2 0.5 %collective-permute-start = (s32[1,128]{1,0:T(1,128)S(1)}, s32[1,128]{1,0:T(1,128)S(1)}, u32[]{:S(2)}, u32[]{:S(2)}) collective-permute-start(s32[1,128]{1,0:T(1,128)S(1)} %pad.4.note_ref), channel_id=1, source_target_pairs={{0,1},{1,0},{2,3},{3,2},{4,5},{5,4},{6,7},{7,6},{8,9},{9,8},{10,11... | collective-permute-start | bytes 1544 | tf_op jit(solution)/shard_map/ppermute | solution.py:257
  3.6 0.8 %collective-permute-done = s32[1,128]{1,0:T(1,128)S(1)} collective-permute-done((s32[1,128]{1,0:T(1,128)S(1)}, s32[1,128]{1,0:T(1,128)S(1)}, u32[]{:S(2)}, u32[]{:S(2)}) %collective-permute-start) | collective-permute-done | bytes 544 | tf_op jit(solution)/shard_map/ppermute | solution.py:257
  4.4 3.7 %collective-permute-start.3 = (s32[2,128]{1,0:T(2,128)S(1)}, s32[2,128]{1,0:T(2,128)S(1)}, u32[]{:S(2)}, u32[]{:S(2)}) collective-permute-start(s32[2,128]{1,0:T(2,128)S(1)} %pad_add_fusion), channel_id=1, source_target_pairs={{0,6},{1,7},{2,4},{3,5},{4,2},{5,3},{6,0},{7,1},{8,14},{9,15},{10,... | collective-permute-start | bytes 3080 | tf_op jit(solution)/shard_map/ppermute | solution.py:257
  8.2 0.5 %collective-permute-start.2 = (s32[2,128]{1,0:T(2,128)S(1)}, s32[2,128]{1,0:T(2,128)S(1)}, u32[]{:S(2)}, u32[]{:S(2)}) collective-permute-start(s32[2,128]{1,0:T(2,128)S(1)} %pad_add_fusion), channel_id=1, source_target_pairs={{0,4},{1,5},{2,6},{3,7},{4,0},{5,1},{6,2},{7,3},{8,12},{9,13},{10,... | collective-permute-start | bytes 3080 | tf_op jit(solution)/shard_map/ppermute | solution.py:257
  8.7 0.1 collective-permute-start.1
  8.8 0.1 pad_add_fusion.2.place_ref
  8.9 1.5 %steer.1 = (bf16[256,2048]{1,0:T(8,128)(2,1)S(1)}, bf16[384,512]{1,0:T(8,128)(2,1)S(1)}) custom-call(s32[1,128]{1,0:T(1,128)S(1)} %pad.4.note_ref, s32[3]{0:T(128)S(1)} %pad_add_fusion.2.place_ref, bf16[384,512]{1,0:T(8,128)(2,1)} %constant.20.clone.table_ref), custom_call_target="tpu_custom_call" | custom-call | bytes 4194304 | tf_op jit(solution)/shard_map/steer/pallas_call | solution.py:200
  10.4 0.0 collective-permute-done.3
  10.5 1.3 %collective-permute-done.2 = s32[2,128]{1,0:T(2,128)S(1)} collective-permute-done((s32[2,128]{1,0:T(2,128)S(1)}, s32[2,128]{1,0:T(2,128)S(1)}, u32[]{:S(2)}, u32[]{:S(2)}) %collective-permute-start.2) | collective-permute-done | bytes 1056 | tf_op jit(solution)/shard_map/ppermute | solution.py:257
  11.8 0.5 %collective-permute-done.1 = s32[2,128]{1,0:T(2,128)S(1)} collective-permute-done((s32[2,128]{1,0:T(2,128)S(1)}, s32[2,128]{1,0:T(2,128)S(1)}, u32[]{:S(2)}, u32[]{:S(2)}) %collective-permute-start.1) | collective-permute-done | bytes 1056 | tf_op jit(solution)/shard_map/ppermute | solution.py:257
  12.3 2.4 %fetch.1 = (bf16[16,2,8,512]{3,2,1,0:T(8,128)(2,1)S(1)}, s32[3,16]{1,0:T(4,128)S(1)}) custom-call(s32[8,128]{1,0:T(8,128)S(1)} %concatenate.18.notes_ref, s32[3]{0:T(128)S(1)} %pad_add_fusion.2.place_ref, bf16[2,32,8,2048]{3,2,1,0:T(8,128)(2,1)} %bitcast.7), custom_call_target="tpu_custom_call" | custom-call | tf_op jit(solution)/shard_map/fetch/pallas_call | solution.py:129
  14.7 0.5 %collective-permute-done.4 = bf16[2,256,384]{2,1,0:T(8,128)(2,1)S(1)} collective-permute-done((bf16[2,256,384]{2,1,0:T(8,128)(2,1)S(1)}, bf16[2,256,384]{2,1,0:T(8,128)(2,1)S(1)}, u32[]{:S(2)}, u32[]{:S(2)}) %collective-permute-start.4) | collective-permute-done | bytes 393248 | tf_op jit(solution)/shard_map/ppermute | solution.py:34
  15.1 1.2 %cut.1 = (bf16[4,2,8,256]{3,2,1,0:T(8,128)(2,1)S(1)}, bf16[4,2,8,256]{3,2,1,0:T(8,128)(2,1)S(1)}, bf16[4,2,8,256]{3,2,1,0:T(8,128)(2,1)S(1)}, bf16[4,2,8,256]{3,2,1,0:T(8,128)(2,1)S(1)}) custom-call(s32[3,16]{1,0:T(4,128)S(1)} %get-tuple-element.19.plan_ref, bf16[16,2,8,512]{3,2,1,0:T(8,128)(2,1)S(1)} %get-tuple-element.20.spans_ref, ...), custom_call_target="tpu_custom_call" | custom-call | tf_op jit(solution)/shard_map/cut/pallas_call | solution.py:141
  16.3 1.7 %collective-permute-start.5 = (bf16[4,2,8,256]{3,2,1,0:T(8,128)(2,1)S(1)}, bf16[4,2,8,256]{3,2,1,0:T(8,128)(2,1)S(1)}, u32[]{:S(2)}, u32[]{:S(2)}) collective-permute-start(bf16[4,2,8,256]{3,2,1,0:T(8,128)(2,1)S(1)} %get-tuple-element.23), channel_id=1, source_target_pairs={{0,2},{1,3},{2,0},{3,1},{4,6},{5,7},{6,4},{7,5},{8,10},{9,11},{10,... | collective-permute-start | bytes 98312 | tf_op jit(solution)/shard_map/ppermute | solution.py:257
  18.0 1.5 %collective-permute-start.6 = (bf16[4,2,8,256]{3,2,1,0:T(8,128)(2,1)S(1)}, bf16[4,2,8,256]{3,2,1,0:T(8,128)(2,1)S(1)}, u32[]{:S(2)}, u32[]{:S(2)}) collective-permute-start(bf16[4,2,8,256]{3,2,1,0:T(8,128)(2,1)S(1)} %get-tuple-element.24), channel_id=1, source_target_pairs={{0,4},{1,5},{2,6},{3,7},{4,0},{5,1},{6,2},{7,3},{8,12},{9,13},{10,... | collective-permute-start | bytes 98312 | tf_op jit(solution)/shard_map/ppermute | solution.py:257
  19.6 0.3 %collective-permute-start.7 = (bf16[4,2,8,256]{3,2,1,0:T(8,128)(2,1)S(1)}, bf16[4,2,8,256]{3,2,1,0:T(8,128)(2,1)S(1)}, u32[]{:S(2)}, u32[]{:S(2)}) collective-permute-start(bf16[4,2,8,256]{3,2,1,0:T(8,128)(2,1)S(1)} %get-tuple-element.25), channel_id=1, source_target_pairs={{0,6},{1,7},{2,4},{3,5},{4,2},{5,3},{6,0},{7,1},{8,14},{9,15},{10,... | collective-permute-start | bytes 98312 | tf_op jit(solution)/shard_map/ppermute | solution.py:257
  19.9 0.4 %collective-permute-done.5 = bf16[4,2,8,256]{3,2,1,0:T(8,128)(2,1)S(1)} collective-permute-done((bf16[4,2,8,256]{3,2,1,0:T(8,128)(2,1)S(1)}, bf16[4,2,8,256]{3,2,1,0:T(8,128)(2,1)S(1)}, u32[]{:S(2)}, u32[]{:S(2)}) %collective-permute-start.5) | collective-permute-done | bytes 32800 | tf_op jit(solution)/shard_map/ppermute | solution.py:257
  20.3 1.9 %collective-permute-done.6 = bf16[4,2,8,256]{3,2,1,0:T(8,128)(2,1)S(1)} collective-permute-done((bf16[4,2,8,256]{3,2,1,0:T(8,128)(2,1)S(1)}, bf16[4,2,8,256]{3,2,1,0:T(8,128)(2,1)S(1)}, u32[]{:S(2)}, u32[]{:S(2)}) %collective-permute-start.6) | collective-permute-done | bytes 32800 | tf_op jit(solution)/shard_map/ppermute | solution.py:257
  22.2 2.2 %collective-permute-done.7 = bf16[4,2,8,256]{3,2,1,0:T(8,128)(2,1)S(1)} collective-permute-done((bf16[4,2,8,256]{3,2,1,0:T(8,128)(2,1)S(1)}, bf16[4,2,8,256]{3,2,1,0:T(8,128)(2,1)S(1)}, u32[]{:S(2)}, u32[]{:S(2)}) %collective-permute-start.7) | collective-permute-done | bytes 32800 | tf_op jit(solution)/shard_map/ppermute | solution.py:257
  24.4 0.1 collective-permute-start.8
  24.5 1.2 %collective-permute-done.8.refs_1_ = bf16[8,2,8,256]{3,2,1,0:T(8,128)(2,1)S(1)} collective-permute-done((bf16[8,2,8,256]{3,2,1,0:T(8,128)(2,1)S(1)}, bf16[8,2,8,256]{3,2,1,0:T(8,128)(2,1)S(1)}, u32[]{:S(2)}, u32[]{:S(2)}) %collective-permute-start.8) | collective-permute-done | bytes 65568 | tf_op jit(solution)/shard_map/ppermute | solution.py:257
  25.7 0.0 copy-done
  25.7 2.8 %image.1 = bf16[1024,2048]{1,0:T(8,128)(2,1)} custom-call(bf16[8,2,8,256]{3,2,1,0:T(8,128)(2,1)S(1)} %pad_maximum_fusion.refs_0_, bf16[8,2,8,256]{3,2,1,0:T(8,128)(2,1)S(1)} %collective-permute-done.8.refs_1_, bf16[256,2048]{1,0:T(8,128)(2,1)S(1)} %get-tuple-element.26.refs_2_, bf16[1024,256]{1,0:T(8,128)(2,1)S(1)} %copy-done), custom_call_target="tpu_custom_call" | custom-call | tf_op jit(solution)/shard_map/image/pallas_call | solution.py:240
  (9 shorter events, 0.1 us)
Async XLA Ops:
  0.0 25.7 %copy-start = (bf16[1024,256]{1,0:T(8,128)(2,1)S(1)}, bf16[1024,256]{1,0:T(8,128)(2,1)}, u32[]{:S(2)}) copy-start(bf16[1024,256]{1,0:T(8,128)(2,1)} %constant.21.clone.refs_3_) | copy-start | bytes 1572868
  1.1 14.0 %collective-permute-start.4 = (bf16[2,256,384]{2,1,0:T(8,128)(2,1)S(1)}, bf16[2,256,384]{2,1,0:T(8,128)(2,1)S(1)}, u32[]{:S(2)}, u32[]{:S(2)}) collective-permute-start(bf16[2,256,384]{2,1,0:T(8,128)(2,1)S(1)} %slice.27), channel_id=1, source_target_pairs={{8,0},{16,8},{24,16},{9,1},{17,9},{25,17},{10,2},{18,10},{26,18},{... | collective-permute-start | bytes 1179656 | tf_op jit(solution)/shard_map/ppermute | solution.py:34
  3.2 1.3 %collective-permute-start = (s32[1,128]{1,0:T(1,128)S(1)}, s32[1,128]{1,0:T(1,128)S(1)}, u32[]{:S(2)}, u32[]{:S(2)}) collective-permute-start(s32[1,128]{1,0:T(1,128)S(1)} %pad.4.note_ref), channel_id=1, source_target_pairs={{0,1},{1,0},{2,3},{3,2},{4,5},{5,4},{6,7},{7,6},{8,9},{9,8},{10,11... | collective-permute-start | bytes 1544 | tf_op jit(solution)/shard_map/ppermute | solution.py:257
  4.4 6.0 %collective-permute-start.3 = (s32[2,128]{1,0:T(2,128)S(1)}, s32[2,128]{1,0:T(2,128)S(1)}, u32[]{:S(2)}, u32[]{:S(2)}) collective-permute-start(s32[2,128]{1,0:T(2,128)S(1)} %pad_add_fusion), channel_id=1, source_target_pairs={{0,6},{1,7},{2,4},{3,5},{4,2},{5,3},{6,0},{7,1},{8,14},{9,15},{10,... | collective-permute-start | bytes 3080 | tf_op jit(solution)/shard_map/ppermute | solution.py:257
  8.2 3.6 %collective-permute-start.2 = (s32[2,128]{1,0:T(2,128)S(1)}, s32[2,128]{1,0:T(2,128)S(1)}, u32[]{:S(2)}, u32[]{:S(2)}) collective-permute-start(s32[2,128]{1,0:T(2,128)S(1)} %pad_add_fusion), channel_id=1, source_target_pairs={{0,4},{1,5},{2,6},{3,7},{4,0},{5,1},{6,2},{7,3},{8,12},{9,13},{10,... | collective-permute-start | bytes 3080 | tf_op jit(solution)/shard_map/ppermute | solution.py:257
  8.7 3.6 %collective-permute-start.1 = (s32[2,128]{1,0:T(2,128)S(1)}, s32[2,128]{1,0:T(2,128)S(1)}, u32[]{:S(2)}, u32[]{:S(2)}) collective-permute-start(s32[2,128]{1,0:T(2,128)S(1)} %pad_add_fusion), channel_id=1, source_target_pairs={{0,2},{1,3},{2,0},{3,1},{4,6},{5,7},{6,4},{7,5},{8,10},{9,11},{10,... | collective-permute-start | bytes 3080 | tf_op jit(solution)/shard_map/ppermute | solution.py:257
  16.3 4.0 %collective-permute-start.5 = (bf16[4,2,8,256]{3,2,1,0:T(8,128)(2,1)S(1)}, bf16[4,2,8,256]{3,2,1,0:T(8,128)(2,1)S(1)}, u32[]{:S(2)}, u32[]{:S(2)}) collective-permute-start(bf16[4,2,8,256]{3,2,1,0:T(8,128)(2,1)S(1)} %get-tuple-element.23), channel_id=1, source_target_pairs={{0,2},{1,3},{2,0},{3,1},{4,6},{5,7},{6,4},{7,5},{8,10},{9,11},{10,... | collective-permute-start | bytes 98312 | tf_op jit(solution)/shard_map/ppermute | solution.py:257
  18.0 4.1 %collective-permute-start.6 = (bf16[4,2,8,256]{3,2,1,0:T(8,128)(2,1)S(1)}, bf16[4,2,8,256]{3,2,1,0:T(8,128)(2,1)S(1)}, u32[]{:S(2)}, u32[]{:S(2)}) collective-permute-start(bf16[4,2,8,256]{3,2,1,0:T(8,128)(2,1)S(1)} %get-tuple-element.24), channel_id=1, source_target_pairs={{0,4},{1,5},{2,6},{3,7},{4,0},{5,1},{6,2},{7,3},{8,12},{9,13},{10,... | collective-permute-start | bytes 98312 | tf_op jit(solution)/shard_map/ppermute | solution.py:257
  19.6 4.8 %collective-permute-start.7 = (bf16[4,2,8,256]{3,2,1,0:T(8,128)(2,1)S(1)}, bf16[4,2,8,256]{3,2,1,0:T(8,128)(2,1)S(1)}, u32[]{:S(2)}, u32[]{:S(2)}) collective-permute-start(bf16[4,2,8,256]{3,2,1,0:T(8,128)(2,1)S(1)} %get-tuple-element.25), channel_id=1, source_target_pairs={{0,6},{1,7},{2,4},{3,5},{4,2},{5,3},{6,0},{7,1},{8,14},{9,15},{10,... | collective-permute-start | bytes 98312 | tf_op jit(solution)/shard_map/ppermute | solution.py:257
  24.4 1.3 %collective-permute-start.8 = (bf16[8,2,8,256]{3,2,1,0:T(8,128)(2,1)S(1)}, bf16[8,2,8,256]{3,2,1,0:T(8,128)(2,1)S(1)}, u32[]{:S(2)}, u32[]{:S(2)}) collective-permute-start(bf16[8,2,8,256]{3,2,1,0:T(8,128)(2,1)S(1)} %pad_maximum_fusion.1), channel_id=1, source_target_pairs={{0,1},{1,0},{2,3},{3,2},{4,5},{5,4},{6,7},{7,6},{8,9},{9,8},{10,11... | collective-permute-start | bytes 196616 | tf_op jit(solution)/shard_map/ppermute | solution.py:257

commit v6 on v5

--- a/solution.py
+++ b/solution.py
@@ -19,6 +19,7 @@
 LANES = 128
 PRIME = 65521
 RIM = WIN + KC
+TURNS = (2, 5, 7)
 SPAN = RIM + LANES
 ROWS = 256
 BF16 = jnp.bfloat16
@@ -64,14 +65,14 @@
     return lowest, highest, count
 
 
-def fetch_kernel(foot, notes_ref, place_ref, raw_ref, out_ref, plan_ref, sem):
+def fetch_kernel(foot, paired, notes_ref, place_ref, raw_ref, out_ref, plan_ref, sem):
     blocks = raw_ref.shape[1]
     last = (raw_ref.shape[3] - SPAN) // LANES
     mine = place_ref[1]
     own_note = mine ^ place_ref[2]
 
-    def one_tile(n, carry):
-        for slot, block in enumerate(named_blocks(notes_ref, n, foot, mine, blocks)[:CAP]):
+    def one_tile(n, row):
+        for slot, block in enumerate(named_blocks(notes_ref, row, foot, mine, blocks)[:CAP]):
             chunk = n * CAP + slot
             start = notes_ref[own_note, foot + block]
             first = pl.multiple_of(jnp.minimum(start >> 7, last) * LANES, LANES)
@@ -81,10 +82,13 @@
             plan_ref[0, chunk] = block
             plan_ref[1, chunk] = jnp.maximum((start >> 7) - last, 0)
             plan_ref[2, chunk] = lax.rem(SPAN - (start & (LANES - 1)), SPAN)
-        return carry
 
     tiles = notes_ref.shape[0]
-    lax.fori_loop(0, tiles, one_tile, 0, unroll=tiles <= 8)
+    if paired:
+        for n in range(tiles):
+            one_tile(n, row_of(n, paired))
+    else:
+        pl.loop(0, tiles)(lambda n: one_tile(n, n))
     pltpu.make_async_copy(out_ref, out_ref, sem).wait()
 
 
@@ -127,7 +131,7 @@
     vmem = pl.BlockSpec(memory_space=pltpu.VMEM)
     params = pltpu.CompilerParams(vmem_limit_bytes=vmem_grant(chunks))
     spans, plan = pl.pallas_call(
-        functools.partial(fetch_kernel, foot),
+        functools.partial(fetch_kernel, foot, groups > 1),
         out_shape=(
             jax.ShapeDtypeStruct((chunks, 2, NP, SPAN), BF16),
             jax.ShapeDtypeStruct((3, chunks), jnp.int32),
@@ -259,14 +263,24 @@
 
 def gather_notes(note):
     pair = jnp.concatenate([note, swapped(note, 1)], axis=0)
-    return jnp.concatenate([pair] + [swapped(pair, 2 * c) for c in range(1, 4)], axis=0)
+    return jnp.concatenate([pair] + [swapped(pair, turn) for turn in TURNS], axis=0)
+
+
+def row_of(position, paired):
+    turns = (0,) + TURNS
+    if not paired:
+        return position
+    return 2 * (position // 2) + (position ^ turns[position // 2]) % 2
 
 
 def exchange(windows):
-    got = [windows[0]] + [swapped(windows[c], 2 * c) for c in range(1, 4)]
-    theirs = jnp.concatenate([part[CAP:] for part in got], axis=0)
-    ours = jnp.concatenate([part[:CAP] for part in got], axis=0)
-    return ours, swapped(theirs, 1)
+    ours, theirs = [windows[0][:CAP]], [windows[0][CAP:]]
+    for window, turn in zip(windows[1:], TURNS):
+        got = swapped(window, turn)
+        halves = (got[:CAP], got[CAP:])
+        ours.append(halves[turn % 2])
+        theirs.append(halves[1 - turn % 2])
+    return jnp.concatenate(ours, axis=0), swapped(jnp.concatenate(theirs, axis=0), 1)
 
 
 def local(raw_echo, footprint, window_start):
@@ -284,7 +298,9 @@
     notes = gather_notes(note) if paired else lax.all_gather(note, "tile", axis=0, tiled=True)
     twist = tile_pos if paired else jnp.int32(0)
     place = jnp.stack([tile_pos * PC + 1 + 7 * row_pos, tile_pos, twist])
-    order = tuple(range(0, tiles, 2)) + tuple(range(1, tiles, 2)) if paired else tuple(range(tiles))
+    order = tuple(range(tiles))
+    if paired:
+        order = (0,) + TURNS + (1,) + tuple(turn ^ 1 for turn in TURNS)
 
     raw = raw_echo.reshape(planes, blocks, NP, bins)
     steer, table = steering(foot, blocks, order, note, place)

time: 28.7 us -> 27.9 us (0.972)
  waiting for transfers between devices: 8.79 us -> 6.83 us
  starting transfers between devices: 9.75 us -> 10.9 us
    ppermute x8, waiting for transfers between devices: 8.33 us -> 6.09 us  [swapped(): return lax.ppermute(value, 'tile', [(i, i ^ turn) for i in range(tiles)])]
    ppermute x8, starting transfers between devices: 8.46 us -> 9.61 us  [swapped(): return lax.ppermute(value, 'tile', [(i, i ^ turn) for i in range(tiles)])]
where the time goes in v6:
time: 27.9 us; the launch traced here: 27.7 us
  starting transfers between devices  10.9 us (39%)
  Pallas kernels  7.88 us (28%)
  waiting for transfers between devices  6.83 us (24%)
  local copies, waits for them, and re-layouts  1.14 us (4%)
  other arithmetic  0.85 us (3%)
    ppermute x8, starting transfers between devices, swapped(): return lax.ppermute(value, 'tile', [(i, i ^ turn) for i in range(tiles)])  9.61 us
    ppermute x8, waiting for transfers between devices, swapped(): return lax.ppermute(value, 'tile', [(i, i ^ turn) for i in range(tiles)])  6.09 us
    pallas_call x1, Pallas kernels, tile_image(): pl.pallas_call(functools.partial(image_kernel, 1.0 / math.sqrt(foot * NP)...  2.77 us
    pallas_call x1, Pallas kernels, cut_windows(): pl.pallas_call(functools.partial(fetch_kernel, foot, groups > 1), out_sha...  2.4 us
    pallas_call x1, Pallas kernels, steering(): pl.pallas_call(functools.partial(steer_kernel, foot, blocks, order), out_...  1.55 us
    ppermute x1, starting transfers between devices, passed_along(): return lax.ppermute(value, axis, pairs)  1.29 us
    pallas_call x1, Pallas kernels, cut_windows(): pl.pallas_call(cut_kernel, out_shape=(jax.ShapeDtypeStruct((chunks // gro...  1.16 us
    slice x1, local copies, waits for them, and re-layouts, local(): rim = passed_along(raw_echo[:, :, :RIM], 'section', -1)  1.09 us
  transfers between devices with their start and end apart: 9, of which 8 were waited for; matrix products, arithmetic and copies ran while one was open for 3% of the time, Pallas kernels for 14%

profile of v6, /device:TPU:0, one launch (start us, length us, event | category | flops | bytes accessed | tf_op | source)
XLA Modules:
  0.0 27.7 jit_solution(16194951647705202961)
XLA Ops:
  0.0 0.0 copy-start
  0.0 1.1 %slice.27 = bf16[2,256,384]{2,1,0:T(8,128)(2,1)S(1)} slice(bf16[2,256,2048]{2,1,0:T(8,128)(2,1)} %param.5), slice={[0:2], [0:256], [0:384]} | slice | bytes 786432 | tf_op jit(solution)/shard_map/slice | solution.py:295
  1.1 1.3 %collective-permute-start.4 = (bf16[2,256,384]{2,1,0:T(8,128)(2,1)S(1)}, bf16[2,256,384]{2,1,0:T(8,128)(2,1)S(1)}, u32[]{:S(2)}, u32[]{:S(2)}) collective-permute-start(bf16[2,256,384]{2,1,0:T(8,128)(2,1)S(1)} %slice.27), channel_id=1, source_target_pairs={{8,0},{16,8},{24,16},{9,1},{17,9},{25,17},{10,2},{18,10},{26,18},{... | collective-permute-start | bytes 1179656 | tf_op jit(solution)/shard_map/ppermute | solution.py:35
  2.4 0.7 %pad_add_fusion.1 = s32[1,40]{1,0:T(1,128)S(1)} fusion(s32[1,32]{1,0:T(1,128)} %param.7, s32[1,8]{1,0:T(1,128)} %bitcast.8), kind=kLoop, calls=%fused_computation.3 | loop fusion | flops 40 | bytes 320 | tf_op jit(solution)/shard_map/concatenate | solution.py:296
  3.2 0.5 %collective-permute-start = (s32[1,128]{1,0:T(1,128)S(1)}, s32[1,128]{1,0:T(1,128)S(1)}, u32[]{:S(2)}, u32[]{:S(2)}) collective-permute-start(s32[1,128]{1,0:T(1,128)S(1)} %pad.4.note_ref), channel_id=1, source_target_pairs={{0,1},{1,0},{2,3},{3,2},{4,5},{5,4},{6,7},{7,6},{8,9},{9,8},{10,11... | collective-permute-start | bytes 1544 | tf_op jit(solution)/shard_map/ppermute | solution.py:261
  3.6 0.8 %collective-permute-done = s32[1,128]{1,0:T(1,128)S(1)} collective-permute-done((s32[1,128]{1,0:T(1,128)S(1)}, s32[1,128]{1,0:T(1,128)S(1)}, u32[]{:S(2)}, u32[]{:S(2)}) %collective-permute-start) | collective-permute-done | bytes 544 | tf_op jit(solution)/shard_map/ppermute | solution.py:261
  4.4 3.6 %collective-permute-start.3 = (s32[2,128]{1,0:T(2,128)S(1)}, s32[2,128]{1,0:T(2,128)S(1)}, u32[]{:S(2)}, u32[]{:S(2)}) collective-permute-start(s32[2,128]{1,0:T(2,128)S(1)} %pad_add_fusion), channel_id=1, source_target_pairs={{0,7},{1,6},{2,5},{3,4},{4,3},{5,2},{6,1},{7,0},{8,15},{9,14},{10,... | collective-permute-start | bytes 3080 | tf_op jit(solution)/shard_map/ppermute | solution.py:261
  8.0 0.4 %collective-permute-start.2 = (s32[2,128]{1,0:T(2,128)S(1)}, s32[2,128]{1,0:T(2,128)S(1)}, u32[]{:S(2)}, u32[]{:S(2)}) collective-permute-start(s32[2,128]{1,0:T(2,128)S(1)} %pad_add_fusion), channel_id=1, source_target_pairs={{0,5},{1,4},{2,7},{3,6},{4,1},{5,0},{6,3},{7,2},{8,13},{9,12},{10,... | collective-permute-start | bytes 3080 | tf_op jit(solution)/shard_map/ppermute | solution.py:261
  8.4 0.2 collective-permute-start.1
  8.6 0.1 pad_add_fusion.2.place_ref
  8.7 1.5 %steer.1 = (bf16[256,2048]{1,0:T(8,128)(2,1)S(1)}, bf16[384,512]{1,0:T(8,128)(2,1)S(1)}) custom-call(s32[1,128]{1,0:T(1,128)S(1)} %pad.4.note_ref, s32[3]{0:T(128)S(1)} %pad_add_fusion.2.place_ref, bf16[384,512]{1,0:T(8,128)(2,1)} %constant.20.clone.table_ref), custom_call_target="tpu_custom_call" | custom-call | bytes 4194304 | tf_op jit(solution)/shard_map/steer/pallas_call | solution.py:204
  10.3 0.0 collective-permute-done.3
  10.3 0.7 %collective-permute-done.2 = s32[2,128]{1,0:T(2,128)S(1)} collective-permute-done((s32[2,128]{1,0:T(2,128)S(1)}, s32[2,128]{1,0:T(2,128)S(1)}, u32[]{:S(2)}, u32[]{:S(2)}) %collective-permute-start.2) | collective-permute-done | bytes 1056 | tf_op jit(solution)/shard_map/ppermute | solution.py:261
  11.0 1.0 %collective-permute-done.1 = s32[2,128]{1,0:T(2,128)S(1)} collective-permute-done((s32[2,128]{1,0:T(2,128)S(1)}, s32[2,128]{1,0:T(2,128)S(1)}, u32[]{:S(2)}, u32[]{:S(2)}) %collective-permute-start.1) | collective-permute-done | bytes 1056 | tf_op jit(solution)/shard_map/ppermute | solution.py:261
  12.0 2.4 %fetch.1 = (bf16[16,2,8,512]{3,2,1,0:T(8,128)(2,1)S(1)}, s32[3,16]{1,0:T(4,128)S(1)}) custom-call(s32[8,128]{1,0:T(8,128)S(1)} %concatenate.18.notes_ref, s32[3]{0:T(128)S(1)} %pad_add_fusion.2.place_ref, bf16[2,32,8,2048]{3,2,1,0:T(8,128)(2,1)} %bitcast.7), custom_call_target="tpu_custom_call" | custom-call | tf_op jit(solution)/shard_map/fetch/pallas_call | solution.py:133
  14.4 0.7 %collective-permute-done.4 = bf16[2,256,384]{2,1,0:T(8,128)(2,1)S(1)} collective-permute-done((bf16[2,256,384]{2,1,0:T(8,128)(2,1)S(1)}, bf16[2,256,384]{2,1,0:T(8,128)(2,1)S(1)}, u32[]{:S(2)}, u32[]{:S(2)}) %collective-permute-start.4) | collective-permute-done | bytes 393248 | tf_op jit(solution)/shard_map/ppermute | solution.py:35
  15.1 1.2 %cut.1 = (bf16[4,2,8,256]{3,2,1,0:T(8,128)(2,1)S(1)}, bf16[4,2,8,256]{3,2,1,0:T(8,128)(2,1)S(1)}, bf16[4,2,8,256]{3,2,1,0:T(8,128)(2,1)S(1)}, bf16[4,2,8,256]{3,2,1,0:T(8,128)(2,1)S(1)}) custom-call(s32[3,16]{1,0:T(4,128)S(1)} %get-tuple-element.19.plan_ref, bf16[16,2,8,512]{3,2,1,0:T(8,128)(2,1)S(1)} %get-tuple-element.20.spans_ref, ...), custom_call_target="tpu_custom_call" | custom-call | tf_op jit(solution)/shard_map/cut/pallas_call | solution.py:145
  16.3 1.7 %collective-permute-start.5 = (bf16[4,2,8,256]{3,2,1,0:T(8,128)(2,1)S(1)}, bf16[4,2,8,256]{3,2,1,0:T(8,128)(2,1)S(1)}, u32[]{:S(2)}, u32[]{:S(2)}) collective-permute-start(bf16[4,2,8,256]{3,2,1,0:T(8,128)(2,1)S(1)} %get-tuple-element.23), channel_id=1, source_target_pairs={{0,2},{1,3},{2,0},{3,1},{4,6},{5,7},{6,4},{7,5},{8,10},{9,11},{10,... | collective-permute-start | bytes 98312 | tf_op jit(solution)/shard_map/ppermute | solution.py:261
  18.0 0.0 collective-permute-start.6
  18.0 1.6 %collective-permute-start.7 = (bf16[4,2,8,256]{3,2,1,0:T(8,128)(2,1)S(1)}, bf16[4,2,8,256]{3,2,1,0:T(8,128)(2,1)S(1)}, u32[]{:S(2)}, u32[]{:S(2)}) collective-permute-start(bf16[4,2,8,256]{3,2,1,0:T(8,128)(2,1)S(1)} %get-tuple-element.25), channel_id=1, source_target_pairs={{0,7},{1,6},{2,5},{3,4},{4,3},{5,2},{6,1},{7,0},{8,15},{9,14},{10,... | collective-permute-start | bytes 98312 | tf_op jit(solution)/shard_map/ppermute | solution.py:261
  19.6 0.7 %collective-permute-done.5 = bf16[4,2,8,256]{3,2,1,0:T(8,128)(2,1)S(1)} collective-permute-done((bf16[4,2,8,256]{3,2,1,0:T(8,128)(2,1)S(1)}, bf16[4,2,8,256]{3,2,1,0:T(8,128)(2,1)S(1)}, u32[]{:S(2)}, u32[]{:S(2)}) %collective-permute-start.5) | collective-permute-done | bytes 32800 | tf_op jit(solution)/shard_map/ppermute | solution.py:261
  20.3 1.4 %collective-permute-done.6 = bf16[4,2,8,256]{3,2,1,0:T(8,128)(2,1)S(1)} collective-permute-done((bf16[4,2,8,256]{3,2,1,0:T(8,128)(2,1)S(1)}, bf16[4,2,8,256]{3,2,1,0:T(8,128)(2,1)S(1)}, u32[]{:S(2)}, u32[]{:S(2)}) %collective-permute-start.6) | collective-permute-done | bytes 32800 | tf_op jit(solution)/shard_map/ppermute | solution.py:261
  21.7 0.6 %collective-permute-done.7 = bf16[4,2,8,256]{3,2,1,0:T(8,128)(2,1)S(1)} collective-permute-done((bf16[4,2,8,256]{3,2,1,0:T(8,128)(2,1)S(1)}, bf16[4,2,8,256]{3,2,1,0:T(8,128)(2,1)S(1)}, u32[]{:S(2)}, u32[]{:S(2)}) %collective-permute-start.7) | collective-permute-done | bytes 32800 | tf_op jit(solution)/shard_map/ppermute | solution.py:261
  22.3 1.7 %collective-permute-start.8 = (bf16[8,2,8,256]{3,2,1,0:T(8,128)(2,1)S(1)}, bf16[8,2,8,256]{3,2,1,0:T(8,128)(2,1)S(1)}, u32[]{:S(2)}, u32[]{:S(2)}) collective-permute-start(bf16[8,2,8,256]{3,2,1,0:T(8,128)(2,1)S(1)} %pad_maximum_fusion.1), channel_id=1, source_target_pairs={{0,1},{1,0},{2,3},{3,2},{4,5},{5,4},{6,7},{7,6},{8,9},{9,8},{10,11... | collective-permute-start | bytes 196616 | tf_op jit(solution)/shard_map/ppermute | solution.py:261
  24.0 0.9 %collective-permute-done.8.refs_1_ = bf16[8,2,8,256]{3,2,1,0:T(8,128)(2,1)S(1)} collective-permute-done((bf16[8,2,8,256]{3,2,1,0:T(8,128)(2,1)S(1)}, bf16[8,2,8,256]{3,2,1,0:T(8,128)(2,1)S(1)}, u32[]{:S(2)}, u32[]{:S(2)}) %collective-permute-start.8) | collective-permute-done | bytes 65568 | tf_op jit(solution)/shard_map/ppermute | solution.py:261
  24.9 0.0 copy-done
  24.9 2.8 %image.1 = bf16[1024,2048]{1,0:T(8,128)(2,1)} custom-call(bf16[8,2,8,256]{3,2,1,0:T(8,128)(2,1)S(1)} %pad_maximum_fusion.refs_0_, bf16[8,2,8,256]{3,2,1,0:T(8,128)(2,1)S(1)} %collective-permute-done.8.refs_1_, bf16[256,2048]{1,0:T(8,128)(2,1)S(1)} %get-tuple-element.26.refs_2_, bf16[1024,256]{1,0:T(8,128)(2,1)S(1)} %copy-done), custom_call_target="tpu_custom_call" | custom-call | tf_op jit(solution)/shard_map/image/pallas_call | solution.py:244
  (9 shorter events, 0.1 us)
Async XLA Ops:
  0.0 24.9 %copy-start = (bf16[1024,256]{1,0:T(8,128)(2,1)S(1)}, bf16[1024,256]{1,0:T(8,128)(2,1)}, u32[]{:S(2)}) copy-start(bf16[1024,256]{1,0:T(8,128)(2,1)} %constant.21.clone.refs_3_) | copy-start | bytes 1572868
  1.1 14.0 %collective-permute-start.4 = (bf16[2,256,384]{2,1,0:T(8,128)(2,1)S(1)}, bf16[2,256,384]{2,1,0:T(8,128)(2,1)S(1)}, u32[]{:S(2)}, u32[]{:S(2)}) collective-permute-start(bf16[2,256,384]{2,1,0:T(8,128)(2,1)S(1)} %slice.27), channel_id=1, source_target_pairs={{8,0},{16,8},{24,16},{9,1},{17,9},{25,17},{10,2},{18,10},{26,18},{... | collective-permute-start | bytes 1179656 | tf_op jit(solution)/shard_map/ppermute | solution.py:35
  3.2 1.3 %collective-permute-start = (s32[1,128]{1,0:T(1,128)S(1)}, s32[1,128]{1,0:T(1,128)S(1)}, u32[]{:S(2)}, u32[]{:S(2)}) collective-permute-start(s32[1,128]{1,0:T(1,128)S(1)} %pad.4.note_ref), channel_id=1, source_target_pairs={{0,1},{1,0},{2,3},{3,2},{4,5},{5,4},{6,7},{7,6},{8,9},{9,8},{10,11... | collective-permute-start | bytes 1544 | tf_op jit(solution)/shard_map/ppermute | solution.py:261
  4.4 5.8 %collective-permute-start.3 = (s32[2,128]{1,0:T(2,128)S(1)}, s32[2,128]{1,0:T(2,128)S(1)}, u32[]{:S(2)}, u32[]{:S(2)}) collective-permute-start(s32[2,128]{1,0:T(2,128)S(1)} %pad_add_fusion), channel_id=1, source_target_pairs={{0,7},{1,6},{2,5},{3,4},{4,3},{5,2},{6,1},{7,0},{8,15},{9,14},{10,... | collective-permute-start | bytes 3080 | tf_op jit(solution)/shard_map/ppermute | solution.py:261
  8.0 3.0 %collective-permute-start.2 = (s32[2,128]{1,0:T(2,128)S(1)}, s32[2,128]{1,0:T(2,128)S(1)}, u32[]{:S(2)}, u32[]{:S(2)}) collective-permute-start(s32[2,128]{1,0:T(2,128)S(1)} %pad_add_fusion), channel_id=1, source_target_pairs={{0,5},{1,4},{2,7},{3,6},{4,1},{5,0},{6,3},{7,2},{8,13},{9,12},{10,... | collective-permute-start | bytes 3080 | tf_op jit(solution)/shard_map/ppermute | solution.py:261
  8.4 3.6 %collective-permute-start.1 = (s32[2,128]{1,0:T(2,128)S(1)}, s32[2,128]{1,0:T(2,128)S(1)}, u32[]{:S(2)}, u32[]{:S(2)}) collective-permute-start(s32[2,128]{1,0:T(2,128)S(1)} %pad_add_fusion), channel_id=1, source_target_pairs={{0,2},{1,3},{2,0},{3,1},{4,6},{5,7},{6,4},{7,5},{8,10},{9,11},{10,... | collective-permute-start | bytes 3080 | tf_op jit(solution)/shard_map/ppermute | solution.py:261
  16.3 4.0 %collective-permute-start.5 = (bf16[4,2,8,256]{3,2,1,0:T(8,128)(2,1)S(1)}, bf16[4,2,8,256]{3,2,1,0:T(8,128)(2,1)S(1)}, u32[]{:S(2)}, u32[]{:S(2)}) collective-permute-start(bf16[4,2,8,256]{3,2,1,0:T(8,128)(2,1)S(1)} %get-tuple-element.23), channel_id=1, source_target_pairs={{0,2},{1,3},{2,0},{3,1},{4,6},{5,7},{6,4},{7,5},{8,10},{9,11},{10,... | collective-permute-start | bytes 98312 | tf_op jit(solution)/shard_map/ppermute | solution.py:261
  18.0 3.6 %collective-permute-start.6 = (bf16[4,2,8,256]{3,2,1,0:T(8,128)(2,1)S(1)}, bf16[4,2,8,256]{3,2,1,0:T(8,128)(2,1)S(1)}, u32[]{:S(2)}, u32[]{:S(2)}) collective-permute-start(bf16[4,2,8,256]{3,2,1,0:T(8,128)(2,1)S(1)} %get-tuple-element.24), channel_id=1, source_target_pairs={{0,5},{1,4},{2,7},{3,6},{4,1},{5,0},{6,3},{7,2},{8,13},{9,12},{10,... | collective-permute-start | bytes 98312 | tf_op jit(solution)/shard_map/ppermute | solution.py:261
  18.0 4.2 %collective-permute-start.7 = (bf16[4,2,8,256]{3,2,1,0:T(8,128)(2,1)S(1)}, bf16[4,2,8,256]{3,2,1,0:T(8,128)(2,1)S(1)}, u32[]{:S(2)}, u32[]{:S(2)}) collective-permute-start(bf16[4,2,8,256]{3,2,1,0:T(8,128)(2,1)S(1)} %get-tuple-element.25), channel_id=1, source_target_pairs={{0,7},{1,6},{2,5},{3,4},{4,3},{5,2},{6,1},{7,0},{8,15},{9,14},{10,... | collective-permute-start | bytes 98312 | tf_op jit(solution)/shard_map/ppermute | solution.py:261
  22.3 2.6 %collective-permute-start.8 = (bf16[8,2,8,256]{3,2,1,0:T(8,128)(2,1)S(1)}, bf16[8,2,8,256]{3,2,1,0:T(8,128)(2,1)S(1)}, u32[]{:S(2)}, u32[]{:S(2)}) collective-permute-start(bf16[8,2,8,256]{3,2,1,0:T(8,128)(2,1)S(1)} %pad_maximum_fusion.1), channel_id=1, source_target_pairs={{0,1},{1,0},{2,3},{3,2},{4,5},{5,4},{6,7},{7,6},{8,9},{9,8},{10,11... | collective-permute-start | bytes 196616 | tf_op jit(solution)/shard_map/ppermute | solution.py:261

commit v7 on v6

--- a/solution.py
+++ b/solution.py
@@ -65,40 +65,53 @@
     return lowest, highest, count
 
 
-def fetch_kernel(foot, paired, notes_ref, place_ref, raw_ref, out_ref, plan_ref, sem):
+def plan_of(foot, blocks, last, mine, note, notes):
+    lane = lax.broadcasted_iota(jnp.int32, notes.shape, 1)
+    block = notes - mine * blocks
+    held = (lane < foot) & (block >= 0) & (block < blocks)
+    block = block.astype(jnp.float32)
+    lowest = jnp.min(jnp.where(held, block, blocks - 1.0), axis=1, keepdims=True)
+    highest = jnp.max(jnp.where(held, block, 0.0), axis=1, keepdims=True)
+    starts = jnp.broadcast_to(note, notes.shape).astype(jnp.float32)
+    plan = jnp.zeros(notes.shape, jnp.int32)
+    for slot, block in enumerate((lowest, highest)):
+        block = block.astype(jnp.int32)
+        start = jnp.sum(jnp.where(lane == foot + block, starts, 0.0), axis=1, keepdims=True)
+        start = start.astype(jnp.int32)
+        tile = start >> 7
+        turn = (SPAN - (start & (LANES - 1))) & (SPAN - 1)
+        code = (block * 4 + jnp.maximum(tile - last, 0)) * 64 + jnp.minimum(tile, last)
+        plan = jnp.where(lane == slot, code * SPAN + turn, plan)
+    return plan
+
+
+def planned(code):
+    return code >> 17, (code >> 15) & 3, (code >> 9) & 63, code & (SPAN - 1)
+
+
+def chunk_places(tiles, paired):
+    return [(row_of(n, paired), slot) for n in range(tiles) for slot in range(CAP)]
+
+
+def fetch_kernel(foot, paired, place_ref, note_ref, notes_ref, raw_ref, out_ref, plan_ref, sem):
     blocks = raw_ref.shape[1]
     last = (raw_ref.shape[3] - SPAN) // LANES
-    mine = place_ref[1]
-    own_note = mine ^ place_ref[2]
-
-    def one_tile(n, row):
-        for slot, block in enumerate(named_blocks(notes_ref, row, foot, mine, blocks)[:CAP]):
-            chunk = n * CAP + slot
-            start = notes_ref[own_note, foot + block]
-            first = pl.multiple_of(jnp.minimum(start >> 7, last) * LANES, LANES)
-            pltpu.make_async_copy(
-                raw_ref.at[:, block, :, pl.ds(first, SPAN)], out_ref.at[chunk], sem
-            ).start()
-            plan_ref[0, chunk] = block
-            plan_ref[1, chunk] = jnp.maximum((start >> 7) - last, 0)
-            plan_ref[2, chunk] = lax.rem(SPAN - (start & (LANES - 1)), SPAN)
-
-    tiles = notes_ref.shape[0]
-    if paired:
-        for n in range(tiles):
-            one_tile(n, row_of(n, paired))
-    else:
-        pl.loop(0, tiles)(lambda n: one_tile(n, n))
+    plan = plan_of(foot, blocks, last, place_ref[0:1, 1:2], note_ref[...], notes_ref[...])
+    for chunk, (row, slot) in enumerate(chunk_places(notes_ref.shape[0], paired)):
+        block, _, first, _ = planned(plan[row, slot])
+        lanes = pl.ds(pl.multiple_of(first * LANES, LANES), SPAN)
+        pltpu.make_async_copy(raw_ref.at[:, block, :, lanes], out_ref.at[chunk], sem).start()
+    plan_ref[...] = plan
     pltpu.make_async_copy(out_ref, out_ref, sem).wait()
 
 
-def cut_kernel(plan_ref, spans_ref, rim_ref, table_ref, *refs):
+def cut_kernel(paired, plan_ref, spans_ref, rim_ref, table_ref, *refs):
     *out_refs, echo = refs
     chunks = spans_ref.shape[0]
     span_tiles = SPAN // LANES
-
-    def one_chunk(chunk, carry):
-        block, over, turn = (plan_ref[row, chunk] for row in range(3))
+    plan = plan_ref[...]
+    for chunk, (row, slot) in enumerate(chunk_places(chunks // CAP, paired)):
+        block, over, _, turn = planned(plan[row, slot])
         pieces = []
         for step in range(span_tiles):
             own = pl.multiple_of(jnp.minimum(step + over, span_tiles - 1) * LANES, LANES)
@@ -109,11 +122,8 @@
                 piece = jnp.where(step + over < span_tiles, piece, rim)
             pieces.append(piece)
         span = jnp.concatenate(pieces, axis=2).reshape(2 * NP, SPAN)
-        rows = pl.ds(pl.multiple_of(chunk * 2 * NP, 2 * NP), 2 * NP)
+        rows = slice(chunk * 2 * NP, (chunk + 1) * 2 * NP)
         echo[rows, :] = pltpu.roll(span, turn, 1)[:, :RIM].astype(BF16)
-        return carry
-
-    lax.fori_loop(0, chunks, one_chunk, 0, unroll=chunks <= 16)
     sums = jnp.dot(echo[...], table_ref[...], preferred_element_type=jnp.float32)
     sums = sums.reshape(chunks, 2, NP, 2 * WIN)
     real = (sums[:, 0, :, :WIN] + sums[:, 1, :, WIN:]).astype(BF16)
@@ -125,27 +135,26 @@
         out_ref[:, 1] = imag[part]
 
 
-def cut_windows(foot, notes, place, raw, rim, table, groups):
+def cut_windows(foot, note, notes, place, raw, rim, table, groups):
     chunks = notes.shape[0] * CAP
-    smem = pl.BlockSpec(memory_space=pltpu.SMEM)
     vmem = pl.BlockSpec(memory_space=pltpu.VMEM)
     params = pltpu.CompilerParams(vmem_limit_bytes=vmem_grant(chunks))
     spans, plan = pl.pallas_call(
         functools.partial(fetch_kernel, foot, groups > 1),
         out_shape=(
             jax.ShapeDtypeStruct((chunks, 2, NP, SPAN), BF16),
-            jax.ShapeDtypeStruct((3, chunks), jnp.int32),
+            jax.ShapeDtypeStruct(notes.shape, jnp.int32),
         ),
-        in_specs=[smem, smem, pl.BlockSpec(memory_space=pltpu.HBM)],
-        out_specs=(vmem, smem),
+        in_specs=[vmem, vmem, vmem, pl.BlockSpec(memory_space=pltpu.HBM)],
+        out_specs=(vmem, vmem),
         scratch_shapes=[pltpu.SemaphoreType.DMA],
         compiler_params=params,
         name="fetch",
-    )(notes, place, pltpu.with_memory_space_constraint(raw, pltpu.HBM))
+    )(place[None], note, notes, pltpu.with_memory_space_constraint(raw, pltpu.HBM))
     return pl.pallas_call(
-        cut_kernel,
+        functools.partial(cut_kernel, groups > 1),
         out_shape=(jax.ShapeDtypeStruct((chunks // groups, 2, NP, WIN), BF16),) * groups,
-        in_specs=[smem, vmem, vmem, vmem],
+        in_specs=[vmem] * 4,
         out_specs=(vmem,) * groups,
         scratch_shapes=[pltpu.VMEM((chunks * 2 * NP, RIM), BF16)],
         compiler_params=params,
@@ -306,7 +315,7 @@
     steer, table = steering(foot, blocks, order, note, place)
     notes, steer, table = lax.optimization_barrier((notes, steer, table))
     windows = cut_windows(
-        foot, notes, place, raw, rim.reshape(planes, blocks, NP, RIM), table, 4 if paired else 1
+        foot, note, notes, place, raw, rim.reshape(planes, blocks, NP, RIM), table, 4 if paired else 1
     )
     if paired:
         windows = exchange(windows)

time: 27.9 us -> 27.4 us (0.982)
  Pallas kernels: 7.88 us -> 6.26 us
  waiting for transfers between devices: 6.83 us -> 7.86 us
    ppermute x1, waiting for transfers between devices: 0.73 us -> 1.84 us  [passed_along(): return lax.ppermute(value, axis, pairs)]
    pallas_call x1, Pallas kernels: 2.4 us -> 1.29 us  [cut_windows(): pl.pallas_call(functools.partial(fetch_kernel, foot, groups > 1), out_sha...]
    pallas_call x1, Pallas kernels: 1.16 us -> 0.65 us  [cut_windows(): pl.pallas_call(functools.partial(cut_kernel, groups > 1), out_shape=(jax....]
  transfers between devices with their start and end apart: 9 -> 9, of which waited for: 8 -> 8; matrix products, arithmetic and copies ran while one was open for 3% -> 4% of each run, Pallas kernels for 14% -> 10%
where the time goes in v7:
time: 27.4 us; the launch traced here: 27.2 us
  starting transfers between devices  10.9 us (40%)
  waiting for transfers between devices  7.86 us (29%)
  Pallas kernels  6.26 us (23%)
  local copies, waits for them, and re-layouts  1.14 us (4%)
  other arithmetic  0.93 us (3%)
    ppermute x8, starting transfers between devices, swapped(): return lax.ppermute(value, 'tile', [(i, i ^ turn) for i in range(tiles)])  9.61 us
    ppermute x8, waiting for transfers between devices, swapped(): return lax.ppermute(value, 'tile', [(i, i ^ turn) for i in range(tiles)])  6.01 us
    pallas_call x1, Pallas kernels, tile_image(): pl.pallas_call(functools.partial(image_kernel, 1.0 / math.sqrt(foot * NP)...  2.77 us
    ppermute x1, waiting for transfers between devices, passed_along(): return lax.ppermute(value, axis, pairs)  1.84 us
    pallas_call x1, Pallas kernels, steering(): pl.pallas_call(functools.partial(steer_kernel, foot, blocks, order), out_...  1.55 us
    ppermute x1, starting transfers between devices, passed_along(): return lax.ppermute(value, axis, pairs)  1.29 us
    pallas_call x1, Pallas kernels, cut_windows(): pl.pallas_call(functools.partial(fetch_kernel, foot, groups > 1), out_sha...  1.29 us
    slice x1, local copies, waits for them, and re-layouts, local(): rim = passed_along(raw_echo[:, :, :RIM], 'section', -1)  1.09 us
  transfers between devices with their start and end apart: 9, of which 8 were waited for; matrix products, arithmetic and copies ran while one was open for 4% of the time, Pallas kernels for 10%

profile of v7, /device:TPU:0, one launch (start us, length us, event | category | flops | bytes accessed | tf_op | source)
XLA Modules:
  0.0 27.2 jit_solution(995324019994118387)
XLA Ops:
  0.0 0.0 copy-start
  0.0 1.1 %slice.27 = bf16[2,256,384]{2,1,0:T(8,128)(2,1)S(1)} slice(bf16[2,256,2048]{2,1,0:T(8,128)(2,1)} %param.5), slice={[0:2], [0:256], [0:384]} | slice | bytes 786432 | tf_op jit(solution)/shard_map/slice | solution.py:304
  1.1 1.3 %collective-permute-start.4 = (bf16[2,256,384]{2,1,0:T(8,128)(2,1)S(1)}, bf16[2,256,384]{2,1,0:T(8,128)(2,1)S(1)}, u32[]{:S(2)}, u32[]{:S(2)}) collective-permute-start(bf16[2,256,384]{2,1,0:T(8,128)(2,1)S(1)} %slice.27), channel_id=1, source_target_pairs={{8,0},{16,8},{24,16},{9,1},{17,9},{25,17},{10,2},{18,10},{26,18},{... | collective-permute-start | bytes 1179656 | tf_op jit(solution)/shard_map/ppermute | solution.py:35
  2.4 0.7 %pad_add_fusion.2 = s32[1,40]{1,0:T(1,128)S(1)} fusion(s32[1,32]{1,0:T(1,128)} %param.7, s32[1,8]{1,0:T(1,128)} %bitcast.10), kind=kLoop, calls=%fused_computation.4 | loop fusion | flops 40 | bytes 320 | tf_op jit(solution)/shard_map/concatenate | solution.py:305
  3.2 0.5 %collective-permute-start = (s32[1,128]{1,0:T(1,128)S(1)}, s32[1,128]{1,0:T(1,128)S(1)}, u32[]{:S(2)}, u32[]{:S(2)}) collective-permute-start(s32[1,128]{1,0:T(1,128)S(1)} %pad.4.note_ref), channel_id=1, source_target_pairs={{0,1},{1,0},{2,3},{3,2},{4,5},{5,4},{6,7},{7,6},{8,9},{9,8},{10,11... | collective-permute-start | bytes 1544 | tf_op jit(solution)/shard_map/ppermute | solution.py:270
  3.6 0.1 fusion.4.place_ref
  3.7 0.7 %collective-permute-done = s32[1,128]{1,0:T(1,128)S(1)} collective-permute-done((s32[1,128]{1,0:T(1,128)S(1)}, s32[1,128]{1,0:T(1,128)S(1)}, u32[]{:S(2)}, u32[]{:S(2)}) %collective-permute-start) | collective-permute-done | bytes 544 | tf_op jit(solution)/shard_map/ppermute | solution.py:270
  4.4 3.6 %collective-permute-start.3 = (s32[2,128]{1,0:T(2,128)S(1)}, s32[2,128]{1,0:T(2,128)S(1)}, u32[]{:S(2)}, u32[]{:S(2)}) collective-permute-start(s32[2,128]{1,0:T(2,128)S(1)} %pad_add_fusion), channel_id=1, source_target_pairs={{0,7},{1,6},{2,5},{3,4},{4,3},{5,2},{6,1},{7,0},{8,15},{9,14},{10,... | collective-permute-start | bytes 3080 | tf_op jit(solution)/shard_map/ppermute | solution.py:270
  8.0 0.4 %collective-permute-start.2 = (s32[2,128]{1,0:T(2,128)S(1)}, s32[2,128]{1,0:T(2,128)S(1)}, u32[]{:S(2)}, u32[]{:S(2)}) collective-permute-start(s32[2,128]{1,0:T(2,128)S(1)} %pad_add_fusion), channel_id=1, source_target_pairs={{0,5},{1,4},{2,7},{3,6},{4,1},{5,0},{6,3},{7,2},{8,13},{9,12},{10,... | collective-permute-start | bytes 3080 | tf_op jit(solution)/shard_map/ppermute | solution.py:270
  8.4 0.2 collective-permute-start.1
  8.6 0.1 pad_add_fusion.1.place_ref
  8.7 1.5 %steer.1 = (bf16[256,2048]{1,0:T(8,128)(2,1)S(1)}, bf16[384,512]{1,0:T(8,128)(2,1)S(1)}) custom-call(s32[1,128]{1,0:T(1,128)S(1)} %pad.4.note_ref, s32[3]{0:T(128)S(1)} %pad_add_fusion.1.place_ref, bf16[384,512]{1,0:T(8,128)(2,1)} %constant.20.clone.table_ref), custom_call_target="tpu_custom_call" | custom-call | bytes 4194304 | tf_op jit(solution)/shard_map/steer/pallas_call | solution.py:213
  10.3 0.0 collective-permute-done.3
  10.3 0.7 %collective-permute-done.2 = s32[2,128]{1,0:T(2,128)S(1)} collective-permute-done((s32[2,128]{1,0:T(2,128)S(1)}, s32[2,128]{1,0:T(2,128)S(1)}, u32[]{:S(2)}, u32[]{:S(2)}) %collective-permute-start.2) | collective-permute-done | bytes 1056 | tf_op jit(solution)/shard_map/ppermute | solution.py:270
  11.0 1.0 %collective-permute-done.1 = s32[2,128]{1,0:T(2,128)S(1)} collective-permute-done((s32[2,128]{1,0:T(2,128)S(1)}, s32[2,128]{1,0:T(2,128)S(1)}, u32[]{:S(2)}, u32[]{:S(2)}) %collective-permute-start.1) | collective-permute-done | bytes 1056 | tf_op jit(solution)/shard_map/ppermute | solution.py:270
  12.0 1.3 %fetch.1 = (bf16[16,2,8,512]{3,2,1,0:T(8,128)(2,1)S(1)}, s32[8,128]{1,0:T(8,128)S(1)}) custom-call(s32[1,3]{1,0:T(1,128)S(1)} %fusion.4.place_ref, s32[1,128]{1,0:T(1,128)S(1)} %pad.4.note_ref, s32[8,128]{1,0:T(8,128)S(1)} %concatenate.18.notes_ref, bf16[2,32,8,2048]{3,2,1,0:T(8,128)(2,1)} %bitcast.9), custom_call_target="tpu_custom_call" | custom-call | tf_op jit(solution)/shard_map/fetch/pallas_call | solution.py:142
  13.3 1.8 %collective-permute-done.4 = bf16[2,256,384]{2,1,0:T(8,128)(2,1)S(1)} collective-permute-done((bf16[2,256,384]{2,1,0:T(8,128)(2,1)S(1)}, bf16[2,256,384]{2,1,0:T(8,128)(2,1)S(1)}, u32[]{:S(2)}, u32[]{:S(2)}) %collective-permute-start.4) | collective-permute-done | bytes 393248 | tf_op jit(solution)/shard_map/ppermute | solution.py:35
  15.1 0.7 %cut.1 = (bf16[4,2,8,256]{3,2,1,0:T(8,128)(2,1)S(1)}, bf16[4,2,8,256]{3,2,1,0:T(8,128)(2,1)S(1)}, bf16[4,2,8,256]{3,2,1,0:T(8,128)(2,1)S(1)}, bf16[4,2,8,256]{3,2,1,0:T(8,128)(2,1)S(1)}) custom-call(s32[8,128]{1,0:T(8,128)S(1)} %get-tuple-element.19.plan_ref, bf16[16,2,8,512]{3,2,1,0:T(8,128)(2,1)S(1)} %get-tuple-element.20.spans_ref, ...), custom_call_target="tpu_custom_call" | custom-call | tf_op jit(solution)/shard_map/cut/pallas_call | solution.py:154
  15.8 1.7 %collective-permute-start.5 = (bf16[4,2,8,256]{3,2,1,0:T(8,128)(2,1)S(1)}, bf16[4,2,8,256]{3,2,1,0:T(8,128)(2,1)S(1)}, u32[]{:S(2)}, u32[]{:S(2)}) collective-permute-start(bf16[4,2,8,256]{3,2,1,0:T(8,128)(2,1)S(1)} %get-tuple-element.23), channel_id=1, source_target_pairs={{0,2},{1,3},{2,0},{3,1},{4,6},{5,7},{6,4},{7,5},{8,10},{9,11},{10,... | collective-permute-start | bytes 98312 | tf_op jit(solution)/shard_map/ppermute | solution.py:270
  17.5 0.0 collective-permute-start.6
  17.5 1.6 %collective-permute-start.7 = (bf16[4,2,8,256]{3,2,1,0:T(8,128)(2,1)S(1)}, bf16[4,2,8,256]{3,2,1,0:T(8,128)(2,1)S(1)}, u32[]{:S(2)}, u32[]{:S(2)}) collective-permute-start(bf16[4,2,8,256]{3,2,1,0:T(8,128)(2,1)S(1)} %get-tuple-element.25), channel_id=1, source_target_pairs={{0,7},{1,6},{2,5},{3,4},{4,3},{5,2},{6,1},{7,0},{8,15},{9,14},{10,... | collective-permute-start | bytes 98312 | tf_op jit(solution)/shard_map/ppermute | solution.py:270
  19.1 0.7 %collective-permute-done.5 = bf16[4,2,8,256]{3,2,1,0:T(8,128)(2,1)S(1)} collective-permute-done((bf16[4,2,8,256]{3,2,1,0:T(8,128)(2,1)S(1)}, bf16[4,2,8,256]{3,2,1,0:T(8,128)(2,1)S(1)}, u32[]{:S(2)}, u32[]{:S(2)}) %collective-permute-start.5) | collective-permute-done | bytes 32800 | tf_op jit(solution)/shard_map/ppermute | solution.py:270
  19.8 1.3 %collective-permute-done.6 = bf16[4,2,8,256]{3,2,1,0:T(8,128)(2,1)S(1)} collective-permute-done((bf16[4,2,8,256]{3,2,1,0:T(8,128)(2,1)S(1)}, bf16[4,2,8,256]{3,2,1,0:T(8,128)(2,1)S(1)}, u32[]{:S(2)}, u32[]{:S(2)}) %collective-permute-start.6) | collective-permute-done | bytes 32800 | tf_op jit(solution)/shard_map/ppermute | solution.py:270
  21.1 0.6 %collective-permute-done.7 = bf16[4,2,8,256]{3,2,1,0:T(8,128)(2,1)S(1)} collective-permute-done((bf16[4,2,8,256]{3,2,1,0:T(8,128)(2,1)S(1)}, bf16[4,2,8,256]{3,2,1,0:T(8,128)(2,1)S(1)}, u32[]{:S(2)}, u32[]{:S(2)}) %collective-permute-start.7) | collective-permute-done | bytes 32800 | tf_op jit(solution)/shard_map/ppermute | solution.py:270
  21.8 1.7 %collective-permute-start.8 = (bf16[8,2,8,256]{3,2,1,0:T(8,128)(2,1)S(1)}, bf16[8,2,8,256]{3,2,1,0:T(8,128)(2,1)S(1)}, u32[]{:S(2)}, u32[]{:S(2)}) collective-permute-start(bf16[8,2,8,256]{3,2,1,0:T(8,128)(2,1)S(1)} %pad_maximum_fusion.1), channel_id=1, source_target_pairs={{0,1},{1,0},{2,3},{3,2},{4,5},{5,4},{6,7},{7,6},{8,9},{9,8},{10,11... | collective-permute-start | bytes 196616 | tf_op jit(solution)/shard_map/ppermute | solution.py:270
  23.5 0.9 %collective-permute-done.8.refs_1_ = bf16[8,2,8,256]{3,2,1,0:T(8,128)(2,1)S(1)} collective-permute-done((bf16[8,2,8,256]{3,2,1,0:T(8,128)(2,1)S(1)}, bf16[8,2,8,256]{3,2,1,0:T(8,128)(2,1)S(1)}, u32[]{:S(2)}, u32[]{:S(2)}) %collective-permute-start.8) | collective-permute-done | bytes 65568 | tf_op jit(solution)/shard_map/ppermute | solution.py:270
  24.4 0.0 copy-done
  24.4 2.8 %image.1 = bf16[1024,2048]{1,0:T(8,128)(2,1)} custom-call(bf16[8,2,8,256]{3,2,1,0:T(8,128)(2,1)S(1)} %pad_maximum_fusion.refs_0_, bf16[8,2,8,256]{3,2,1,0:T(8,128)(2,1)S(1)} %collective-permute-done.8.refs_1_, bf16[256,2048]{1,0:T(8,128)(2,1)S(1)} %get-tuple-element.26.refs_2_, bf16[1024,256]{1,0:T(8,128)(2,1)S(1)} %copy-done), custom_call_target="tpu_custom_call" | custom-call | tf_op jit(solution)/shard_map/image/pallas_call | solution.py:253
  (9 shorter events, 0.1 us)
Async XLA Ops:
  0.0 24.4 %copy-start = (bf16[1024,256]{1,0:T(8,128)(2,1)S(1)}, bf16[1024,256]{1,0:T(8,128)(2,1)}, u32[]{:S(2)}) copy-start(bf16[1024,256]{1,0:T(8,128)(2,1)} %constant.21.clone.refs_3_) | copy-start | bytes 1572868
  1.1 14.0 %collective-permute-start.4 = (bf16[2,256,384]{2,1,0:T(8,128)(2,1)S(1)}, bf16[2,256,384]{2,1,0:T(8,128)(2,1)S(1)}, u32[]{:S(2)}, u32[]{:S(2)}) collective-permute-start(bf16[2,256,384]{2,1,0:T(8,128)(2,1)S(1)} %slice.27), channel_id=1, source_target_pairs={{8,0},{16,8},{24,16},{9,1},{17,9},{25,17},{10,2},{18,10},{26,18},{... | collective-permute-start | bytes 1179656 | tf_op jit(solution)/shard_map/ppermute | solution.py:35
  3.2 1.3 %collective-permute-start = (s32[1,128]{1,0:T(1,128)S(1)}, s32[1,128]{1,0:T(1,128)S(1)}, u32[]{:S(2)}, u32[]{:S(2)}) collective-permute-start(s32[1,128]{1,0:T(1,128)S(1)} %pad.4.note_ref), channel_id=1, source_target_pairs={{0,1},{1,0},{2,3},{3,2},{4,5},{5,4},{6,7},{7,6},{8,9},{9,8},{10,11... | collective-permute-start | bytes 1544 | tf_op jit(solution)/shard_map/ppermute | solution.py:270
  4.4 5.8 %collective-permute-start.3 = (s32[2,128]{1,0:T(2,128)S(1)}, s32[2,128]{1,0:T(2,128)S(1)}, u32[]{:S(2)}, u32[]{:S(2)}) collective-permute-start(s32[2,128]{1,0:T(2,128)S(1)} %pad_add_fusion), channel_id=1, source_target_pairs={{0,7},{1,6},{2,5},{3,4},{4,3},{5,2},{6,1},{7,0},{8,15},{9,14},{10,... | collective-permute-start | bytes 3080 | tf_op jit(solution)/shard_map/ppermute | solution.py:270
  8.0 3.0 %collective-permute-start.2 = (s32[2,128]{1,0:T(2,128)S(1)}, s32[2,128]{1,0:T(2,128)S(1)}, u32[]{:S(2)}, u32[]{:S(2)}) collective-permute-start(s32[2,128]{1,0:T(2,128)S(1)} %pad_add_fusion), channel_id=1, source_target_pairs={{0,5},{1,4},{2,7},{3,6},{4,1},{5,0},{6,3},{7,2},{8,13},{9,12},{10,... | collective-permute-start | bytes 3080 | tf_op jit(solution)/shard_map/ppermute | solution.py:270
  8.4 3.6 %collective-permute-start.1 = (s32[2,128]{1,0:T(2,128)S(1)}, s32[2,128]{1,0:T(2,128)S(1)}, u32[]{:S(2)}, u32[]{:S(2)}) collective-permute-start(s32[2,128]{1,0:T(2,128)S(1)} %pad_add_fusion), channel_id=1, source_target_pairs={{0,2},{1,3},{2,0},{3,1},{4,6},{5,7},{6,4},{7,5},{8,10},{9,11},{10,... | collective-permute-start | bytes 3080 | tf_op jit(solution)/shard_map/ppermute | solution.py:270
  15.8 4.0 %collective-permute-start.5 = (bf16[4,2,8,256]{3,2,1,0:T(8,128)(2,1)S(1)}, bf16[4,2,8,256]{3,2,1,0:T(8,128)(2,1)S(1)}, u32[]{:S(2)}, u32[]{:S(2)}) collective-permute-start(bf16[4,2,8,256]{3,2,1,0:T(8,128)(2,1)S(1)} %get-tuple-element.23), channel_id=1, source_target_pairs={{0,2},{1,3},{2,0},{3,1},{4,6},{5,7},{6,4},{7,5},{8,10},{9,11},{10,... | collective-permute-start | bytes 98312 | tf_op jit(solution)/shard_map/ppermute | solution.py:270
  17.5 3.6 %collective-permute-start.6 = (bf16[4,2,8,256]{3,2,1,0:T(8,128)(2,1)S(1)}, bf16[4,2,8,256]{3,2,1,0:T(8,128)(2,1)S(1)}, u32[]{:S(2)}, u32[]{:S(2)}) collective-permute-start(bf16[4,2,8,256]{3,2,1,0:T(8,128)(2,1)S(1)} %get-tuple-element.24), channel_id=1, source_target_pairs={{0,5},{1,4},{2,7},{3,6},{4,1},{5,0},{6,3},{7,2},{8,13},{9,12},{10,... | collective-permute-start | bytes 98312 | tf_op jit(solution)/shard_map/ppermute | solution.py:270
  17.5 4.2 %collective-permute-start.7 = (bf16[4,2,8,256]{3,2,1,0:T(8,128)(2,1)S(1)}, bf16[4,2,8,256]{3,2,1,0:T(8,128)(2,1)S(1)}, u32[]{:S(2)}, u32[]{:S(2)}) collective-permute-start(bf16[4,2,8,256]{3,2,1,0:T(8,128)(2,1)S(1)} %get-tuple-element.25), channel_id=1, source_target_pairs={{0,7},{1,6},{2,5},{3,4},{4,3},{5,2},{6,1},{7,0},{8,15},{9,14},{10,... | collective-permute-start | bytes 98312 | tf_op jit(solution)/shard_map/ppermute | solution.py:270
  21.8 2.6 %collective-permute-start.8 = (bf16[8,2,8,256]{3,2,1,0:T(8,128)(2,1)S(1)}, bf16[8,2,8,256]{3,2,1,0:T(8,128)(2,1)S(1)}, u32[]{:S(2)}, u32[]{:S(2)}) collective-permute-start(bf16[8,2,8,256]{3,2,1,0:T(8,128)(2,1)S(1)} %pad_maximum_fusion.1), channel_id=1, source_target_pairs={{0,1},{1,0},{2,3},{3,2},{4,5},{5,4},{6,7},{7,6},{8,9},{9,8},{10,11... | collective-permute-start | bytes 196616 | tf_op jit(solution)/shard_map/ppermute | solution.py:270

commit v8 on v7

--- a/solution.py
+++ b/solution.py
@@ -19,7 +19,7 @@
 LANES = 128
 PRIME = 65521
 RIM = WIN + KC
-TURNS = (2, 5, 7)
+TURNS = (2, 5, 6)
 SPAN = RIM + LANES
 ROWS = 256
 BF16 = jnp.bfloat16
@@ -231,19 +231,22 @@
         [ref[...].reshape(ref.shape[0] * 2 * NP, WIN) for ref in window_refs], axis=0
     )
     contract = (((0,), (0,)), ((), ()))
-    focused[...] = (
-        lax.dot_general(windows, steer_ref[...], contract, preferred_element_type=jnp.float32)
-        * jnp.float32(scale)
-    ).astype(BF16)
     copies = []
-    for step in range(PR // ROWS):
-        rows = pl.ds(step * ROWS, ROWS)
-        pixels[rows, :] = jnp.dot(
-            interp_ref[rows, :], focused[...], preferred_element_type=jnp.float32
+    for columns in (slice(0, PC), slice(PC, 2 * PC)):
+        focused[:, columns] = (
+            lax.dot_general(
+                windows, steer_ref[:, columns], contract, preferred_element_type=jnp.float32
+            )
+            * jnp.float32(scale)
         ).astype(BF16)
-        copy = pltpu.make_async_copy(pixels.at[rows], out_ref.at[rows], sem.at[step])
-        copy.start()
-        copies.append(copy)
+        for first in range(0, PR, ROWS):
+            part = (slice(first, first + ROWS), columns)
+            pixels[part] = jnp.dot(
+                interp_ref[part[0], :], focused[:, columns], preferred_element_type=jnp.float32
+            ).astype(BF16)
+            copy = pltpu.make_async_copy(pixels.at[part], out_ref.at[part], sem.at[len(copies)])
+            copy.start()
+            copies.append(copy)
     for copy in copies:
         copy.wait()
 
@@ -258,7 +261,7 @@
         scratch_shapes=[
             pltpu.VMEM((WIN, 2 * PC), BF16),
             pltpu.VMEM((PR, 2 * PC), BF16),
-            pltpu.SemaphoreType.DMA((PR // ROWS,)),
+            pltpu.SemaphoreType.DMA((2 * PR // ROWS,)),
         ],
         compiler_params=pltpu.CompilerParams(vmem_limit_bytes=vmem_grant(steer.shape[0] // (2 * NP), 5)),
         name="image",

time: 27.4 us -> 26.7 us (0.974)
  starting transfers between devices: 10.9 us -> 9.78 us
  waiting for transfers between devices: 7.86 us -> 8.41 us
    ppermute x8, starting transfers between devices: 9.61 us -> 8.49 us  [swapped(): return lax.ppermute(value, 'tile', [(i, i ^ turn) for i in range(tiles)])]
    ppermute x8, waiting for transfers between devices: 6.01 us -> 6.38 us  [swapped(): return lax.ppermute(value, 'tile', [(i, i ^ turn) for i in range(tiles)])]
  transfers between devices with their start and end apart: 9 -> 9, of which waited for: 8 -> 8; matrix products, arithmetic and copies ran while one was open for 4% -> 4% of each run, Pallas kernels for 10% -> 11%
where the time goes in v8:
time: 26.7 us; the launch traced here: 26.5 us
  starting transfers between devices  9.78 us (37%)
  waiting for transfers between devices  8.41 us (31%)
  Pallas kernels  6.16 us (23%)
  local copies, waits for them, and re-layouts  1.14 us (4%)
  other arithmetic  0.93 us (3%)
    ppermute x8, starting transfers between devices, swapped(): return lax.ppermute(value, 'tile', [(i, i ^ turn) for i in range(tiles)])  8.49 us
    ppermute x8, waiting for transfers between devices, swapped(): return lax.ppermute(value, 'tile', [(i, i ^ turn) for i in range(tiles)])  6.38 us
    pallas_call x1, Pallas kernels, tile_image(): pl.pallas_call(functools.partial(image_kernel, 1.0 / math.sqrt(foot * NP)...  2.68 us
    ppermute x1, waiting for transfers between devices, passed_along(): return lax.ppermute(value, axis, pairs)  2.03 us
    pallas_call x1, Pallas kernels, steering(): pl.pallas_call(functools.partial(steer_kernel, foot, blocks, order), out_...  1.55 us
    ppermute x1, starting transfers between devices, passed_along(): return lax.ppermute(value, axis, pairs)  1.29 us
    pallas_call x1, Pallas kernels, cut_windows(): pl.pallas_call(functools.partial(fetch_kernel, foot, groups > 1), out_sha...  1.29 us
    slice x1, local copies, waits for them, and re-layouts, local(): rim = passed_along(raw_echo[:, :, :RIM], 'section', -1)  1.09 us
  transfers between devices with their start and end apart: 9, of which 8 were waited for; matrix products, arithmetic and copies ran while one was open for 4% of the time, Pallas kernels for 11%

profile of v8, /device:TPU:0, one launch (start us, length us, event | category | flops | bytes accessed | tf_op | source)
XLA Modules:
  0.0 26.5 jit_solution(5078929108555849241)
XLA Ops:
  0.0 0.0 copy-start
  0.0 1.1 %slice.27 = bf16[2,256,384]{2,1,0:T(8,128)(2,1)S(1)} slice(bf16[2,256,2048]{2,1,0:T(8,128)(2,1)} %param.5), slice={[0:2], [0:256], [0:384]} | slice | bytes 786432 | tf_op jit(solution)/shard_map/slice | solution.py:307
  1.1 1.3 %collective-permute-start.4 = (bf16[2,256,384]{2,1,0:T(8,128)(2,1)S(1)}, bf16[2,256,384]{2,1,0:T(8,128)(2,1)S(1)}, u32[]{:S(2)}, u32[]{:S(2)}) collective-permute-start(bf16[2,256,384]{2,1,0:T(8,128)(2,1)S(1)} %slice.27), channel_id=1, source_target_pairs={{8,0},{16,8},{24,16},{9,1},{17,9},{25,17},{10,2},{18,10},{26,18},{... | collective-permute-start | bytes 1179656 | tf_op jit(solution)/shard_map/ppermute | solution.py:35
  2.4 0.7 %pad_add_fusion.2 = s32[1,40]{1,0:T(1,128)S(1)} fusion(s32[1,32]{1,0:T(1,128)} %param.7, s32[1,8]{1,0:T(1,128)} %bitcast.10), kind=kLoop, calls=%fused_computation.4 | loop fusion | flops 40 | bytes 320 | tf_op jit(solution)/shard_map/concatenate | solution.py:308
  3.2 0.5 %collective-permute-start = (s32[1,128]{1,0:T(1,128)S(1)}, s32[1,128]{1,0:T(1,128)S(1)}, u32[]{:S(2)}, u32[]{:S(2)}) collective-permute-start(s32[1,128]{1,0:T(1,128)S(1)} %pad.4.note_ref), channel_id=1, source_target_pairs={{0,1},{1,0},{2,3},{3,2},{4,5},{5,4},{6,7},{7,6},{8,9},{9,8},{10,11... | collective-permute-start | bytes 1544 | tf_op jit(solution)/shard_map/ppermute | solution.py:273
  3.6 0.1 fusion.4.place_ref
  3.7 0.7 %collective-permute-done = s32[1,128]{1,0:T(1,128)S(1)} collective-permute-done((s32[1,128]{1,0:T(1,128)S(1)}, s32[1,128]{1,0:T(1,128)S(1)}, u32[]{:S(2)}, u32[]{:S(2)}) %collective-permute-start) | collective-permute-done | bytes 544 | tf_op jit(solution)/shard_map/ppermute | solution.py:273
  4.4 3.7 %collective-permute-start.3 = (s32[2,128]{1,0:T(2,128)S(1)}, s32[2,128]{1,0:T(2,128)S(1)}, u32[]{:S(2)}, u32[]{:S(2)}) collective-permute-start(s32[2,128]{1,0:T(2,128)S(1)} %pad_add_fusion), channel_id=1, source_target_pairs={{0,6},{1,7},{2,4},{3,5},{4,2},{5,3},{6,0},{7,1},{8,14},{9,15},{10,... | collective-permute-start | bytes 3080 | tf_op jit(solution)/shard_map/ppermute | solution.py:273
  8.2 0.0 collective-permute-start.2
  8.2 0.5 %collective-permute-start.1 = (s32[2,128]{1,0:T(2,128)S(1)}, s32[2,128]{1,0:T(2,128)S(1)}, u32[]{:S(2)}, u32[]{:S(2)}) collective-permute-start(s32[2,128]{1,0:T(2,128)S(1)} %pad_add_fusion), channel_id=1, source_target_pairs={{0,2},{1,3},{2,0},{3,1},{4,6},{5,7},{6,4},{7,5},{8,10},{9,11},{10,... | collective-permute-start | bytes 3080 | tf_op jit(solution)/shard_map/ppermute | solution.py:273
  8.7 0.1 pad_add_fusion.1.place_ref
  8.8 1.5 %steer.1 = (bf16[256,2048]{1,0:T(8,128)(2,1)S(1)}, bf16[384,512]{1,0:T(8,128)(2,1)S(1)}) custom-call(s32[1,128]{1,0:T(1,128)S(1)} %pad.4.note_ref, s32[3]{0:T(128)S(1)} %pad_add_fusion.1.place_ref, bf16[384,512]{1,0:T(8,128)(2,1)} %constant.20.clone.table_ref), custom_call_target="tpu_custom_call" | custom-call | bytes 4194304 | tf_op jit(solution)/shard_map/steer/pallas_call | solution.py:213
  10.4 0.0 collective-permute-done.3
  10.4 0.8 %collective-permute-done.2 = s32[2,128]{1,0:T(2,128)S(1)} collective-permute-done((s32[2,128]{1,0:T(2,128)S(1)}, s32[2,128]{1,0:T(2,128)S(1)}, u32[]{:S(2)}, u32[]{:S(2)}) %collective-permute-start.2) | collective-permute-done | bytes 1056 | tf_op jit(solution)/shard_map/ppermute | solution.py:273
  11.2 0.6 %collective-permute-done.1 = s32[2,128]{1,0:T(2,128)S(1)} collective-permute-done((s32[2,128]{1,0:T(2,128)S(1)}, s32[2,128]{1,0:T(2,128)S(1)}, u32[]{:S(2)}, u32[]{:S(2)}) %collective-permute-start.1) | collective-permute-done | bytes 1056 | tf_op jit(solution)/shard_map/ppermute | solution.py:273
  11.8 1.3 %fetch.1 = (bf16[16,2,8,512]{3,2,1,0:T(8,128)(2,1)S(1)}, s32[8,128]{1,0:T(8,128)S(1)}) custom-call(s32[1,3]{1,0:T(1,128)S(1)} %fusion.4.place_ref, s32[1,128]{1,0:T(1,128)S(1)} %pad.4.note_ref, s32[8,128]{1,0:T(8,128)S(1)} %concatenate.18.notes_ref, bf16[2,32,8,2048]{3,2,1,0:T(8,128)(2,1)} %bitcast.9), custom_call_target="tpu_custom_call" | custom-call | tf_op jit(solution)/shard_map/fetch/pallas_call | solution.py:142
  13.1 2.0 %collective-permute-done.4 = bf16[2,256,384]{2,1,0:T(8,128)(2,1)S(1)} collective-permute-done((bf16[2,256,384]{2,1,0:T(8,128)(2,1)S(1)}, bf16[2,256,384]{2,1,0:T(8,128)(2,1)S(1)}, u32[]{:S(2)}, u32[]{:S(2)}) %collective-permute-start.4) | collective-permute-done | bytes 393248 | tf_op jit(solution)/shard_map/ppermute | solution.py:35
  15.1 0.7 %cut.1 = (bf16[4,2,8,256]{3,2,1,0:T(8,128)(2,1)S(1)}, bf16[4,2,8,256]{3,2,1,0:T(8,128)(2,1)S(1)}, bf16[4,2,8,256]{3,2,1,0:T(8,128)(2,1)S(1)}, bf16[4,2,8,256]{3,2,1,0:T(8,128)(2,1)S(1)}) custom-call(s32[8,128]{1,0:T(8,128)S(1)} %get-tuple-element.19.plan_ref, bf16[16,2,8,512]{3,2,1,0:T(8,128)(2,1)S(1)} %get-tuple-element.20.spans_ref, ...), custom_call_target="tpu_custom_call" | custom-call | tf_op jit(solution)/shard_map/cut/pallas_call | solution.py:154
  15.8 1.7 %collective-permute-start.5 = (bf16[4,2,8,256]{3,2,1,0:T(8,128)(2,1)S(1)}, bf16[4,2,8,256]{3,2,1,0:T(8,128)(2,1)S(1)}, u32[]{:S(2)}, u32[]{:S(2)}) collective-permute-start(bf16[4,2,8,256]{3,2,1,0:T(8,128)(2,1)S(1)} %get-tuple-element.23), channel_id=1, source_target_pairs={{0,2},{1,3},{2,0},{3,1},{4,6},{5,7},{6,4},{7,5},{8,10},{9,11},{10,... | collective-permute-start | bytes 98312 | tf_op jit(solution)/shard_map/ppermute | solution.py:273
  17.5 0.0 collective-permute-start.6
  17.5 1.5 %collective-permute-start.7 = (bf16[4,2,8,256]{3,2,1,0:T(8,128)(2,1)S(1)}, bf16[4,2,8,256]{3,2,1,0:T(8,128)(2,1)S(1)}, u32[]{:S(2)}, u32[]{:S(2)}) collective-permute-start(bf16[4,2,8,256]{3,2,1,0:T(8,128)(2,1)S(1)} %get-tuple-element.25), channel_id=1, source_target_pairs={{0,6},{1,7},{2,4},{3,5},{4,2},{5,3},{6,0},{7,1},{8,14},{9,15},{10,... | collective-permute-start | bytes 98312 | tf_op jit(solution)/shard_map/ppermute | solution.py:273
  19.0 0.8 %collective-permute-done.5 = bf16[4,2,8,256]{3,2,1,0:T(8,128)(2,1)S(1)} collective-permute-done((bf16[4,2,8,256]{3,2,1,0:T(8,128)(2,1)S(1)}, bf16[4,2,8,256]{3,2,1,0:T(8,128)(2,1)S(1)}, u32[]{:S(2)}, u32[]{:S(2)}) %collective-permute-start.5) | collective-permute-done | bytes 32800 | tf_op jit(solution)/shard_map/ppermute | solution.py:273
  19.8 1.3 %collective-permute-done.6 = bf16[4,2,8,256]{3,2,1,0:T(8,128)(2,1)S(1)} collective-permute-done((bf16[4,2,8,256]{3,2,1,0:T(8,128)(2,1)S(1)}, bf16[4,2,8,256]{3,2,1,0:T(8,128)(2,1)S(1)}, u32[]{:S(2)}, u32[]{:S(2)}) %collective-permute-start.6) | collective-permute-done | bytes 32800 | tf_op jit(solution)/shard_map/ppermute | solution.py:273
  21.1 1.2 %collective-permute-done.7 = bf16[4,2,8,256]{3,2,1,0:T(8,128)(2,1)S(1)} collective-permute-done((bf16[4,2,8,256]{3,2,1,0:T(8,128)(2,1)S(1)}, bf16[4,2,8,256]{3,2,1,0:T(8,128)(2,1)S(1)}, u32[]{:S(2)}, u32[]{:S(2)}) %collective-permute-start.7) | collective-permute-done | bytes 32800 | tf_op jit(solution)/shard_map/ppermute | solution.py:273
  22.4 0.5 %collective-permute-start.8 = (bf16[8,2,8,256]{3,2,1,0:T(8,128)(2,1)S(1)}, bf16[8,2,8,256]{3,2,1,0:T(8,128)(2,1)S(1)}, u32[]{:S(2)}, u32[]{:S(2)}) collective-permute-start(bf16[8,2,8,256]{3,2,1,0:T(8,128)(2,1)S(1)} %pad_maximum_fusion.1), channel_id=1, source_target_pairs={{0,1},{1,0},{2,3},{3,2},{4,5},{5,4},{6,7},{7,6},{8,9},{9,8},{10,11... | collective-permute-start | bytes 196616 | tf_op jit(solution)/shard_map/ppermute | solution.py:273
  22.9 0.9 %collective-permute-done.8.refs_1_ = bf16[8,2,8,256]{3,2,1,0:T(8,128)(2,1)S(1)} collective-permute-done((bf16[8,2,8,256]{3,2,1,0:T(8,128)(2,1)S(1)}, bf16[8,2,8,256]{3,2,1,0:T(8,128)(2,1)S(1)}, u32[]{:S(2)}, u32[]{:S(2)}) %collective-permute-start.8) | collective-permute-done | bytes 65568 | tf_op jit(solution)/shard_map/ppermute | solution.py:273
  23.8 0.0 copy-done
  23.8 2.7 %image.1 = bf16[1024,2048]{1,0:T(8,128)(2,1)} custom-call(bf16[8,2,8,256]{3,2,1,0:T(8,128)(2,1)S(1)} %pad_maximum_fusion.refs_0_, bf16[8,2,8,256]{3,2,1,0:T(8,128)(2,1)S(1)} %collective-permute-done.8.refs_1_, bf16[256,2048]{1,0:T(8,128)(2,1)S(1)} %get-tuple-element.26.refs_2_, bf16[1024,256]{1,0:T(8,128)(2,1)S(1)} %copy-done), custom_call_target="tpu_custom_call" | custom-call | tf_op jit(solution)/shard_map/image/pallas_call | solution.py:256
  (9 shorter events, 0.1 us)
Async XLA Ops:
  0.0 23.8 %copy-start = (bf16[1024,256]{1,0:T(8,128)(2,1)S(1)}, bf16[1024,256]{1,0:T(8,128)(2,1)}, u32[]{:S(2)}) copy-start(bf16[1024,256]{1,0:T(8,128)(2,1)} %constant.21.clone.refs_3_) | copy-start | bytes 1572868
  1.1 14.0 %collective-permute-start.4 = (bf16[2,256,384]{2,1,0:T(8,128)(2,1)S(1)}, bf16[2,256,384]{2,1,0:T(8,128)(2,1)S(1)}, u32[]{:S(2)}, u32[]{:S(2)}) collective-permute-start(bf16[2,256,384]{2,1,0:T(8,128)(2,1)S(1)} %slice.27), channel_id=1, source_target_pairs={{8,0},{16,8},{24,16},{9,1},{17,9},{25,17},{10,2},{18,10},{26,18},{... | collective-permute-start | bytes 1179656 | tf_op jit(solution)/shard_map/ppermute | solution.py:35
  3.2 1.3 %collective-permute-start = (s32[1,128]{1,0:T(1,128)S(1)}, s32[1,128]{1,0:T(1,128)S(1)}, u32[]{:S(2)}, u32[]{:S(2)}) collective-permute-start(s32[1,128]{1,0:T(1,128)S(1)} %pad.4.note_ref), channel_id=1, source_target_pairs={{0,1},{1,0},{2,3},{3,2},{4,5},{5,4},{6,7},{7,6},{8,9},{9,8},{10,11... | collective-permute-start | bytes 1544 | tf_op jit(solution)/shard_map/ppermute | solution.py:273
  4.4 5.9 %collective-permute-start.3 = (s32[2,128]{1,0:T(2,128)S(1)}, s32[2,128]{1,0:T(2,128)S(1)}, u32[]{:S(2)}, u32[]{:S(2)}) collective-permute-start(s32[2,128]{1,0:T(2,128)S(1)} %pad_add_fusion), channel_id=1, source_target_pairs={{0,6},{1,7},{2,4},{3,5},{4,2},{5,3},{6,0},{7,1},{8,14},{9,15},{10,... | collective-permute-start | bytes 3080 | tf_op jit(solution)/shard_map/ppermute | solution.py:273
  8.2 3.0 %collective-permute-start.2 = (s32[2,128]{1,0:T(2,128)S(1)}, s32[2,128]{1,0:T(2,128)S(1)}, u32[]{:S(2)}, u32[]{:S(2)}) collective-permute-start(s32[2,128]{1,0:T(2,128)S(1)} %pad_add_fusion), channel_id=1, source_target_pairs={{0,5},{1,4},{2,7},{3,6},{4,1},{5,0},{6,3},{7,2},{8,13},{9,12},{10,... | collective-permute-start | bytes 3080 | tf_op jit(solution)/shard_map/ppermute | solution.py:273
  8.2 3.6 %collective-permute-start.1 = (s32[2,128]{1,0:T(2,128)S(1)}, s32[2,128]{1,0:T(2,128)S(1)}, u32[]{:S(2)}, u32[]{:S(2)}) collective-permute-start(s32[2,128]{1,0:T(2,128)S(1)} %pad_add_fusion), channel_id=1, source_target_pairs={{0,2},{1,3},{2,0},{3,1},{4,6},{5,7},{6,4},{7,5},{8,10},{9,11},{10,... | collective-permute-start | bytes 3080 | tf_op jit(solution)/shard_map/ppermute | solution.py:273
  15.8 4.0 %collective-permute-start.5 = (bf16[4,2,8,256]{3,2,1,0:T(8,128)(2,1)S(1)}, bf16[4,2,8,256]{3,2,1,0:T(8,128)(2,1)S(1)}, u32[]{:S(2)}, u32[]{:S(2)}) collective-permute-start(bf16[4,2,8,256]{3,2,1,0:T(8,128)(2,1)S(1)} %get-tuple-element.23), channel_id=1, source_target_pairs={{0,2},{1,3},{2,0},{3,1},{4,6},{5,7},{6,4},{7,5},{8,10},{9,11},{10,... | collective-permute-start | bytes 98312 | tf_op jit(solution)/shard_map/ppermute | solution.py:273
  17.5 3.6 %collective-permute-start.6 = (bf16[4,2,8,256]{3,2,1,0:T(8,128)(2,1)S(1)}, bf16[4,2,8,256]{3,2,1,0:T(8,128)(2,1)S(1)}, u32[]{:S(2)}, u32[]{:S(2)}) collective-permute-start(bf16[4,2,8,256]{3,2,1,0:T(8,128)(2,1)S(1)} %get-tuple-element.24), channel_id=1, source_target_pairs={{0,5},{1,4},{2,7},{3,6},{4,1},{5,0},{6,3},{7,2},{8,13},{9,12},{10,... | collective-permute-start | bytes 98312 | tf_op jit(solution)/shard_map/ppermute | solution.py:273
  17.5 4.8 %collective-permute-start.7 = (bf16[4,2,8,256]{3,2,1,0:T(8,128)(2,1)S(1)}, bf16[4,2,8,256]{3,2,1,0:T(8,128)(2,1)S(1)}, u32[]{:S(2)}, u32[]{:S(2)}) collective-permute-start(bf16[4,2,8,256]{3,2,1,0:T(8,128)(2,1)S(1)} %get-tuple-element.25), channel_id=1, source_target_pairs={{0,6},{1,7},{2,4},{3,5},{4,2},{5,3},{6,0},{7,1},{8,14},{9,15},{10,... | collective-permute-start | bytes 98312 | tf_op jit(solution)/shard_map/ppermute | solution.py:273
  22.4 1.5 %collective-permute-start.8 = (bf16[8,2,8,256]{3,2,1,0:T(8,128)(2,1)S(1)}, bf16[8,2,8,256]{3,2,1,0:T(8,128)(2,1)S(1)}, u32[]{:S(2)}, u32[]{:S(2)}) collective-permute-start(bf16[8,2,8,256]{3,2,1,0:T(8,128)(2,1)S(1)} %pad_maximum_fusion.1), channel_id=1, source_target_pairs={{0,1},{1,0},{2,3},{3,2},{4,5},{5,4},{6,7},{7,6},{8,9},{9,8},{10,11... | collective-permute-start | bytes 196616 | tf_op jit(solution)/shard_map/ppermute | solution.py:273

commit v9 on v8

--- a/solution.py
+++ b/solution.py
@@ -36,7 +36,7 @@
 
 
 def correlation_table():
-    lag = np.arange(RIM)[:, None] - np.arange(WIN)[None, :]
+    lag = np.arange(2 * KC)[:, None] - np.arange(KC)[None, :]
     inside = (lag >= 0) & (lag < KC)
     lag = np.where(inside, lag, 0)
     angle = (lag * lag % (2 * KC)).astype(np.float64) * (math.pi / KC)
@@ -115,24 +115,26 @@
         pieces = []
         for step in range(span_tiles):
             own = pl.multiple_of(jnp.minimum(step + over, span_tiles - 1) * LANES, LANES)
-            piece = spans_ref[chunk, :, :, pl.ds(own, LANES)].astype(jnp.float32)
+            piece = spans_ref[chunk, :, :, pl.ds(own, LANES)]
             if step:
                 beyond = pl.multiple_of(jnp.maximum(step + over - span_tiles, 0) * LANES, LANES)
-                rim = rim_ref[:, block, :, pl.ds(beyond, LANES)].astype(jnp.float32)
+                rim = rim_ref[:, block, :, pl.ds(beyond, LANES)]
                 piece = jnp.where(step + over < span_tiles, piece, rim)
-            pieces.append(piece)
+            pieces.append(piece.astype(jnp.float32))
         span = jnp.concatenate(pieces, axis=2).reshape(2 * NP, SPAN)
         rows = slice(chunk * 2 * NP, (chunk + 1) * 2 * NP)
         echo[rows, :] = pltpu.roll(span, turn, 1)[:, :RIM].astype(BF16)
-    sums = jnp.dot(echo[...], table_ref[...], preferred_element_type=jnp.float32)
-    sums = sums.reshape(chunks, 2, NP, 2 * WIN)
-    real = (sums[:, 0, :, :WIN] + sums[:, 1, :, WIN:]).astype(BF16)
-    imag = (sums[:, 1, :, :WIN] - sums[:, 0, :, WIN:]).astype(BF16)
     each = chunks // len(out_refs)
-    for group, out_ref in enumerate(out_refs):
-        part = slice(group * each, (group + 1) * each)
-        out_ref[:, 0] = real[part]
-        out_ref[:, 1] = imag[part]
+    for first in range(0, WIN, KC):
+        sums = jnp.dot(
+            echo[:, first : first + 2 * KC], table_ref[...], preferred_element_type=jnp.float32
+        ).reshape(chunks, 2, NP, 2 * KC)
+        real = (sums[:, 0, :, :KC] + sums[:, 1, :, KC:]).astype(BF16)
+        imag = (sums[:, 1, :, :KC] - sums[:, 0, :, KC:]).astype(BF16)
+        for group, out_ref in enumerate(out_refs):
+            part = slice(group * each, (group + 1) * each)
+            out_ref[:, 0, :, first : first + KC] = real[part]
+            out_ref[:, 1, :, first : first + KC] = imag[part]
 
 
 def cut_windows(foot, note, notes, place, raw, rim, table, groups):

time: 26.7 us -> 26.7 us (level)
  transfers between devices with their start and end apart: 9 -> 9, of which waited for: 8 -> 8; matrix products, arithmetic and copies ran while one was open for 4% -> 4% of each run, Pallas kernels for 11% -> 10%
where the time goes in v9:
time: 26.7 us; the launch traced here: 26.4 us
  starting transfers between devices  9.78 us (37%)
  waiting for transfers between devices  8.51 us (32%)
  Pallas kernels  5.99 us (22%)
  local copies, waits for them, and re-layouts  1.14 us (4%)
  other arithmetic  0.93 us (3%)
    ppermute x8, starting transfers between devices, swapped(): return lax.ppermute(value, 'tile', [(i, i ^ turn) for i in range(tiles)])  8.49 us
    ppermute x8, waiting for transfers between devices, swapped(): return lax.ppermute(value, 'tile', [(i, i ^ turn) for i in range(tiles)])  6.47 us
    pallas_call x1, Pallas kernels, tile_image(): pl.pallas_call(functools.partial(image_kernel, 1.0 / math.sqrt(foot * NP)...  2.68 us
    ppermute x1, waiting for transfers between devices, passed_along(): return lax.ppermute(value, axis, pairs)  2.05 us
    pallas_call x1, Pallas kernels, steering(): pl.pallas_call(functools.partial(steer_kernel, foot, blocks, order), out_...  1.46 us
    ppermute x1, starting transfers between devices, passed_along(): return lax.ppermute(value, axis, pairs)  1.29 us
    pallas_call x1, Pallas kernels, cut_windows(): pl.pallas_call(functools.partial(fetch_kernel, foot, groups > 1), out_sha...  1.27 us
    slice x1, local copies, waits for them, and re-layouts, local(): rim = passed_along(raw_echo[:, :, :RIM], 'section', -1)  1.09 us
  transfers between devices with their start and end apart: 9, of which 8 were waited for; matrix products, arithmetic and copies ran while one was open for 4% of the time, Pallas kernels for 10%

profile of v9, /device:TPU:0, one launch (start us, length us, event | category | flops | bytes accessed | tf_op | source)
XLA Modules:
  0.0 26.4 jit_solution(4365878886566512411)
XLA Ops:
  0.0 0.0 copy-start
  0.0 1.1 %slice.27 = bf16[2,256,384]{2,1,0:T(8,128)(2,1)S(1)} slice(bf16[2,256,2048]{2,1,0:T(8,128)(2,1)} %param.5), slice={[0:2], [0:256], [0:384]} | slice | bytes 786432 | tf_op jit(solution)/shard_map/slice | solution.py:309
  1.1 1.3 %collective-permute-start.4 = (bf16[2,256,384]{2,1,0:T(8,128)(2,1)S(1)}, bf16[2,256,384]{2,1,0:T(8,128)(2,1)S(1)}, u32[]{:S(2)}, u32[]{:S(2)}) collective-permute-start(bf16[2,256,384]{2,1,0:T(8,128)(2,1)S(1)} %slice.27), channel_id=1, source_target_pairs={{8,0},{16,8},{24,16},{9,1},{17,9},{25,17},{10,2},{18,10},{26,18},{... | collective-permute-start | bytes 1179656 | tf_op jit(solution)/shard_map/ppermute | solution.py:35
  2.4 0.7 %pad_add_fusion.2 = s32[1,40]{1,0:T(1,128)S(1)} fusion(s32[1,32]{1,0:T(1,128)} %param.7, s32[1,8]{1,0:T(1,128)} %bitcast.10), kind=kLoop, calls=%fused_computation.4 | loop fusion | flops 40 | bytes 320 | tf_op jit(solution)/shard_map/concatenate | solution.py:310
  3.2 0.5 %collective-permute-start = (s32[1,128]{1,0:T(1,128)S(1)}, s32[1,128]{1,0:T(1,128)S(1)}, u32[]{:S(2)}, u32[]{:S(2)}) collective-permute-start(s32[1,128]{1,0:T(1,128)S(1)} %pad.4.note_ref), channel_id=1, source_target_pairs={{0,1},{1,0},{2,3},{3,2},{4,5},{5,4},{6,7},{7,6},{8,9},{9,8},{10,11... | collective-permute-start | bytes 1544 | tf_op jit(solution)/shard_map/ppermute | solution.py:275
  3.6 0.1 fusion.4.place_ref
  3.7 0.7 %collective-permute-done = s32[1,128]{1,0:T(1,128)S(1)} collective-permute-done((s32[1,128]{1,0:T(1,128)S(1)}, s32[1,128]{1,0:T(1,128)S(1)}, u32[]{:S(2)}, u32[]{:S(2)}) %collective-permute-start) | collective-permute-done | bytes 544 | tf_op jit(solution)/shard_map/ppermute | solution.py:275
  4.4 3.7 %collective-permute-start.3 = (s32[2,128]{1,0:T(2,128)S(1)}, s32[2,128]{1,0:T(2,128)S(1)}, u32[]{:S(2)}, u32[]{:S(2)}) collective-permute-start(s32[2,128]{1,0:T(2,128)S(1)} %pad_add_fusion), channel_id=1, source_target_pairs={{0,6},{1,7},{2,4},{3,5},{4,2},{5,3},{6,0},{7,1},{8,14},{9,15},{10,... | collective-permute-start | bytes 3080 | tf_op jit(solution)/shard_map/ppermute | solution.py:275
  8.2 0.0 collective-permute-start.2
  8.2 0.5 %collective-permute-start.1 = (s32[2,128]{1,0:T(2,128)S(1)}, s32[2,128]{1,0:T(2,128)S(1)}, u32[]{:S(2)}, u32[]{:S(2)}) collective-permute-start(s32[2,128]{1,0:T(2,128)S(1)} %pad_add_fusion), channel_id=1, source_target_pairs={{0,2},{1,3},{2,0},{3,1},{4,6},{5,7},{6,4},{7,5},{8,10},{9,11},{10,... | collective-permute-start | bytes 3080 | tf_op jit(solution)/shard_map/ppermute | solution.py:275
  8.7 0.1 pad_add_fusion.1.place_ref
  8.8 1.5 %steer.1 = (bf16[256,2048]{1,0:T(8,128)(2,1)S(1)}, bf16[256,256]{1,0:T(8,128)(2,1)S(1)}) custom-call(s32[1,128]{1,0:T(1,128)S(1)} %pad.4.note_ref, s32[3]{0:T(128)S(1)} %pad_add_fusion.1.place_ref, bf16[256,256]{1,0:T(8,128)(2,1)} %constant.20.clone.table_ref), custom_call_target="tpu_custom_call" | custom-call | bytes 4194304 | tf_op jit(solution)/shard_map/steer/pallas_call | solution.py:215
  10.3 0.0 collective-permute-done.3
  10.3 0.9 %collective-permute-done.2 = s32[2,128]{1,0:T(2,128)S(1)} collective-permute-done((s32[2,128]{1,0:T(2,128)S(1)}, s32[2,128]{1,0:T(2,128)S(1)}, u32[]{:S(2)}, u32[]{:S(2)}) %collective-permute-start.2) | collective-permute-done | bytes 1056 | tf_op jit(solution)/shard_map/ppermute | solution.py:275
  11.2 0.6 %collective-permute-done.1 = s32[2,128]{1,0:T(2,128)S(1)} collective-permute-done((s32[2,128]{1,0:T(2,128)S(1)}, s32[2,128]{1,0:T(2,128)S(1)}, u32[]{:S(2)}, u32[]{:S(2)}) %collective-permute-start.1) | collective-permute-done | bytes 1056 | tf_op jit(solution)/shard_map/ppermute | solution.py:275
  11.8 1.3 %fetch.1 = (bf16[16,2,8,512]{3,2,1,0:T(8,128)(2,1)S(1)}, s32[8,128]{1,0:T(8,128)S(1)}) custom-call(s32[1,3]{1,0:T(1,128)S(1)} %fusion.4.place_ref, s32[1,128]{1,0:T(1,128)S(1)} %pad.4.note_ref, s32[8,128]{1,0:T(8,128)S(1)} %concatenate.18.notes_ref, bf16[2,32,8,2048]{3,2,1,0:T(8,128)(2,1)} %bitcast.9), custom_call_target="tpu_custom_call" | custom-call | tf_op jit(solution)/shard_map/fetch/pallas_call | solution.py:144
  13.1 2.0 %collective-permute-done.4 = bf16[2,256,384]{2,1,0:T(8,128)(2,1)S(1)} collective-permute-done((bf16[2,256,384]{2,1,0:T(8,128)(2,1)S(1)}, bf16[2,256,384]{2,1,0:T(8,128)(2,1)S(1)}, u32[]{:S(2)}, u32[]{:S(2)}) %collective-permute-start.4) | collective-permute-done | bytes 393248 | tf_op jit(solution)/shard_map/ppermute | solution.py:35
  15.1 0.6 %cut.1 = (bf16[4,2,8,256]{3,2,1,0:T(8,128)(2,1)S(1)}, bf16[4,2,8,256]{3,2,1,0:T(8,128)(2,1)S(1)}, bf16[4,2,8,256]{3,2,1,0:T(8,128)(2,1)S(1)}, bf16[4,2,8,256]{3,2,1,0:T(8,128)(2,1)S(1)}) custom-call(s32[8,128]{1,0:T(8,128)S(1)} %get-tuple-element.19.plan_ref, bf16[16,2,8,512]{3,2,1,0:T(8,128)(2,1)S(1)} %get-tuple-element.20.spans_ref, ...), custom_call_target="tpu_custom_call" | custom-call | tf_op jit(solution)/shard_map/cut/pallas_call | solution.py:156
  15.7 1.7 %collective-permute-start.5 = (bf16[4,2,8,256]{3,2,1,0:T(8,128)(2,1)S(1)}, bf16[4,2,8,256]{3,2,1,0:T(8,128)(2,1)S(1)}, u32[]{:S(2)}, u32[]{:S(2)}) collective-permute-start(bf16[4,2,8,256]{3,2,1,0:T(8,128)(2,1)S(1)} %get-tuple-element.23), channel_id=1, source_target_pairs={{0,2},{1,3},{2,0},{3,1},{4,6},{5,7},{6,4},{7,5},{8,10},{9,11},{10,... | collective-permute-start | bytes 98312 | tf_op jit(solution)/shard_map/ppermute | solution.py:275
  17.4 0.0 collective-permute-start.6
  17.4 1.5 %collective-permute-start.7 = (bf16[4,2,8,256]{3,2,1,0:T(8,128)(2,1)S(1)}, bf16[4,2,8,256]{3,2,1,0:T(8,128)(2,1)S(1)}, u32[]{:S(2)}, u32[]{:S(2)}) collective-permute-start(bf16[4,2,8,256]{3,2,1,0:T(8,128)(2,1)S(1)} %get-tuple-element.25), channel_id=1, source_target_pairs={{0,6},{1,7},{2,4},{3,5},{4,2},{5,3},{6,0},{7,1},{8,14},{9,15},{10,... | collective-permute-start | bytes 98312 | tf_op jit(solution)/shard_map/ppermute | solution.py:275
  18.9 0.8 %collective-permute-done.5 = bf16[4,2,8,256]{3,2,1,0:T(8,128)(2,1)S(1)} collective-permute-done((bf16[4,2,8,256]{3,2,1,0:T(8,128)(2,1)S(1)}, bf16[4,2,8,256]{3,2,1,0:T(8,128)(2,1)S(1)}, u32[]{:S(2)}, u32[]{:S(2)}) %collective-permute-start.5) | collective-permute-done | bytes 32800 | tf_op jit(solution)/shard_map/ppermute | solution.py:275
  19.7 1.4 %collective-permute-done.6 = bf16[4,2,8,256]{3,2,1,0:T(8,128)(2,1)S(1)} collective-permute-done((bf16[4,2,8,256]{3,2,1,0:T(8,128)(2,1)S(1)}, bf16[4,2,8,256]{3,2,1,0:T(8,128)(2,1)S(1)}, u32[]{:S(2)}, u32[]{:S(2)}) %collective-permute-start.6) | collective-permute-done | bytes 32800 | tf_op jit(solution)/shard_map/ppermute | solution.py:275
  21.1 1.2 %collective-permute-done.7 = bf16[4,2,8,256]{3,2,1,0:T(8,128)(2,1)S(1)} collective-permute-done((bf16[4,2,8,256]{3,2,1,0:T(8,128)(2,1)S(1)}, bf16[4,2,8,256]{3,2,1,0:T(8,128)(2,1)S(1)}, u32[]{:S(2)}, u32[]{:S(2)}) %collective-permute-start.7) | collective-permute-done | bytes 32800 | tf_op jit(solution)/shard_map/ppermute | solution.py:275
  22.3 0.5 %collective-permute-start.8 = (bf16[8,2,8,256]{3,2,1,0:T(8,128)(2,1)S(1)}, bf16[8,2,8,256]{3,2,1,0:T(8,128)(2,1)S(1)}, u32[]{:S(2)}, u32[]{:S(2)}) collective-permute-start(bf16[8,2,8,256]{3,2,1,0:T(8,128)(2,1)S(1)} %pad_maximum_fusion.1), channel_id=1, source_target_pairs={{0,1},{1,0},{2,3},{3,2},{4,5},{5,4},{6,7},{7,6},{8,9},{9,8},{10,11... | collective-permute-start | bytes 196616 | tf_op jit(solution)/shard_map/ppermute | solution.py:275
  22.8 0.9 %collective-permute-done.8.refs_1_ = bf16[8,2,8,256]{3,2,1,0:T(8,128)(2,1)S(1)} collective-permute-done((bf16[8,2,8,256]{3,2,1,0:T(8,128)(2,1)S(1)}, bf16[8,2,8,256]{3,2,1,0:T(8,128)(2,1)S(1)}, u32[]{:S(2)}, u32[]{:S(2)}) %collective-permute-start.8) | collective-permute-done | bytes 65568 | tf_op jit(solution)/shard_map/ppermute | solution.py:275
  23.7 0.0 copy-done
  23.7 2.7 %image.1 = bf16[1024,2048]{1,0:T(8,128)(2,1)} custom-call(bf16[8,2,8,256]{3,2,1,0:T(8,128)(2,1)S(1)} %pad_maximum_fusion.refs_0_, bf16[8,2,8,256]{3,2,1,0:T(8,128)(2,1)S(1)} %collective-permute-done.8.refs_1_, bf16[256,2048]{1,0:T(8,128)(2,1)S(1)} %get-tuple-element.26.refs_2_, bf16[1024,256]{1,0:T(8,128)(2,1)S(1)} %copy-done), custom_call_target="tpu_custom_call" | custom-call | tf_op jit(solution)/shard_map/image/pallas_call | solution.py:258
  (9 shorter events, 0.1 us)
Async XLA Ops:
  0.0 23.7 %copy-start = (bf16[1024,256]{1,0:T(8,128)(2,1)S(1)}, bf16[1024,256]{1,0:T(8,128)(2,1)}, u32[]{:S(2)}) copy-start(bf16[1024,256]{1,0:T(8,128)(2,1)} %constant.21.clone.refs_3_) | copy-start | bytes 1572868
  1.1 14.0 %collective-permute-start.4 = (bf16[2,256,384]{2,1,0:T(8,128)(2,1)S(1)}, bf16[2,256,384]{2,1,0:T(8,128)(2,1)S(1)}, u32[]{:S(2)}, u32[]{:S(2)}) collective-permute-start(bf16[2,256,384]{2,1,0:T(8,128)(2,1)S(1)} %slice.27), channel_id=1, source_target_pairs={{8,0},{16,8},{24,16},{9,1},{17,9},{25,17},{10,2},{18,10},{26,18},{... | collective-permute-start | bytes 1179656 | tf_op jit(solution)/shard_map/ppermute | solution.py:35
  3.2 1.3 %collective-permute-start = (s32[1,128]{1,0:T(1,128)S(1)}, s32[1,128]{1,0:T(1,128)S(1)}, u32[]{:S(2)}, u32[]{:S(2)}) collective-permute-start(s32[1,128]{1,0:T(1,128)S(1)} %pad.4.note_ref), channel_id=1, source_target_pairs={{0,1},{1,0},{2,3},{3,2},{4,5},{5,4},{6,7},{7,6},{8,9},{9,8},{10,11... | collective-permute-start | bytes 1544 | tf_op jit(solution)/shard_map/ppermute | solution.py:275
  4.4 5.8 %collective-permute-start.3 = (s32[2,128]{1,0:T(2,128)S(1)}, s32[2,128]{1,0:T(2,128)S(1)}, u32[]{:S(2)}, u32[]{:S(2)}) collective-permute-start(s32[2,128]{1,0:T(2,128)S(1)} %pad_add_fusion), channel_id=1, source_target_pairs={{0,6},{1,7},{2,4},{3,5},{4,2},{5,3},{6,0},{7,1},{8,14},{9,15},{10,... | collective-permute-start | bytes 3080 | tf_op jit(solution)/shard_map/ppermute | solution.py:275
  8.2 3.0 %collective-permute-start.2 = (s32[2,128]{1,0:T(2,128)S(1)}, s32[2,128]{1,0:T(2,128)S(1)}, u32[]{:S(2)}, u32[]{:S(2)}) collective-permute-start(s32[2,128]{1,0:T(2,128)S(1)} %pad_add_fusion), channel_id=1, source_target_pairs={{0,5},{1,4},{2,7},{3,6},{4,1},{5,0},{6,3},{7,2},{8,13},{9,12},{10,... | collective-permute-start | bytes 3080 | tf_op jit(solution)/shard_map/ppermute | solution.py:275
  8.2 3.6 %collective-permute-start.1 = (s32[2,128]{1,0:T(2,128)S(1)}, s32[2,128]{1,0:T(2,128)S(1)}, u32[]{:S(2)}, u32[]{:S(2)}) collective-permute-start(s32[2,128]{1,0:T(2,128)S(1)} %pad_add_fusion), channel_id=1, source_target_pairs={{0,2},{1,3},{2,0},{3,1},{4,6},{5,7},{6,4},{7,5},{8,10},{9,11},{10,... | collective-permute-start | bytes 3080 | tf_op jit(solution)/shard_map/ppermute | solution.py:275
  15.7 4.0 %collective-permute-start.5 = (bf16[4,2,8,256]{3,2,1,0:T(8,128)(2,1)S(1)}, bf16[4,2,8,256]{3,2,1,0:T(8,128)(2,1)S(1)}, u32[]{:S(2)}, u32[]{:S(2)}) collective-permute-start(bf16[4,2,8,256]{3,2,1,0:T(8,128)(2,1)S(1)} %get-tuple-element.23), channel_id=1, source_target_pairs={{0,2},{1,3},{2,0},{3,1},{4,6},{5,7},{6,4},{7,5},{8,10},{9,11},{10,... | collective-permute-start | bytes 98312 | tf_op jit(solution)/shard_map/ppermute | solution.py:275
  17.4 3.6 %collective-permute-start.6 = (bf16[4,2,8,256]{3,2,1,0:T(8,128)(2,1)S(1)}, bf16[4,2,8,256]{3,2,1,0:T(8,128)(2,1)S(1)}, u32[]{:S(2)}, u32[]{:S(2)}) collective-permute-start(bf16[4,2,8,256]{3,2,1,0:T(8,128)(2,1)S(1)} %get-tuple-element.24), channel_id=1, source_target_pairs={{0,5},{1,4},{2,7},{3,6},{4,1},{5,0},{6,3},{7,2},{8,13},{9,12},{10,... | collective-permute-start | bytes 98312 | tf_op jit(solution)/shard_map/ppermute | solution.py:275
  17.4 4.8 %collective-permute-start.7 = (bf16[4,2,8,256]{3,2,1,0:T(8,128)(2,1)S(1)}, bf16[4,2,8,256]{3,2,1,0:T(8,128)(2,1)S(1)}, u32[]{:S(2)}, u32[]{:S(2)}) collective-permute-start(bf16[4,2,8,256]{3,2,1,0:T(8,128)(2,1)S(1)} %get-tuple-element.25), channel_id=1, source_target_pairs={{0,6},{1,7},{2,4},{3,5},{4,2},{5,3},{6,0},{7,1},{8,14},{9,15},{10,... | collective-permute-start | bytes 98312 | tf_op jit(solution)/shard_map/ppermute | solution.py:275
  22.3 1.5 %collective-permute-start.8 = (bf16[8,2,8,256]{3,2,1,0:T(8,128)(2,1)S(1)}, bf16[8,2,8,256]{3,2,1,0:T(8,128)(2,1)S(1)}, u32[]{:S(2)}, u32[]{:S(2)}) collective-permute-start(bf16[8,2,8,256]{3,2,1,0:T(8,128)(2,1)S(1)} %pad_maximum_fusion.1), channel_id=1, source_target_pairs={{0,1},{1,0},{2,3},{3,2},{4,5},{5,4},{6,7},{7,6},{8,9},{9,8},{10,11... | collective-permute-start | bytes 196616 | tf_op jit(solution)/shard_map/ppermute | solution.py:275

commit v10 on v9

--- a/solution.py
+++ b/solution.py
@@ -78,52 +78,54 @@
         block = block.astype(jnp.int32)
         start = jnp.sum(jnp.where(lane == foot + block, starts, 0.0), axis=1, keepdims=True)
         start = start.astype(jnp.int32)
-        tile = start >> 7
-        turn = (SPAN - (start & (LANES - 1))) & (SPAN - 1)
-        code = (block * 4 + jnp.maximum(tile - last, 0)) * 64 + jnp.minimum(tile, last)
-        plan = jnp.where(lane == slot, code * SPAN + turn, plan)
+        first = jnp.minimum(start >> 7, last)
+        turn = (SPAN - (start - first * LANES)) & (SPAN - 1)
+        plan = jnp.where(lane == slot, (block * 64 + first) * SPAN + turn, plan)
     return plan
 
 
 def planned(code):
-    return code >> 17, (code >> 15) & 3, (code >> 9) & 63, code & (SPAN - 1)
+    return code >> 15, (code >> 9) & 63, code & (SPAN - 1)
 
 
 def chunk_places(tiles, paired):
     return [(row_of(n, paired), slot) for n in range(tiles) for slot in range(CAP)]
 
 
-def fetch_kernel(foot, paired, place_ref, note_ref, notes_ref, raw_ref, out_ref, plan_ref, sem):
+def chunk_rows(chunk):
+    return slice(chunk * 2 * NP, (chunk + 1) * 2 * NP)
+
+
+def fetch_kernel(foot, paired, place_ref, note_ref, notes_ref, raw_ref, out_ref, plan_ref, spans, sem):
     blocks = raw_ref.shape[1]
     last = (raw_ref.shape[3] - SPAN) // LANES
     plan = plan_of(foot, blocks, last, place_ref[0:1, 1:2], note_ref[...], notes_ref[...])
-    for chunk, (row, slot) in enumerate(chunk_places(notes_ref.shape[0], paired)):
-        block, _, first, _ = planned(plan[row, slot])
+    places = chunk_places(notes_ref.shape[0], paired)
+    for chunk, (row, slot) in enumerate(places):
+        block, first, _ = planned(plan[row, slot])
         lanes = pl.ds(pl.multiple_of(first * LANES, LANES), SPAN)
-        pltpu.make_async_copy(raw_ref.at[:, block, :, lanes], out_ref.at[chunk], sem).start()
+        pltpu.make_async_copy(raw_ref.at[:, block, :, lanes], spans.at[chunk], sem).start()
     plan_ref[...] = plan
-    pltpu.make_async_copy(out_ref, out_ref, sem).wait()
-
-
-def cut_kernel(paired, plan_ref, spans_ref, rim_ref, table_ref, *refs):
+    pltpu.make_async_copy(spans, spans, sem).wait()
+    for chunk, (row, slot) in enumerate(places):
+        _, _, turn = planned(plan[row, slot])
+        span = spans[chunk].astype(jnp.float32).reshape(2 * NP, SPAN)
+        out_ref[chunk_rows(chunk), :] = pltpu.roll(span, turn, 1)[:, :RIM].astype(BF16)
+
+
+def cut_kernel(paired, plan_ref, held_ref, rim_ref, table_ref, *refs):
     *out_refs, echo = refs
-    chunks = spans_ref.shape[0]
-    span_tiles = SPAN // LANES
+    chunks = held_ref.shape[0] // (2 * NP)
     plan = plan_ref[...]
+    lane = lax.broadcasted_iota(jnp.int32, (2 * NP, RIM), 1)
+    blank = jnp.zeros((2 * NP, SPAN - RIM), jnp.float32)
     for chunk, (row, slot) in enumerate(chunk_places(chunks // CAP, paired)):
-        block, over, _, turn = planned(plan[row, slot])
-        pieces = []
-        for step in range(span_tiles):
-            own = pl.multiple_of(jnp.minimum(step + over, span_tiles - 1) * LANES, LANES)
-            piece = spans_ref[chunk, :, :, pl.ds(own, LANES)]
-            if step:
-                beyond = pl.multiple_of(jnp.maximum(step + over - span_tiles, 0) * LANES, LANES)
-                rim = rim_ref[:, block, :, pl.ds(beyond, LANES)]
-                piece = jnp.where(step + over < span_tiles, piece, rim)
-            pieces.append(piece.astype(jnp.float32))
-        span = jnp.concatenate(pieces, axis=2).reshape(2 * NP, SPAN)
-        rows = slice(chunk * 2 * NP, (chunk + 1) * 2 * NP)
-        echo[rows, :] = pltpu.roll(span, turn, 1)[:, :RIM].astype(BF16)
+        block, _, turn = planned(plan[row, slot])
+        rim = rim_ref[:, block].astype(jnp.float32).reshape(2 * NP, RIM)
+        beyond = pltpu.roll(jnp.concatenate([rim, blank], axis=1), turn, 1)[:, :RIM]
+        held = held_ref[chunk_rows(chunk), :].astype(jnp.float32)
+        here = jnp.where(turn == 0, SPAN, turn)
+        echo[chunk_rows(chunk), :] = jnp.where(lane < here, held, beyond).astype(BF16)
     each = chunks // len(out_refs)
     for first in range(0, WIN, KC):
         sums = jnp.dot(
@@ -141,15 +143,15 @@
     chunks = notes.shape[0] * CAP
     vmem = pl.BlockSpec(memory_space=pltpu.VMEM)
     params = pltpu.CompilerParams(vmem_limit_bytes=vmem_grant(chunks))
-    spans, plan = pl.pallas_call(
+    held, plan = pl.pallas_call(
         functools.partial(fetch_kernel, foot, groups > 1),
         out_shape=(
-            jax.ShapeDtypeStruct((chunks, 2, NP, SPAN), BF16),
+            jax.ShapeDtypeStruct((chunks * 2 * NP, RIM), BF16),
             jax.ShapeDtypeStruct(notes.shape, jnp.int32),
         ),
         in_specs=[vmem, vmem, vmem, pl.BlockSpec(memory_space=pltpu.HBM)],
         out_specs=(vmem, vmem),
-        scratch_shapes=[pltpu.SemaphoreType.DMA],
+        scratch_shapes=[pltpu.VMEM((chunks, 2, NP, SPAN), BF16), pltpu.SemaphoreType.DMA],
         compiler_params=params,
         name="fetch",
     )(place[None], note, notes, pltpu.with_memory_space_constraint(raw, pltpu.HBM))
@@ -161,7 +163,7 @@
         scratch_shapes=[pltpu.VMEM((chunks * 2 * NP, RIM), BF16)],
         compiler_params=params,
         name="cut",
-    )(plan, spans, rim, table)
+    )(plan, held, rim, table)
 
 
 def mod_prime(value):
@@ -170,9 +172,13 @@
     return jnp.where(value >= PRIME, value - PRIME, value)
 
 
-def steer_kernel(foot, blocks, order, note_ref, place_ref, table_ref, out_ref, held_ref, sem):
-    holding = pltpu.make_async_copy(table_ref, held_ref, sem)
-    holding.start()
+def steer_kernel(foot, blocks, order, note_ref, place_ref, table_ref, interp_ref, out_ref, held_ref, interp_held, sems):
+    holding = [
+        pltpu.make_async_copy(table_ref, held_ref, sems.at[0]),
+        pltpu.make_async_copy(interp_ref, interp_held, sems.at[1]),
+    ]
+    for copy in holding:
+        copy.start()
     chunks = len(order) * CAP
     to_angle = jnp.float32(2.0 * math.pi / PRIME)
     first, twist = place_ref[0], place_ref[2]
@@ -203,28 +209,30 @@
         rows = slice(i * 2 * NP, (i + 1) * 2 * NP)
         out_ref[rows, :PC] = jnp.concatenate([real, -imag], axis=0).astype(BF16)
         out_ref[rows, PC:] = jnp.concatenate([imag, real], axis=0).astype(BF16)
-    holding.wait()
+    for copy in holding:
+        copy.wait()
 
 
 def steering(foot, blocks, order, note, place):
     smem = pl.BlockSpec(memory_space=pltpu.SMEM)
     vmem = pl.BlockSpec(memory_space=pltpu.VMEM)
     hbm = pl.BlockSpec(memory_space=pltpu.HBM)
-    table = jnp.asarray(correlation_table())
+    table, interp = jnp.asarray(correlation_table()), jnp.asarray(interp_table())
     rows = len(order) * CAP * 2 * NP
     return pl.pallas_call(
         functools.partial(steer_kernel, foot, blocks, order),
         out_shape=(
             jax.ShapeDtypeStruct((rows, 2 * PC), BF16),
             jax.ShapeDtypeStruct(table.shape, BF16),
+            jax.ShapeDtypeStruct(interp.shape, BF16),
         ),
-        in_specs=[smem, smem, hbm],
-        out_specs=(vmem, vmem),
-        scratch_shapes=[pltpu.SemaphoreType.DMA],
+        in_specs=[smem, smem, hbm, hbm],
+        out_specs=(vmem,) * 3,
+        scratch_shapes=[pltpu.SemaphoreType.DMA((2,))],
         compiler_params=pltpu.CompilerParams(vmem_limit_bytes=vmem_grant(len(order) * CAP)),
         cost_estimate=pl.CostEstimate(flops=0, bytes_accessed=4 << 20, transcendentals=0),
         name="steer",
-    )(note, place, pltpu.with_memory_space_constraint(table, pltpu.HBM))
+    )(note, place, *(pltpu.with_memory_space_constraint(x, pltpu.HBM) for x in (table, interp)))
 
 
 def image_kernel(scale, *refs):
@@ -253,7 +261,7 @@
         copy.wait()
 
 
-def tile_image(foot, windows, steer):
+def tile_image(foot, windows, steer, interp):
     vmem = pl.BlockSpec(memory_space=pltpu.VMEM)
     return pl.pallas_call(
         functools.partial(image_kernel, 1.0 / math.sqrt(foot * NP)),
@@ -267,7 +275,7 @@
         ],
         compiler_params=pltpu.CompilerParams(vmem_limit_bytes=vmem_grant(steer.shape[0] // (2 * NP), 5)),
         name="image",
-    )(*windows, steer, jnp.asarray(interp_table()))
+    )(*windows, steer, interp)
 
 
 def swapped(value, turn):
@@ -317,8 +325,8 @@
         order = (0,) + TURNS + (1,) + tuple(turn ^ 1 for turn in TURNS)
 
     raw = raw_echo.reshape(planes, blocks, NP, bins)
-    steer, table = steering(foot, blocks, order, note, place)
-    notes, steer, table = lax.optimization_barrier((notes, steer, table))
+    steer, table, interp = steering(foot, blocks, order, note, place)
+    notes, steer, table, interp = lax.optimization_barrier((notes, steer, table, interp))
     windows = cut_windows(
         foot, note, notes, place, raw, rim.reshape(planes, blocks, NP, RIM), table, 4 if paired else 1
     )
@@ -328,7 +336,7 @@
         sent = windows[0].reshape((tiles, CAP, 2, NP, WIN))
         got = lax.all_to_all(sent, "tile", 0, 0, tiled=True)
         windows = (got.reshape(windows[0].shape),)
-    return tile_image(foot, windows, steer)[None, None]
+    return tile_image(foot, windows, steer, interp)[None, None]
 
 
 def solution(mesh):

time: 26.7 us -> 26.5 us (level)
  waiting for transfers between devices: 8.51 us -> 8.14 us
  transfers between devices with their start and end apart: 9 -> 9, of which waited for: 8 -> 8; matrix products, arithmetic and copies ran while one was open for 4% -> 4% of each run, Pallas kernels for 10% -> 12%
where the time goes in v10:
time: 26.5 us; the launch traced here: 26.2 us
  starting transfers between devices  9.78 us (37%)
  waiting for transfers between devices  8.14 us (31%)
  Pallas kernels  6.21 us (23%)
  local copies, waits for them, and re-layouts  1.08 us (4%)
  other arithmetic  0.93 us (4%)
    ppermute x8, starting transfers between devices, swapped(): return lax.ppermute(value, 'tile', [(i, i ^ turn) for i in range(tiles)])  8.49 us
    ppermute x8, waiting for transfers between devices, swapped(): return lax.ppermute(value, 'tile', [(i, i ^ turn) for i in range(tiles)])  6.25 us
    pallas_call x1, Pallas kernels, tile_image(): pl.pallas_call(functools.partial(image_kernel, 1.0 / math.sqrt(foot * NP)...  2.67 us
    ppermute x1, waiting for transfers between devices, passed_along(): return lax.ppermute(value, axis, pairs)  1.89 us
    pallas_call x1, Pallas kernels, steering(): pl.pallas_call(functools.partial(steer_kernel, foot, blocks, order), out_...  1.68 us
    pallas_call x1, Pallas kernels, cut_windows(): pl.pallas_call(functools.partial(fetch_kernel, foot, groups > 1), out_sha...  1.42 us
    ppermute x1, starting transfers between devices, passed_along(): return lax.ppermute(value, axis, pairs)  1.29 us
    slice x1, local copies, waits for them, and re-layouts, local(): rim = passed_along(raw_echo[:, :, :RIM], 'section', -1)  1.04 us
  transfers between devices with their start and end apart: 9, of which 8 were waited for; matrix products, arithmetic and copies ran while one was open for 4% of the time, Pallas kernels for 12%

profile of v10, /device:TPU:0, one launch (start us, length us, event | category | flops | bytes accessed | tf_op | source)
XLA Modules:
  0.0 26.2 jit_solution(12871603544272656033)
XLA Ops:
  0.0 1.0 %slice.27 = bf16[2,256,384]{2,1,0:T(8,128)(2,1)S(1)} slice(bf16[2,256,2048]{2,1,0:T(8,128)(2,1)} %param.5), slice={[0:2], [0:256], [0:384]} | slice | bytes 786432 | tf_op jit(solution)/shard_map/slice | solution.py:317
  1.0 1.3 %collective-permute-start.4 = (bf16[2,256,384]{2,1,0:T(8,128)(2,1)S(1)}, bf16[2,256,384]{2,1,0:T(8,128)(2,1)S(1)}, u32[]{:S(2)}, u32[]{:S(2)}) collective-permute-start(bf16[2,256,384]{2,1,0:T(8,128)(2,1)S(1)} %slice.27), channel_id=1, source_target_pairs={{8,0},{16,8},{24,16},{9,1},{17,9},{25,17},{10,2},{18,10},{26,18},{... | collective-permute-start | bytes 1179656 | tf_op jit(solution)/shard_map/ppermute | solution.py:35
  2.3 0.7 %pad_add_fusion.2 = s32[1,40]{1,0:T(1,128)S(1)} fusion(s32[1,32]{1,0:T(1,128)} %param.7, s32[1,8]{1,0:T(1,128)} %bitcast.10), kind=kLoop, calls=%fused_computation.4 | loop fusion | flops 40 | bytes 320 | tf_op jit(solution)/shard_map/concatenate | solution.py:318
  3.1 0.5 %collective-permute-start = (s32[1,128]{1,0:T(1,128)S(1)}, s32[1,128]{1,0:T(1,128)S(1)}, u32[]{:S(2)}, u32[]{:S(2)}) collective-permute-start(s32[1,128]{1,0:T(1,128)S(1)} %pad.4.note_ref), channel_id=1, source_target_pairs={{0,1},{1,0},{2,3},{3,2},{4,5},{5,4},{6,7},{7,6},{8,9},{9,8},{10,11... | collective-permute-start | bytes 1544 | tf_op jit(solution)/shard_map/ppermute | solution.py:283
  3.5 0.1 fusion.4.place_ref
  3.6 0.7 %collective-permute-done = s32[1,128]{1,0:T(1,128)S(1)} collective-permute-done((s32[1,128]{1,0:T(1,128)S(1)}, s32[1,128]{1,0:T(1,128)S(1)}, u32[]{:S(2)}, u32[]{:S(2)}) %collective-permute-start) | collective-permute-done | bytes 544 | tf_op jit(solution)/shard_map/ppermute | solution.py:283
  4.4 3.7 %collective-permute-start.3 = (s32[2,128]{1,0:T(2,128)S(1)}, s32[2,128]{1,0:T(2,128)S(1)}, u32[]{:S(2)}, u32[]{:S(2)}) collective-permute-start(s32[2,128]{1,0:T(2,128)S(1)} %pad_add_fusion), channel_id=1, source_target_pairs={{0,6},{1,7},{2,4},{3,5},{4,2},{5,3},{6,0},{7,1},{8,14},{9,15},{10,... | collective-permute-start | bytes 3080 | tf_op jit(solution)/shard_map/ppermute | solution.py:283
  8.1 0.0 collective-permute-start.2
  8.2 0.5 %collective-permute-start.1 = (s32[2,128]{1,0:T(2,128)S(1)}, s32[2,128]{1,0:T(2,128)S(1)}, u32[]{:S(2)}, u32[]{:S(2)}) collective-permute-start(s32[2,128]{1,0:T(2,128)S(1)} %pad_add_fusion), channel_id=1, source_target_pairs={{0,2},{1,3},{2,0},{3,1},{4,6},{5,7},{6,4},{7,5},{8,10},{9,11},{10,... | collective-permute-start | bytes 3080 | tf_op jit(solution)/shard_map/ppermute | solution.py:283
  8.7 0.1 pad_add_fusion.1.place_ref
  8.7 1.7 %steer.1 = (bf16[256,2048]{1,0:T(8,128)(2,1)S(1)}, bf16[256,256]{1,0:T(8,128)(2,1)S(1)}, bf16[1024,256]{1,0:T(8,128)(2,1)S(1)}) custom-call(s32[1,128]{1,0:T(1,128)S(1)} %pad.4.note_ref, s32[3]{0:T(128)S(1)} %pad_add_fusion.1.place_ref, bf16[256,256]{1,0:T(8,128)(2,1)} %constant.20.clone.table_ref, bf16[1024,256]{1,0:T(8,128)(2,1)} %constant.21.clone.interp_ref), custom_call_target="tpu_custom_call" | custom-call | bytes 4194304 | tf_op jit(solution)/shard_map/steer/pallas_call | solution.py:222
  10.4 0.0 collective-permute-done.3
  10.4 0.7 %collective-permute-done.2 = s32[2,128]{1,0:T(2,128)S(1)} collective-permute-done((s32[2,128]{1,0:T(2,128)S(1)}, s32[2,128]{1,0:T(2,128)S(1)}, u32[]{:S(2)}, u32[]{:S(2)}) %collective-permute-start.2) | collective-permute-done | bytes 1056 | tf_op jit(solution)/shard_map/ppermute | solution.py:283
  11.1 0.6 %collective-permute-done.1 = s32[2,128]{1,0:T(2,128)S(1)} collective-permute-done((s32[2,128]{1,0:T(2,128)S(1)}, s32[2,128]{1,0:T(2,128)S(1)}, u32[]{:S(2)}, u32[]{:S(2)}) %collective-permute-start.1) | collective-permute-done | bytes 1056 | tf_op jit(solution)/shard_map/ppermute | solution.py:283
  11.8 1.4 %fetch.1 = (bf16[256,384]{1,0:T(8,128)(2,1)S(1)}, s32[8,128]{1,0:T(8,128)S(1)}) custom-call(s32[1,3]{1,0:T(1,128)S(1)} %fusion.4.place_ref, s32[1,128]{1,0:T(1,128)S(1)} %pad.4.note_ref, s32[8,128]{1,0:T(8,128)S(1)} %concatenate.18.notes_ref, bf16[2,32,8,2048]{3,2,1,0:T(8,128)(2,1)} %bitcast.9), custom_call_target="tpu_custom_call" | custom-call | tf_op jit(solution)/shard_map/fetch/pallas_call | solution.py:146
  13.2 1.9 %collective-permute-done.4 = bf16[2,256,384]{2,1,0:T(8,128)(2,1)S(1)} collective-permute-done((bf16[2,256,384]{2,1,0:T(8,128)(2,1)S(1)}, bf16[2,256,384]{2,1,0:T(8,128)(2,1)S(1)}, u32[]{:S(2)}, u32[]{:S(2)}) %collective-permute-start.4) | collective-permute-done | bytes 393248 | tf_op jit(solution)/shard_map/ppermute | solution.py:35
  15.1 0.4 %cut.1 = (bf16[4,2,8,256]{3,2,1,0:T(8,128)(2,1)S(1)}, bf16[4,2,8,256]{3,2,1,0:T(8,128)(2,1)S(1)}, bf16[4,2,8,256]{3,2,1,0:T(8,128)(2,1)S(1)}, bf16[4,2,8,256]{3,2,1,0:T(8,128)(2,1)S(1)}) custom-call(s32[8,128]{1,0:T(8,128)S(1)} %get-tuple-element.22.plan_ref, bf16[256,384]{1,0:T(8,128)(2,1)S(1)} %get-tuple-element.23.held_ref, ...), custom_call_target="tpu_custom_call" | custom-call | tf_op jit(solution)/shard_map/cut/pallas_call | solution.py:158
  15.5 1.7 %collective-permute-start.5 = (bf16[4,2,8,256]{3,2,1,0:T(8,128)(2,1)S(1)}, bf16[4,2,8,256]{3,2,1,0:T(8,128)(2,1)S(1)}, u32[]{:S(2)}, u32[]{:S(2)}) collective-permute-start(bf16[4,2,8,256]{3,2,1,0:T(8,128)(2,1)S(1)} %get-tuple-element.26), channel_id=1, source_target_pairs={{0,2},{1,3},{2,0},{3,1},{4,6},{5,7},{6,4},{7,5},{8,10},{9,11},{10,... | collective-permute-start | bytes 98312 | tf_op jit(solution)/shard_map/ppermute | solution.py:283
  17.2 0.0 collective-permute-start.6
  17.2 1.5 %collective-permute-start.7 = (bf16[4,2,8,256]{3,2,1,0:T(8,128)(2,1)S(1)}, bf16[4,2,8,256]{3,2,1,0:T(8,128)(2,1)S(1)}, u32[]{:S(2)}, u32[]{:S(2)}) collective-permute-start(bf16[4,2,8,256]{3,2,1,0:T(8,128)(2,1)S(1)} %get-tuple-element.28), channel_id=1, source_target_pairs={{0,6},{1,7},{2,4},{3,5},{4,2},{5,3},{6,0},{7,1},{8,14},{9,15},{10,... | collective-permute-start | bytes 98312 | tf_op jit(solution)/shard_map/ppermute | solution.py:283
  18.7 0.8 %collective-permute-done.5 = bf16[4,2,8,256]{3,2,1,0:T(8,128)(2,1)S(1)} collective-permute-done((bf16[4,2,8,256]{3,2,1,0:T(8,128)(2,1)S(1)}, bf16[4,2,8,256]{3,2,1,0:T(8,128)(2,1)S(1)}, u32[]{:S(2)}, u32[]{:S(2)}) %collective-permute-start.5) | collective-permute-done | bytes 32800 | tf_op jit(solution)/shard_map/ppermute | solution.py:283
  19.5 1.4 %collective-permute-done.6 = bf16[4,2,8,256]{3,2,1,0:T(8,128)(2,1)S(1)} collective-permute-done((bf16[4,2,8,256]{3,2,1,0:T(8,128)(2,1)S(1)}, bf16[4,2,8,256]{3,2,1,0:T(8,128)(2,1)S(1)}, u32[]{:S(2)}, u32[]{:S(2)}) %collective-permute-start.6) | collective-permute-done | bytes 32800 | tf_op jit(solution)/shard_map/ppermute | solution.py:283
  20.9 1.2 %collective-permute-done.7 = bf16[4,2,8,256]{3,2,1,0:T(8,128)(2,1)S(1)} collective-permute-done((bf16[4,2,8,256]{3,2,1,0:T(8,128)(2,1)S(1)}, bf16[4,2,8,256]{3,2,1,0:T(8,128)(2,1)S(1)}, u32[]{:S(2)}, u32[]{:S(2)}) %collective-permute-start.7) | collective-permute-done | bytes 32800 | tf_op jit(solution)/shard_map/ppermute | solution.py:283
  22.1 0.5 %collective-permute-start.8 = (bf16[8,2,8,256]{3,2,1,0:T(8,128)(2,1)S(1)}, bf16[8,2,8,256]{3,2,1,0:T(8,128)(2,1)S(1)}, u32[]{:S(2)}, u32[]{:S(2)}) collective-permute-start(bf16[8,2,8,256]{3,2,1,0:T(8,128)(2,1)S(1)} %pad_maximum_fusion.1), channel_id=1, source_target_pairs={{0,1},{1,0},{2,3},{3,2},{4,5},{5,4},{6,7},{7,6},{8,9},{9,8},{10,11... | collective-permute-start | bytes 196616 | tf_op jit(solution)/shard_map/ppermute | solution.py:283
  22.6 0.9 %collective-permute-done.8.refs_1_ = bf16[8,2,8,256]{3,2,1,0:T(8,128)(2,1)S(1)} collective-permute-done((bf16[8,2,8,256]{3,2,1,0:T(8,128)(2,1)S(1)}, bf16[8,2,8,256]{3,2,1,0:T(8,128)(2,1)S(1)}, u32[]{:S(2)}, u32[]{:S(2)}) %collective-permute-start.8) | collective-permute-done | bytes 65568 | tf_op jit(solution)/shard_map/ppermute | solution.py:283
  23.5 2.7 %image.1 = bf16[1024,2048]{1,0:T(8,128)(2,1)} custom-call(bf16[8,2,8,256]{3,2,1,0:T(8,128)(2,1)S(1)} %pad_maximum_fusion.refs_0_, bf16[8,2,8,256]{3,2,1,0:T(8,128)(2,1)S(1)} %collective-permute-done.8.refs_1_, bf16[256,2048]{1,0:T(8,128)(2,1)S(1)} %get-tuple-element.29.refs_2_, bf16[1024,256]{1,0:T(8,128)(2,1)S(1)} %get-tuple-element.30.refs_3_), custom_call_target="tpu_custom_call" | custom-call | tf_op jit(solution)/shard_map/image/pallas_call | solution.py:266
  (9 shorter events, 0.1 us)
Async XLA Ops:
  1.0 14.0 %collective-permute-start.4 = (bf16[2,256,384]{2,1,0:T(8,128)(2,1)S(1)}, bf16[2,256,384]{2,1,0:T(8,128)(2,1)S(1)}, u32[]{:S(2)}, u32[]{:S(2)}) collective-permute-start(bf16[2,256,384]{2,1,0:T(8,128)(2,1)S(1)} %slice.27), channel_id=1, source_target_pairs={{8,0},{16,8},{24,16},{9,1},{17,9},{25,17},{10,2},{18,10},{26,18},{... | collective-permute-start | bytes 1179656 | tf_op jit(solution)/shard_map/ppermute | solution.py:35
  3.1 1.3 %collective-permute-start = (s32[1,128]{1,0:T(1,128)S(1)}, s32[1,128]{1,0:T(1,128)S(1)}, u32[]{:S(2)}, u32[]{:S(2)}) collective-permute-start(s32[1,128]{1,0:T(1,128)S(1)} %pad.4.note_ref), channel_id=1, source_target_pairs={{0,1},{1,0},{2,3},{3,2},{4,5},{5,4},{6,7},{7,6},{8,9},{9,8},{10,11... | collective-permute-start | bytes 1544 | tf_op jit(solution)/shard_map/ppermute | solution.py:283
  4.4 6.0 %collective-permute-start.3 = (s32[2,128]{1,0:T(2,128)S(1)}, s32[2,128]{1,0:T(2,128)S(1)}, u32[]{:S(2)}, u32[]{:S(2)}) collective-permute-start(s32[2,128]{1,0:T(2,128)S(1)} %pad_add_fusion), channel_id=1, source_target_pairs={{0,6},{1,7},{2,4},{3,5},{4,2},{5,3},{6,0},{7,1},{8,14},{9,15},{10,... | collective-permute-start | bytes 3080 | tf_op jit(solution)/shard_map/ppermute | solution.py:283
  8.1 3.0 %collective-permute-start.2 = (s32[2,128]{1,0:T(2,128)S(1)}, s32[2,128]{1,0:T(2,128)S(1)}, u32[]{:S(2)}, u32[]{:S(2)}) collective-permute-start(s32[2,128]{1,0:T(2,128)S(1)} %pad_add_fusion), channel_id=1, source_target_pairs={{0,5},{1,4},{2,7},{3,6},{4,1},{5,0},{6,3},{7,2},{8,13},{9,12},{10,... | collective-permute-start | bytes 3080 | tf_op jit(solution)/shard_map/ppermute | solution.py:283
  8.2 3.6 %collective-permute-start.1 = (s32[2,128]{1,0:T(2,128)S(1)}, s32[2,128]{1,0:T(2,128)S(1)}, u32[]{:S(2)}, u32[]{:S(2)}) collective-permute-start(s32[2,128]{1,0:T(2,128)S(1)} %pad_add_fusion), channel_id=1, source_target_pairs={{0,2},{1,3},{2,0},{3,1},{4,6},{5,7},{6,4},{7,5},{8,10},{9,11},{10,... | collective-permute-start | bytes 3080 | tf_op jit(solution)/shard_map/ppermute | solution.py:283
  15.5 4.0 %collective-permute-start.5 = (bf16[4,2,8,256]{3,2,1,0:T(8,128)(2,1)S(1)}, bf16[4,2,8,256]{3,2,1,0:T(8,128)(2,1)S(1)}, u32[]{:S(2)}, u32[]{:S(2)}) collective-permute-start(bf16[4,2,8,256]{3,2,1,0:T(8,128)(2,1)S(1)} %get-tuple-element.26), channel_id=1, source_target_pairs={{0,2},{1,3},{2,0},{3,1},{4,6},{5,7},{6,4},{7,5},{8,10},{9,11},{10,... | collective-permute-start | bytes 98312 | tf_op jit(solution)/shard_map/ppermute | solution.py:283
  17.2 3.6 %collective-permute-start.6 = (bf16[4,2,8,256]{3,2,1,0:T(8,128)(2,1)S(1)}, bf16[4,2,8,256]{3,2,1,0:T(8,128)(2,1)S(1)}, u32[]{:S(2)}, u32[]{:S(2)}) collective-permute-start(bf16[4,2,8,256]{3,2,1,0:T(8,128)(2,1)S(1)} %get-tuple-element.27), channel_id=1, source_target_pairs={{0,5},{1,4},{2,7},{3,6},{4,1},{5,0},{6,3},{7,2},{8,13},{9,12},{10,... | collective-permute-start | bytes 98312 | tf_op jit(solution)/shard_map/ppermute | solution.py:283
  17.2 4.8 %collective-permute-start.7 = (bf16[4,2,8,256]{3,2,1,0:T(8,128)(2,1)S(1)}, bf16[4,2,8,256]{3,2,1,0:T(8,128)(2,1)S(1)}, u32[]{:S(2)}, u32[]{:S(2)}) collective-permute-start(bf16[4,2,8,256]{3,2,1,0:T(8,128)(2,1)S(1)} %get-tuple-element.28), channel_id=1, source_target_pairs={{0,6},{1,7},{2,4},{3,5},{4,2},{5,3},{6,0},{7,1},{8,14},{9,15},{10,... | collective-permute-start | bytes 98312 | tf_op jit(solution)/shard_map/ppermute | solution.py:283
  22.1 1.4 %collective-permute-start.8 = (bf16[8,2,8,256]{3,2,1,0:T(8,128)(2,1)S(1)}, bf16[8,2,8,256]{3,2,1,0:T(8,128)(2,1)S(1)}, u32[]{:S(2)}, u32[]{:S(2)}) collective-permute-start(bf16[8,2,8,256]{3,2,1,0:T(8,128)(2,1)S(1)} %pad_maximum_fusion.1), channel_id=1, source_target_pairs={{0,1},{1,0},{2,3},{3,2},{4,5},{5,4},{6,7},{7,6},{8,9},{9,8},{10,11... | collective-permute-start | bytes 196616 | tf_op jit(solution)/shard_map/ppermute | solution.py:283

commit v11 on v10

--- a/solution.py
+++ b/solution.py
@@ -123,9 +123,9 @@
         block, _, turn = planned(plan[row, slot])
         rim = rim_ref[:, block].astype(jnp.float32).reshape(2 * NP, RIM)
         beyond = pltpu.roll(jnp.concatenate([rim, blank], axis=1), turn, 1)[:, :RIM]
-        held = held_ref[chunk_rows(chunk), :].astype(jnp.float32)
+        held = held_ref[chunk_rows(chunk), :]
         here = jnp.where(turn == 0, SPAN, turn)
-        echo[chunk_rows(chunk), :] = jnp.where(lane < here, held, beyond).astype(BF16)
+        echo[chunk_rows(chunk), :] = jnp.where(lane < here, held, beyond.astype(BF16))
     each = chunks // len(out_refs)
     for first in range(0, WIN, KC):
         sums = jnp.dot(

time: 26.5 us -> 26.4 us (level)
  no operation moved by 1% of the time
where the time goes in v11:
time: 26.4 us; the launch traced here: 26.2 us
  starting transfers between devices  9.78 us (37%)
  waiting for transfers between devices  8.14 us (31%)
  Pallas kernels  6.19 us (23%)
  local copies, waits for them, and re-layouts  1.08 us (4%)
  other arithmetic  0.93 us (4%)
    ppermute x8, starting transfers between devices, swapped(): return lax.ppermute(value, 'tile', [(i, i ^ turn) for i in range(tiles)])  8.49 us
    ppermute x8, waiting for transfers between devices, swapped(): return lax.ppermute(value, 'tile', [(i, i ^ turn) for i in range(tiles)])  6.25 us
    pallas_call x1, Pallas kernels, tile_image(): pl.pallas_call(functools.partial(image_kernel, 1.0 / math.sqrt(foot * NP)...  2.68 us
    ppermute x1, waiting for transfers between devices, passed_along(): return lax.ppermute(value, axis, pairs)  1.89 us
    pallas_call x1, Pallas kernels, steering(): pl.pallas_call(functools.partial(steer_kernel, foot, blocks, order), out_...  1.68 us
    pallas_call x1, Pallas kernels, cut_windows(): pl.pallas_call(functools.partial(fetch_kernel, foot, groups > 1), out_sha...  1.42 us
    ppermute x1, starting transfers between devices, passed_along(): return lax.ppermute(value, axis, pairs)  1.29 us
    slice x1, local copies, waits for them, and re-layouts, local(): rim = passed_along(raw_echo[:, :, :RIM], 'section', -1)  1.04 us
  transfers between devices with their start and end apart: 9, of which 8 were waited for; matrix products, arithmetic and copies ran while one was open for 4% of the time, Pallas kernels for 12%

profile of v11, /device:TPU:0, one launch (start us, length us, event | category | flops | bytes accessed | tf_op | source)
XLA Modules:
  0.0 26.2 jit_solution(11181652773624926060)
XLA Ops:
  0.0 1.0 %slice.27 = bf16[2,256,384]{2,1,0:T(8,128)(2,1)S(1)} slice(bf16[2,256,2048]{2,1,0:T(8,128)(2,1)} %param.5), slice={[0:2], [0:256], [0:384]} | slice | bytes 786432 | tf_op jit(solution)/shard_map/slice | solution.py:317
  1.0 1.3 %collective-permute-start.4 = (bf16[2,256,384]{2,1,0:T(8,128)(2,1)S(1)}, bf16[2,256,384]{2,1,0:T(8,128)(2,1)S(1)}, u32[]{:S(2)}, u32[]{:S(2)}) collective-permute-start(bf16[2,256,384]{2,1,0:T(8,128)(2,1)S(1)} %slice.27), channel_id=1, source_target_pairs={{8,0},{16,8},{24,16},{9,1},{17,9},{25,17},{10,2},{18,10},{26,18},{... | collective-permute-start | bytes 1179656 | tf_op jit(solution)/shard_map/ppermute | solution.py:35
  2.3 0.7 %pad_add_fusion.2 = s32[1,40]{1,0:T(1,128)S(1)} fusion(s32[1,32]{1,0:T(1,128)} %param.7, s32[1,8]{1,0:T(1,128)} %bitcast.10), kind=kLoop, calls=%fused_computation.4 | loop fusion | flops 40 | bytes 320 | tf_op jit(solution)/shard_map/concatenate | solution.py:318
  3.1 0.5 %collective-permute-start = (s32[1,128]{1,0:T(1,128)S(1)}, s32[1,128]{1,0:T(1,128)S(1)}, u32[]{:S(2)}, u32[]{:S(2)}) collective-permute-start(s32[1,128]{1,0:T(1,128)S(1)} %pad.4.note_ref), channel_id=1, source_target_pairs={{0,1},{1,0},{2,3},{3,2},{4,5},{5,4},{6,7},{7,6},{8,9},{9,8},{10,11... | collective-permute-start | bytes 1544 | tf_op jit(solution)/shard_map/ppermute | solution.py:283
  3.5 0.1 fusion.4.place_ref
  3.6 0.7 %collective-permute-done = s32[1,128]{1,0:T(1,128)S(1)} collective-permute-done((s32[1,128]{1,0:T(1,128)S(1)}, s32[1,128]{1,0:T(1,128)S(1)}, u32[]{:S(2)}, u32[]{:S(2)}) %collective-permute-start) | collective-permute-done | bytes 544 | tf_op jit(solution)/shard_map/ppermute | solution.py:283
  4.4 3.7 %collective-permute-start.3 = (s32[2,128]{1,0:T(2,128)S(1)}, s32[2,128]{1,0:T(2,128)S(1)}, u32[]{:S(2)}, u32[]{:S(2)}) collective-permute-start(s32[2,128]{1,0:T(2,128)S(1)} %pad_add_fusion), channel_id=1, source_target_pairs={{0,6},{1,7},{2,4},{3,5},{4,2},{5,3},{6,0},{7,1},{8,14},{9,15},{10,... | collective-permute-start | bytes 3080 | tf_op jit(solution)/shard_map/ppermute | solution.py:283
  8.1 0.0 collective-permute-start.2
  8.2 0.5 %collective-permute-start.1 = (s32[2,128]{1,0:T(2,128)S(1)}, s32[2,128]{1,0:T(2,128)S(1)}, u32[]{:S(2)}, u32[]{:S(2)}) collective-permute-start(s32[2,128]{1,0:T(2,128)S(1)} %pad_add_fusion), channel_id=1, source_target_pairs={{0,2},{1,3},{2,0},{3,1},{4,6},{5,7},{6,4},{7,5},{8,10},{9,11},{10,... | collective-permute-start | bytes 3080 | tf_op jit(solution)/shard_map/ppermute | solution.py:283
  8.7 0.1 pad_add_fusion.1.place_ref
  8.7 1.7 %steer.1 = (bf16[256,2048]{1,0:T(8,128)(2,1)S(1)}, bf16[256,256]{1,0:T(8,128)(2,1)S(1)}, bf16[1024,256]{1,0:T(8,128)(2,1)S(1)}) custom-call(s32[1,128]{1,0:T(1,128)S(1)} %pad.4.note_ref, s32[3]{0:T(128)S(1)} %pad_add_fusion.1.place_ref, bf16[256,256]{1,0:T(8,128)(2,1)} %constant.20.clone.table_ref, bf16[1024,256]{1,0:T(8,128)(2,1)} %constant.21.clone.interp_ref), custom_call_target="tpu_custom_call" | custom-call | bytes 4194304 | tf_op jit(solution)/shard_map/steer/pallas_call | solution.py:222
  10.4 0.0 collective-permute-done.3
  10.4 0.7 %collective-permute-done.2 = s32[2,128]{1,0:T(2,128)S(1)} collective-permute-done((s32[2,128]{1,0:T(2,128)S(1)}, s32[2,128]{1,0:T(2,128)S(1)}, u32[]{:S(2)}, u32[]{:S(2)}) %collective-permute-start.2) | collective-permute-done | bytes 1056 | tf_op jit(solution)/shard_map/ppermute | solution.py:283
  11.1 0.6 %collective-permute-done.1 = s32[2,128]{1,0:T(2,128)S(1)} collective-permute-done((s32[2,128]{1,0:T(2,128)S(1)}, s32[2,128]{1,0:T(2,128)S(1)}, u32[]{:S(2)}, u32[]{:S(2)}) %collective-permute-start.1) | collective-permute-done | bytes 1056 | tf_op jit(solution)/shard_map/ppermute | solution.py:283
  11.8 1.4 %fetch.1 = (bf16[256,384]{1,0:T(8,128)(2,1)S(1)}, s32[8,128]{1,0:T(8,128)S(1)}) custom-call(s32[1,3]{1,0:T(1,128)S(1)} %fusion.4.place_ref, s32[1,128]{1,0:T(1,128)S(1)} %pad.4.note_ref, s32[8,128]{1,0:T(8,128)S(1)} %concatenate.18.notes_ref, bf16[2,32,8,2048]{3,2,1,0:T(8,128)(2,1)} %bitcast.9), custom_call_target="tpu_custom_call" | custom-call | tf_op jit(solution)/shard_map/fetch/pallas_call | solution.py:146
  13.2 1.9 %collective-permute-done.4 = bf16[2,256,384]{2,1,0:T(8,128)(2,1)S(1)} collective-permute-done((bf16[2,256,384]{2,1,0:T(8,128)(2,1)S(1)}, bf16[2,256,384]{2,1,0:T(8,128)(2,1)S(1)}, u32[]{:S(2)}, u32[]{:S(2)}) %collective-permute-start.4) | collective-permute-done | bytes 393248 | tf_op jit(solution)/shard_map/ppermute | solution.py:35
  15.1 0.4 %cut.1 = (bf16[4,2,8,256]{3,2,1,0:T(8,128)(2,1)S(1)}, bf16[4,2,8,256]{3,2,1,0:T(8,128)(2,1)S(1)}, bf16[4,2,8,256]{3,2,1,0:T(8,128)(2,1)S(1)}, bf16[4,2,8,256]{3,2,1,0:T(8,128)(2,1)S(1)}) custom-call(s32[8,128]{1,0:T(8,128)S(1)} %get-tuple-element.22.plan_ref, bf16[256,384]{1,0:T(8,128)(2,1)S(1)} %get-tuple-element.23.held_ref, ...), custom_call_target="tpu_custom_call" | custom-call | tf_op jit(solution)/shard_map/cut/pallas_call | solution.py:158
  15.5 1.7 %collective-permute-start.5 = (bf16[4,2,8,256]{3,2,1,0:T(8,128)(2,1)S(1)}, bf16[4,2,8,256]{3,2,1,0:T(8,128)(2,1)S(1)}, u32[]{:S(2)}, u32[]{:S(2)}) collective-permute-start(bf16[4,2,8,256]{3,2,1,0:T(8,128)(2,1)S(1)} %get-tuple-element.26), channel_id=1, source_target_pairs={{0,2},{1,3},{2,0},{3,1},{4,6},{5,7},{6,4},{7,5},{8,10},{9,11},{10,... | collective-permute-start | bytes 98312 | tf_op jit(solution)/shard_map/ppermute | solution.py:283
  17.2 0.0 collective-permute-start.6
  17.2 1.5 %collective-permute-start.7 = (bf16[4,2,8,256]{3,2,1,0:T(8,128)(2,1)S(1)}, bf16[4,2,8,256]{3,2,1,0:T(8,128)(2,1)S(1)}, u32[]{:S(2)}, u32[]{:S(2)}) collective-permute-start(bf16[4,2,8,256]{3,2,1,0:T(8,128)(2,1)S(1)} %get-tuple-element.28), channel_id=1, source_target_pairs={{0,6},{1,7},{2,4},{3,5},{4,2},{5,3},{6,0},{7,1},{8,14},{9,15},{10,... | collective-permute-start | bytes 98312 | tf_op jit(solution)/shard_map/ppermute | solution.py:283
  18.7 0.8 %collective-permute-done.5 = bf16[4,2,8,256]{3,2,1,0:T(8,128)(2,1)S(1)} collective-permute-done((bf16[4,2,8,256]{3,2,1,0:T(8,128)(2,1)S(1)}, bf16[4,2,8,256]{3,2,1,0:T(8,128)(2,1)S(1)}, u32[]{:S(2)}, u32[]{:S(2)}) %collective-permute-start.5) | collective-permute-done | bytes 32800 | tf_op jit(solution)/shard_map/ppermute | solution.py:283
  19.5 1.3 %collective-permute-done.6 = bf16[4,2,8,256]{3,2,1,0:T(8,128)(2,1)S(1)} collective-permute-done((bf16[4,2,8,256]{3,2,1,0:T(8,128)(2,1)S(1)}, bf16[4,2,8,256]{3,2,1,0:T(8,128)(2,1)S(1)}, u32[]{:S(2)}, u32[]{:S(2)}) %collective-permute-start.6) | collective-permute-done | bytes 32800 | tf_op jit(solution)/shard_map/ppermute | solution.py:283
  20.8 1.2 %collective-permute-done.7 = bf16[4,2,8,256]{3,2,1,0:T(8,128)(2,1)S(1)} collective-permute-done((bf16[4,2,8,256]{3,2,1,0:T(8,128)(2,1)S(1)}, bf16[4,2,8,256]{3,2,1,0:T(8,128)(2,1)S(1)}, u32[]{:S(2)}, u32[]{:S(2)}) %collective-permute-start.7) | collective-permute-done | bytes 32800 | tf_op jit(solution)/shard_map/ppermute | solution.py:283
  22.1 0.5 %collective-permute-start.8 = (bf16[8,2,8,256]{3,2,1,0:T(8,128)(2,1)S(1)}, bf16[8,2,8,256]{3,2,1,0:T(8,128)(2,1)S(1)}, u32[]{:S(2)}, u32[]{:S(2)}) collective-permute-start(bf16[8,2,8,256]{3,2,1,0:T(8,128)(2,1)S(1)} %pad_maximum_fusion.1), channel_id=1, source_target_pairs={{0,1},{1,0},{2,3},{3,2},{4,5},{5,4},{6,7},{7,6},{8,9},{9,8},{10,11... | collective-permute-start | bytes 196616 | tf_op jit(solution)/shard_map/ppermute | solution.py:283
  22.6 0.9 %collective-permute-done.8.refs_1_ = bf16[8,2,8,256]{3,2,1,0:T(8,128)(2,1)S(1)} collective-permute-done((bf16[8,2,8,256]{3,2,1,0:T(8,128)(2,1)S(1)}, bf16[8,2,8,256]{3,2,1,0:T(8,128)(2,1)S(1)}, u32[]{:S(2)}, u32[]{:S(2)}) %collective-permute-start.8) | collective-permute-done | bytes 65568 | tf_op jit(solution)/shard_map/ppermute | solution.py:283
  23.5 2.7 %image.1 = bf16[1024,2048]{1,0:T(8,128)(2,1)} custom-call(bf16[8,2,8,256]{3,2,1,0:T(8,128)(2,1)S(1)} %pad_maximum_fusion.refs_0_, bf16[8,2,8,256]{3,2,1,0:T(8,128)(2,1)S(1)} %collective-permute-done.8.refs_1_, bf16[256,2048]{1,0:T(8,128)(2,1)S(1)} %get-tuple-element.29.refs_2_, bf16[1024,256]{1,0:T(8,128)(2,1)S(1)} %get-tuple-element.30.refs_3_), custom_call_target="tpu_custom_call" | custom-call | tf_op jit(solution)/shard_map/image/pallas_call | solution.py:266
  (9 shorter events, 0.1 us)
Async XLA Ops:
  1.0 14.0 %collective-permute-start.4 = (bf16[2,256,384]{2,1,0:T(8,128)(2,1)S(1)}, bf16[2,256,384]{2,1,0:T(8,128)(2,1)S(1)}, u32[]{:S(2)}, u32[]{:S(2)}) collective-permute-start(bf16[2,256,384]{2,1,0:T(8,128)(2,1)S(1)} %slice.27), channel_id=1, source_target_pairs={{8,0},{16,8},{24,16},{9,1},{17,9},{25,17},{10,2},{18,10},{26,18},{... | collective-permute-start | bytes 1179656 | tf_op jit(solution)/shard_map/ppermute | solution.py:35
  3.1 1.3 %collective-permute-start = (s32[1,128]{1,0:T(1,128)S(1)}, s32[1,128]{1,0:T(1,128)S(1)}, u32[]{:S(2)}, u32[]{:S(2)}) collective-permute-start(s32[1,128]{1,0:T(1,128)S(1)} %pad.4.note_ref), channel_id=1, source_target_pairs={{0,1},{1,0},{2,3},{3,2},{4,5},{5,4},{6,7},{7,6},{8,9},{9,8},{10,11... | collective-permute-start | bytes 1544 | tf_op jit(solution)/shard_map/ppermute | solution.py:283
  4.4 6.0 %collective-permute-start.3 = (s32[2,128]{1,0:T(2,128)S(1)}, s32[2,128]{1,0:T(2,128)S(1)}, u32[]{:S(2)}, u32[]{:S(2)}) collective-permute-start(s32[2,128]{1,0:T(2,128)S(1)} %pad_add_fusion), channel_id=1, source_target_pairs={{0,6},{1,7},{2,4},{3,5},{4,2},{5,3},{6,0},{7,1},{8,14},{9,15},{10,... | collective-permute-start | bytes 3080 | tf_op jit(solution)/shard_map/ppermute | solution.py:283
  8.1 3.0 %collective-permute-start.2 = (s32[2,128]{1,0:T(2,128)S(1)}, s32[2,128]{1,0:T(2,128)S(1)}, u32[]{:S(2)}, u32[]{:S(2)}) collective-permute-start(s32[2,128]{1,0:T(2,128)S(1)} %pad_add_fusion), channel_id=1, source_target_pairs={{0,5},{1,4},{2,7},{3,6},{4,1},{5,0},{6,3},{7,2},{8,13},{9,12},{10,... | collective-permute-start | bytes 3080 | tf_op jit(solution)/shard_map/ppermute | solution.py:283
  8.2 3.6 %collective-permute-start.1 = (s32[2,128]{1,0:T(2,128)S(1)}, s32[2,128]{1,0:T(2,128)S(1)}, u32[]{:S(2)}, u32[]{:S(2)}) collective-permute-start(s32[2,128]{1,0:T(2,128)S(1)} %pad_add_fusion), channel_id=1, source_target_pairs={{0,2},{1,3},{2,0},{3,1},{4,6},{5,7},{6,4},{7,5},{8,10},{9,11},{10,... | collective-permute-start | bytes 3080 | tf_op jit(solution)/shard_map/ppermute | solution.py:283
  15.5 4.0 %collective-permute-start.5 = (bf16[4,2,8,256]{3,2,1,0:T(8,128)(2,1)S(1)}, bf16[4,2,8,256]{3,2,1,0:T(8,128)(2,1)S(1)}, u32[]{:S(2)}, u32[]{:S(2)}) collective-permute-start(bf16[4,2,8,256]{3,2,1,0:T(8,128)(2,1)S(1)} %get-tuple-element.26), channel_id=1, source_target_pairs={{0,2},{1,3},{2,0},{3,1},{4,6},{5,7},{6,4},{7,5},{8,10},{9,11},{10,... | collective-permute-start | bytes 98312 | tf_op jit(solution)/shard_map/ppermute | solution.py:283
  17.2 3.6 %collective-permute-start.6 = (bf16[4,2,8,256]{3,2,1,0:T(8,128)(2,1)S(1)}, bf16[4,2,8,256]{3,2,1,0:T(8,128)(2,1)S(1)}, u32[]{:S(2)}, u32[]{:S(2)}) collective-permute-start(bf16[4,2,8,256]{3,2,1,0:T(8,128)(2,1)S(1)} %get-tuple-element.27), channel_id=1, source_target_pairs={{0,5},{1,4},{2,7},{3,6},{4,1},{5,0},{6,3},{7,2},{8,13},{9,12},{10,... | collective-permute-start | bytes 98312 | tf_op jit(solution)/shard_map/ppermute | solution.py:283
  17.2 4.8 %collective-permute-start.7 = (bf16[4,2,8,256]{3,2,1,0:T(8,128)(2,1)S(1)}, bf16[4,2,8,256]{3,2,1,0:T(8,128)(2,1)S(1)}, u32[]{:S(2)}, u32[]{:S(2)}) collective-permute-start(bf16[4,2,8,256]{3,2,1,0:T(8,128)(2,1)S(1)} %get-tuple-element.28), channel_id=1, source_target_pairs={{0,6},{1,7},{2,4},{3,5},{4,2},{5,3},{6,0},{7,1},{8,14},{9,15},{10,... | collective-permute-start | bytes 98312 | tf_op jit(solution)/shard_map/ppermute | solution.py:283
  22.1 1.5 %collective-permute-start.8 = (bf16[8,2,8,256]{3,2,1,0:T(8,128)(2,1)S(1)}, bf16[8,2,8,256]{3,2,1,0:T(8,128)(2,1)S(1)}, u32[]{:S(2)}, u32[]{:S(2)}) collective-permute-start(bf16[8,2,8,256]{3,2,1,0:T(8,128)(2,1)S(1)} %pad_maximum_fusion.1), channel_id=1, source_target_pairs={{0,1},{1,0},{2,3},{3,2},{4,5},{5,4},{6,7},{7,6},{8,9},{9,8},{10,11... | collective-permute-start | bytes 196616 | tf_op jit(solution)/shard_map/ppermute | solution.py:283
